TPU v7x, 128 devices: a whole 4x4x4 slice. The times are simulated.
128 devices in a mesh: seq: 16 (over y, z_lo, core), chan: 8 (over x, z_hi).
Axes of the slice: x: 4, y: 4, z: 4 (z_hi: 2, z_lo: 2; z = z_hi * 2 + z_lo), core: 2. Of those that a mesh axis runs over, the one named last changes fastest.
Arguments:
- token_ids: int32 [8192], P('seq'), may hold values from 0 to 511
- embed_table: bfloat16 [512, 4096], replicated, may hold values from -6 to 6
- in_weight: bfloat16 [4096, 3, 2048], P(None, None, 'chan'), may hold values from -0.09375 to 0.09375
- short_filter: float32 [3, 3, 2048], P(None, None, 'chan'), may hold values from -3 to 3
- long_filter: float32 [8192, 2048], P('seq', 'chan'), may hold values from -1.5 to 1.5
- skip_gain: float32 [2048], P('chan'), may hold values from -4 to 4
- out_weight: bfloat16 [2048, 4096], P('chan'), may hold values from -0.125 to 0.125
Outputs:
- mixed: bfloat16 [8192, 4096], P(('seq', 'chan'))
All inputs are finite; a program needn't handle non-finite values.
Results may differ from a plain program's by a relative error of at most 0.0072.
Values may be sent and summed in bfloat16 or wider, within the bound.
No kernel may reach another device: no remote copies, remote signals or barrier semaphores. Data moves between devices by JAX's collectives and lax.ppermute only.
A program may use at most 128 MiB of HBM per device.

v0:
```python
import functools
import itertools

import jax
import jax.numpy as jnp
import ml_dtypes
import numpy as np
from jax import lax
from jax.experimental import pallas as pl
from jax.experimental.pallas import tpu as pltpu
from jax.sharding import Mesh
from jax.sharding import PartitionSpec as P


SIZES = {"y": 4, "zl": 2, "core": 2, "x": 4, "zh": 2}
AXES = tuple(SIZES)
SEQ, CHAN = ("y", "zl", "core"), ("x", "zh")

N1 = 128
HALF = 72
CH = 16
BF, F32 = jnp.bfloat16, jnp.float32


def split_np(array):
    high = array.astype(np.float32).astype(ml_dtypes.bfloat16)
    low = (array - high.astype(np.float64)).astype(np.float32).astype(ml_dtypes.bfloat16)
    return high, low


@functools.cache
def tables():
    full = 2 * 8192
    freq = np.arange(HALF)[:, None]
    valid = (freq <= N1 // 2).astype(np.float64)
    block = np.arange(64)[None, :]
    angle = 2 * np.pi * (freq * block % N1) / N1
    first = np.concatenate([np.cos(angle) * valid, -np.sin(angle) * valid], 0)
    high, low = split_np(first)
    zero = np.zeros_like(high)
    first_signal = np.concatenate([high, high, low, zero], 1)
    rank = np.arange(64)
    order = 4 * (rank % 16) + rank // 16
    first_filter = np.concatenate([high[:, order], low[:, order]], 1)
    lane = np.arange(128)[None, :]
    turn = 2 * np.pi * (freq * lane) / full
    twiddle = np.stack([np.cos(turn) * valid, -np.sin(turn) * valid]).astype(np.float32)
    pair = 2 * np.pi * (np.arange(128)[:, None] * lane % 128) / 128
    cosine, sine = np.cos(pair), np.sin(pair)
    second = np.concatenate(
        [np.concatenate([cosine, -sine], 1), np.concatenate([sine, cosine], 1)], 0
    )
    second = np.stack(split_np(second))
    weight = np.where((freq == 0) | (freq == N1 // 2), 1.0, 2.0) * valid / full
    last = np.concatenate([np.cos(angle) * weight, -np.sin(angle) * weight], 0).T
    high, low = split_np(last)
    last = np.concatenate([high, high, low, np.zeros((64, 80), high.dtype)], 1)
    return first_signal, first_filter, twiddle, second, last


def halves(value):
    high = value.astype(BF)
    return high, (value - high.astype(F32)).astype(BF)


def mm(left, right, dims=(((1,), (0,)), ((), ()))):
    return lax.dot_general(left, right, dims, preferred_element_type=F32)


def seq_index():
    return (lax.axis_index("y") * 2 + lax.axis_index("zl")) * 2 + lax.axis_index("core")


def chan_index():
    return lax.axis_index("x") * 2 + lax.axis_index("zh")


def column_index():
    return lax.rem(lax.axis_index("y"), 2) * 2 + lax.axis_index("zl")


def pack_kernel(filt, tokens, payload):
    payload[:, :, :512] = filt[...].T.astype(BF).reshape(16, CH, 512)
    high = jnp.right_shift(tokens[...], 4)
    low = jnp.bitwise_and(tokens[...], 15)
    gap = jnp.zeros((4, 128), F32)
    digits = jnp.concatenate([high.astype(F32), gap, low.astype(F32), gap], 0).astype(BF)
    payload[:, :, 512:] = jnp.broadcast_to(digits[None], (16, CH, 128))


def pack(long_filter, token_ids):
    whole = pl.BlockSpec(memory_space=pltpu.VMEM)
    return pl.pallas_call(
        pack_kernel,
        out_shape=jax.ShapeDtypeStruct((16, CH, 640), BF),
        in_specs=[whole, whole],
        out_specs=whole,
        cost_estimate=pl.CostEstimate(flops=1 << 18, bytes_accessed=1 << 20, transcendentals=0),
        name="pack",
    )(long_filter, token_ids.reshape(4, 128))


def vocab_kernel(embed, weight, table, acc):
    step = pl.program_id(0)
    wide = jnp.concatenate([weight[0], weight[1], weight[2]], 1)
    part = mm(embed[...], wide)

    @pl.when(step == 0)
    def _():
        acc[...] = part

    @pl.when(step > 0)
    def _():
        acc[...] += part

    @pl.when(step == pl.num_programs(0) - 1)
    def _():
        lane = lax.broadcasted_iota(jnp.int32, (CH, 128), 1)
        row = lax.broadcasted_iota(jnp.int32, (CH, 128), 0)
        pick = (lane == row + CH * lax.rem(seq_index(), 8)).astype(F32).astype(BF)
        for branch in range(3):
            rows = acc[:, branch * 128 : (branch + 1) * 128].astype(BF)
            table[branch * CH : (branch + 1) * CH, :] = mm(pick, rows, (((1,), (1,)), ((), ())))


def vocab(embed_table, in_weight):
    steps = 8
    depth = in_weight.shape[0] // steps
    return pl.pallas_call(
        vocab_kernel,
        out_shape=jax.ShapeDtypeStruct((3 * CH, 512), F32),
        grid_spec=pltpu.PrefetchScalarGridSpec(
            num_scalar_prefetch=0,
            grid=(steps,),
            in_specs=[
                pl.BlockSpec((512, depth), lambda i: (0, i)),
                pl.BlockSpec((3, depth, 128), lambda i: (0, i, lax.div(seq_index(), 8))),
            ],
            out_specs=pl.BlockSpec((3 * CH, 512), lambda i: (0, 0)),
            scratch_shapes=[pltpu.VMEM((512, 384), F32)],
        ),
        compiler_params=pltpu.CompilerParams(dimension_semantics=("arbitrary",)),
        cost_estimate=pl.CostEstimate(flops=2 * 512 * 4096 * 384, bytes_accessed=8 << 20, transcendentals=0),
        name="vocab",
    )(embed_table, in_weight.transpose(1, 0, 2))


def convolve_kernel(
    recv, table, short, direct, first_signal, first_filter, twiddle, second, last,
    out, taps, token, gated, other, shaped, spec_high, spec_low, lags,
):
    seq, core = seq_index(), lax.axis_index("core")
    lane = lax.broadcasted_iota(jnp.int32, (CH, 256), 1)
    row = lax.broadcasted_iota(jnp.int32, (CH, 256), 0)
    mine = lane == row + CH * seq
    for index in range(10):
        wide = short[index // 3, index % 3 : index % 3 + 1, :] if index < 9 else direct[...]
        column = jnp.sum(jnp.where(mine, wide, 0.0), axis=1, keepdims=True)
        taps[index * CH : (index + 1) * CH, :] = jnp.broadcast_to(column, (CH, 128))

    for source in range(16):
        digits = recv[source, :, 512:].astype(F32)
        token[source * 8 : source * 8 + 8, :] = (digits[:8] * 16.0 + digits[8:]).astype(jnp.int32)
        for q in range(4):
            rows = slice(q * 256 + source * CH, q * 256 + (source + 1) * CH)
            lags[rows, :] = recv[source, :, q * 128 : (q + 1) * 128].astype(F32)

    position = lax.broadcasted_iota(jnp.int32, (3 * CH, 128), 1)

    def select(source, carried):
        before_one, before_two = carried
        for quarter in range(4):
            ids = jnp.broadcast_to(token[pl.ds(source * 8 + quarter, 1), :], (3 * CH, 128))
            place = jnp.bitwise_and(ids, 127)
            bank = jnp.right_shift(ids, 7)
            value = None
            for index in range(4):
                found = jnp.take_along_axis(
                    table[:, index * 128 : (index + 1) * 128], place, axis=1, mode="promise_in_bounds"
                )
                value = found if index == 0 else jnp.where(bank == index, found, value)
            one = pltpu.roll(value, 1, 1)
            two = pltpu.roll(value, 2, 1)
            lag_one = jnp.where(position < 1, before_one, one)
            lag_two = jnp.where(position < 2, before_two, two)
            before_one, before_two = one, two
            filtered = taps[: 3 * CH, :] * value
            filtered = filtered + taps[3 * CH : 6 * CH, :] * lag_one
            filtered = filtered + taps[6 * CH : 9 * CH, :] * lag_two
            rows = pl.ds(pl.multiple_of((source * 4 + quarter) * CH, CH), CH)
            gated[rows, :] = filtered[:CH] * filtered[2 * CH :]
            other[rows, :] = filtered[CH : 2 * CH]
        return before_one, before_two

    nothing = jnp.zeros((3 * CH, 128), F32)
    lax.fori_loop(0, 16, select, (nothing, nothing))

    cos_turn, sin_turn = twiddle[0], twiddle[1]
    rows_all = CH * HALF

    def turned(stage, sign):
        real, imag = stage[:HALF], stage[HALF:]
        return jnp.concatenate(
            [real * cos_turn - sign * imag * sin_turn, sign * real * sin_turn + imag * cos_turn], 1
        )

    for pair in range(CH // 2):
        signal = jnp.concatenate(
            [gated[pl.ds(2 * pair + i, 64, stride=CH), :] for i in range(2)], 1
        )
        high, low = halves(signal)
        stage = mm(first_signal[...], jnp.concatenate([high, low, high, high], 0))
        spectrum = jnp.concatenate([turned(stage[:, :128], 1), turned(stage[:, 128:], 1)], 0)
        at = slice(pair * 2 * HALF, (pair + 1) * 2 * HALF)
        spec_high[at, :], spec_low[at, :] = halves(spectrum)

        kernel = jnp.concatenate(
            [lags[pl.ds(2 * pair + i, 64, stride=CH), :] for i in range(2)], 1
        ).astype(BF)
        stage = mm(first_filter[...], jnp.concatenate([kernel, kernel], 0))
        spectrum = jnp.concatenate([turned(stage[:, :128], 1), turned(stage[:, 128:], 1)], 0)
        at = slice(rows_all + pair * 2 * HALF, rows_all + (pair + 1) * 2 * HALF)
        spec_high[at, :], spec_low[at, :] = halves(spectrum)

    def transform(at, dims):
        high, low = spec_high[at, :], spec_low[at, :]
        return mm(high, second[0], dims) + (mm(low, second[0], dims) + mm(high, second[1], dims))

    straight, flipped = (((1,), (0,)), ((), ())), (((1,), (1,)), ((), ()))
    for pair in range(CH // 2):
        at = slice(pair * 2 * HALF, (pair + 1) * 2 * HALF)
        left = transform(at, straight)
        right = transform(slice(rows_all + at.start, rows_all + at.stop), straight)
        left_real, left_imag, right_real, right_imag = left[:, :128], left[:, 128:], right[:, :128], right[:, 128:]
        product = jnp.concatenate(
            [left_real * right_real - left_imag * right_imag, left_real * right_imag + left_imag * right_real], 1
        )
        spec_high[at, :], spec_low[at, :] = halves(product)

    for pair in range(CH // 2):
        at = slice(pair * 2 * HALF, (pair + 1) * 2 * HALF)
        back = transform(at, flipped)
        columns = []
        for i in range(2):
            part = back[i * HALF : (i + 1) * HALF]
            real, imag = part[:, :128], part[:, 128:]
            columns.append(
                jnp.concatenate([real * cos_turn + imag * sin_turn, imag * cos_turn - real * sin_turn], 0)
            )
        high, low = halves(jnp.concatenate(columns, 1))
        result = mm(last[...], jnp.concatenate([high, low, high, high[:80]], 0))
        for i in range(2):
            shaped[pl.ds(2 * pair + i, 64, stride=CH), :] = result[:, i * 128 : (i + 1) * 128]

    skip = taps[9 * CH :, :]
    low_half = lax.broadcasted_iota(jnp.int32, (CH, 128), 1) < 64
    for a, top, core_to, h in itertools.product(range(2), range(2), range(2), range(4)):
        done = []
        for zl in range(2):
            shard = 8 * a + top * 4 + zl * 2 + core_to
            rows = slice((4 * shard + h) * CH, (4 * shard + h + 1) * CH)
            done.append(other[rows, :] * (shaped[rows, :] + skip * gated[rows, :]))
        first, then = done
        even = jnp.where(low_half, first, pltpu.roll(then, 64, 1)).astype(BF)
        odd = jnp.where(low_half, pltpu.roll(first, 64, 1), then).astype(BF)
        half = jnp.bitwise_xor(core, core_to) if core_to else core
        columns = pl.ds(pl.multiple_of(half * 256 + top * 128, 128), 128)
        for to_y, to_z in itertools.product(range(2), range(2)):
            out[a, to_y, to_z, 2 * h, :, columns] = even
            out[a, to_y, to_z, 2 * h + 1, :, columns] = odd


def convolve(recv, table, short_filter, skip_gain):
    consts = [jnp.asarray(c) for c in tables()]
    whole = pl.BlockSpec(memory_space=pltpu.VMEM)
    positions = 8192
    return pl.pallas_call(
        convolve_kernel,
        out_shape=jax.ShapeDtypeStruct((2, 2, 2, 8, CH, 512), BF),
        in_specs=[whole] * 9,
        out_specs=whole,
        scratch_shapes=[
            pltpu.VMEM((10 * CH, 128), F32),
            pltpu.VMEM((128, 128), jnp.int32),
            pltpu.VMEM((positions // 128 * CH, 128), F32),
            pltpu.VMEM((positions // 128 * CH, 128), F32),
            pltpu.VMEM((positions // 128 * CH, 128), F32),
            pltpu.VMEM((2 * CH * HALF, 256), BF),
            pltpu.VMEM((2 * CH * HALF, 256), BF),
            pltpu.VMEM((64 * CH, 128), F32),
        ],
        cost_estimate=pl.CostEstimate(flops=4 << 30, bytes_accessed=4 << 20, transcendentals=0),
        name="convolve",
    )(recv, table, short_filter, skip_gain[None, :], *consts)


def project_kernel(recv, *refs):
    weights, keep, send = refs[:8], refs[8], refs[9]
    total = None
    for pair in range(4):
        lhs = jnp.concatenate(
            [recv[:, jnp.bitwise_xor(chan_index(), 2 * pair + i)].reshape(128, 512) for i in range(2)], 0
        )
        rhs = jnp.concatenate([weights[2 * pair + i][...] for i in range(2)], 0)
        part = mm(lhs, rhs, (((0,), (0,)), ((), ())))
        total = part if total is None else total + part
    keep[...] = total[:256]
    send[...] = total[256:].astype(BF)


def project(recv, weights):
    whole = pl.BlockSpec(memory_space=pltpu.VMEM)
    return pl.pallas_call(
        project_kernel,
        out_shape=(jax.ShapeDtypeStruct((256, 1024), F32), jax.ShapeDtypeStruct((256, 1024), BF)),
        in_specs=[whole] * 9,
        out_specs=(whole, whole),
        cost_estimate=pl.CostEstimate(flops=1 << 30, bytes_accessed=5 << 20, transcendentals=0),
        name="project",
    )(recv.reshape(8, 8, CH, 512), *weights)


def combine_kernel(keep, came, *outs):
    for index, out in enumerate(outs):
        block = jnp.bitwise_xor(column_index(), index)
        rows = pl.ds(pl.multiple_of(block * 64, 64), 64)
        out[...] = (keep[rows, :] + came[rows, :].astype(F32)).astype(BF)


def combine(keep, came):
    whole = pl.BlockSpec(memory_space=pltpu.VMEM)
    return pl.pallas_call(
        combine_kernel,
        out_shape=(jax.ShapeDtypeStruct((64, 1024), BF),) * 4,
        in_specs=[whole, whole],
        out_specs=(whole,) * 4,
        cost_estimate=pl.CostEstimate(flops=1 << 18, bytes_accessed=2 << 20, transcendentals=0),
        name="combine",
    )(keep, came)


def assemble_kernel(*refs):
    out = refs[-1]
    for index, piece in enumerate(refs[:-1]):
        block = jnp.bitwise_xor(column_index(), index)
        out[:, pl.ds(pl.multiple_of(block * 1024, 1024), 1024)] = piece[...]


def assemble(pieces):
    whole = pl.BlockSpec(memory_space=pltpu.VMEM)
    return pl.pallas_call(
        assemble_kernel,
        out_shape=jax.ShapeDtypeStruct((64, 4096), BF),
        in_specs=[whole] * 4,
        out_specs=whole,
        cost_estimate=pl.CostEstimate(flops=0, bytes_accessed=1 << 20, transcendentals=0),
        name="assemble",
    )(*pieces)


def permuted(block, move):
    pairs = []
    for place in itertools.product(*[range(SIZES[axis]) for axis in AXES]):
        here = dict(zip(AXES, place))
        there = {**here, **move(here)}
        index = [0, 0]
        for axis in AXES:
            index = [index[0] * SIZES[axis] + here[axis], index[1] * SIZES[axis] + there[axis]]
        pairs.append(tuple(index))
    return lax.ppermute(block, AXES, pairs)


def body(token_ids, embed_table, in_weight, short_filter, long_filter, skip_gain, out_weight):
    held = lax.dynamic_slice(
        out_weight.reshape(8, 2 * CH, 4096),
        (0, lax.axis_index("core") * CH, column_index() * 1024),
        (8, CH, 1024),
    ).reshape(128, 1024)
    weights = [held]
    for index in range(1, 8):
        dx, dz = index // 2, index % 2
        weights.append(permuted(held, lambda d: {"x": d["x"] ^ dx, "zh": d["zh"] ^ dz}))
    payload = pack(long_filter, token_ids)
    recv = lax.all_to_all(payload, SEQ, 0, 0, tiled=True)
    table = vocab(embed_table, in_weight)
    chunks = convolve(recv, table, short_filter, skip_gain)
    recv = lax.all_to_all(chunks.reshape(64, CH, 512), ("y", "zl", "x", "zh"), 0, 0, tiled=True)
    keep, send = project(recv, weights)
    came = permuted(send, lambda d: {"core": 1 - d["core"]})
    pieces = list(combine(keep, came))
    for index in range(1, 4):
        pieces[index] = permuted(pieces[index], lambda d: {"y": d["y"] ^ (index // 2), "zl": d["zl"] ^ (index % 2)})
    return assemble(pieces)


def solution(mesh):
    fine = Mesh(mesh.devices.reshape(tuple(SIZES.values())), AXES)
    return jax.shard_map(
        body,
        mesh=fine,
        in_specs=(
            P(SEQ),
            P(),
            P(None, None, CHAN),
            P(None, None, CHAN),
            P(SEQ, CHAN),
            P(CHAN),
            P(CHAN, None),
        ),
        out_specs=P(AXES, None),
        check_vma=False,
    )
```

profile of v0, /device:TPU:0, one launch (start us, length us, event | category | flops | bytes accessed | tf_op | source)
XLA Modules:
  0.0 113.3 jit_solution(11527633055626197797)
XLA Ops:
  0.0 2.1 %pack.1 = bf16[16,16,640]{2,1,0:T(8,128)(2,1)} custom-call(f32[512,256]{1,0:T(8,128)} %filt.1, s32[4,128]{1,0:T(4,128)} %bitcast.19), custom_call_target="tpu_custom_call" | custom-call | flops 262144 | bytes 1048576 | tf_op jit(solution)/shard_map/pack/pallas_call | solution.py:93
  2.1 6.0 %all-to-all-start = ((bf16[16,16,640]{2,1,0:T(8,128)(2,1)}), bf16[16,16,640]{2,1,0:T(8,128)(2,1)S(1)}, u32[]{:S(2)}, u32[]{:S(2)}) async-start(bf16[16,16,640]{2,1,0:T(8,128)(2,1)} %pack.1), calls=%async_computation | async-start | bytes 655360 | tf_op jit(solution)/shard_map/all_to_all | solution.py:384
  8.1 8.4 %vocab.1.table = f32[48,512]{1,0:T(8,128)} custom-call(bf16[512,4096]{1,0:T(8,128)(2,1)} %embed.1, bf16[3,4096,256]{2,1,0:T(8,128)(2,1)} %bitcast.8), custom_call_target="tpu_custom_call" | custom-call | flops 1610612736 | bytes 8388608 | tf_op jit(solution)/shard_map/vocab/pallas_call | solution.py:129
  17.2 13.8 %convolve.1 = bf16[2,2,2,8,16,512]{5,4,3,2,1,0:T(8,128)(2,1)} custom-call(bf16[16,16,640]{2,1,0:T(8,128)(2,1)} %copy-done.3, f32[48,512]{1,0:T(8,128)} %vocab.1.table, f32[3,3,256]{2,1,0:T(4,128)} %short.1, f32[1,256]{1,0:T(1,128)} %bitcast.20, bf16[144,256]{1,0:T(8,128)(2,1)} %constant.40.clone.first_signal, bf16[144,128]{1,0:T(8,128)(2,1)} %constant.41.clone.first_filter, ...), custom_call_target="tpu_custom_call" | custom-call | flops 4294967296 | bytes 4194304 | tf_op jit(solution)/shard_map/convolve/pallas_call | solution.py:277
  31.0 11.2 %all-to-all-start.1 = ((bf16[64,16,512]{2,1,0:T(8,128)(2,1)}), bf16[64,16,512]{2,1,0:T(8,128)(2,1)S(1)}, u32[]{:S(2)}, u32[]{:S(2)}) async-start(bf16[64,16,512]{2,1,0:T(8,128)(2,1)} %bitcast.9), calls=%async_computation.1 | async-start | bytes 2097152 | tf_op jit(solution)/shard_map/all_to_all | solution.py:387
  42.3 5.3 %collective-permute-start.6 = (bf16[128,1024]{1,0:T(8,128)(2,1)S(1)}, bf16[128,1024]{1,0:T(8,128)(2,1)S(1)}, u32[]{:S(2)}, u32[]{:S(2)}) collective-permute-start(bf16[128,1024]{1,0:T(8,128)(2,1)S(1)} %bitcast.11), channel_id=1, source_target_pairs={{0,7},{1,6},{2,5},{3,4},{4,3},{5,2},{6,1},{7,0},{8,15},{9,14},{10,... | collective-permute-start | bytes 786440 | tf_op jit(solution)/shard_map/ppermute | solution.py:370
  48.1 1.8 %collective-permute-start.4 = (bf16[128,1024]{1,0:T(8,128)(2,1)S(1)}, bf16[128,1024]{1,0:T(8,128)(2,1)S(1)}, u32[]{:S(2)}, u32[]{:S(2)}) collective-permute-start(bf16[128,1024]{1,0:T(8,128)(2,1)S(1)} %bitcast.13), channel_id=1, source_target_pairs={{0,5},{1,4},{2,7},{3,6},{4,1},{5,0},{6,3},{7,2},{8,13},{9,12},{10,... | collective-permute-start | bytes 786440 | tf_op jit(solution)/shard_map/ppermute | solution.py:370
  49.9 1.7 %collective-permute-start.3 = (bf16[128,1024]{1,0:T(8,128)(2,1)S(1)}, bf16[128,1024]{1,0:T(8,128)(2,1)S(1)}, u32[]{:S(2)}, u32[]{:S(2)}) collective-permute-start(bf16[128,1024]{1,0:T(8,128)(2,1)S(1)} %bitcast.14), channel_id=1, source_target_pairs={{0,4},{1,5},{2,6},{3,7},{4,0},{5,1},{6,2},{7,3},{8,12},{9,13},{10,... | collective-permute-start | bytes 786440 | tf_op jit(solution)/shard_map/ppermute | solution.py:370
  51.5 2.8 %collective-permute-start.2 = (bf16[128,1024]{1,0:T(8,128)(2,1)S(1)}, bf16[128,1024]{1,0:T(8,128)(2,1)S(1)}, u32[]{:S(2)}, u32[]{:S(2)}) collective-permute-start(bf16[128,1024]{1,0:T(8,128)(2,1)S(1)} %bitcast.15), channel_id=1, source_target_pairs={{0,3},{1,2},{2,1},{3,0},{4,7},{5,6},{6,5},{7,4},{8,11},{9,10},{10,... | collective-permute-start | bytes 786440 | tf_op jit(solution)/shard_map/ppermute | solution.py:370
  54.3 25.5 %collective-permute-done.6.refs_7_ = bf16[128,1024]{1,0:T(8,128)(2,1)S(1)} collective-permute-done((bf16[128,1024]{1,0:T(8,128)(2,1)S(1)}, bf16[128,1024]{1,0:T(8,128)(2,1)S(1)}, u32[]{:S(2)}, u32[]{:S(2)}) %collective-permute-start.6) | collective-permute-done | bytes 262176 | tf_op jit(solution)/shard_map/ppermute | solution.py:370
  79.9 1.5 %collective-permute-done.5.refs_6_ = bf16[128,1024]{1,0:T(8,128)(2,1)S(1)} collective-permute-done((bf16[128,1024]{1,0:T(8,128)(2,1)S(1)}, bf16[128,1024]{1,0:T(8,128)(2,1)S(1)}, u32[]{:S(2)}, u32[]{:S(2)}) %collective-permute-start.5) | collective-permute-done | bytes 262176 | tf_op jit(solution)/shard_map/ppermute | solution.py:370
  81.4 2.5 %collective-permute-start = (bf16[128,1024]{1,0:T(8,128)(2,1)S(1)}, bf16[128,1024]{1,0:T(8,128)(2,1)}, u32[]{:S(2)}, u32[]{:S(2)}) collective-permute-start(bf16[128,1024]{1,0:T(8,128)(2,1)S(1)} %bitcast.17), channel_id=1, source_target_pairs={{0,1},{1,0},{2,3},{3,2},{4,5},{5,4},{6,7},{7,6},{8,9},{9,8},{10,11... | collective-permute-start | bytes 786440 | tf_op jit(solution)/shard_map/ppermute | solution.py:370
  84.0 2.5 %collective-permute-done.1.refs_2_ = bf16[128,1024]{1,0:T(8,128)(2,1)S(1)} collective-permute-done((bf16[128,1024]{1,0:T(8,128)(2,1)S(1)}, bf16[128,1024]{1,0:T(8,128)(2,1)S(1)}, u32[]{:S(2)}, u32[]{:S(2)}) %collective-permute-start.1) | collective-permute-done | bytes 262176 | tf_op jit(solution)/shard_map/ppermute | solution.py:370
  87.2 3.5 %collective-permute-done.refs_1_ = bf16[128,1024]{1,0:T(8,128)(2,1)} collective-permute-done((bf16[128,1024]{1,0:T(8,128)(2,1)S(1)}, bf16[128,1024]{1,0:T(8,128)(2,1)}, u32[]{:S(2)}, u32[]{:S(2)}) %collective-permute-start) | collective-permute-done | bytes 262176 | tf_op jit(solution)/shard_map/ppermute | solution.py:370
  90.7 1.0 copy-done.1
  91.7 4.2 %project.1 = (f32[256,1024]{1,0:T(8,128)}, bf16[256,1024]{1,0:T(8,128)(2,1)}) custom-call(bf16[8,8,16,512]{3,2,1,0:T(8,128)(2,1)} %bitcast.10, bf16[128,1024]{1,0:T(8,128)(2,1)} %bitcast.18, bf16[128,1024]{1,0:T(8,128)(2,1)} %collective-permute-done.refs_1_, bf16[128,1024]{1,0:T(8,128)(2,1)} %copy-done.13, bf16[128,1024]{1,0:T(8,128)(2,1)} %copy-done.12, ...), custom_call_target="tpu_custom_call" | custom-call | flops 1073741824 | bytes 5242880 | tf_op jit(solution)/shard_map/project/pallas_call | solution.py:313
  95.9 2.1 %collective-permute-done.7.came = bf16[256,1024]{1,0:T(8,128)(2,1)S(1)} collective-permute-done((bf16[256,1024]{1,0:T(8,128)(2,1)}, bf16[256,1024]{1,0:T(8,128)(2,1)S(1)}, u32[]{:S(2)}, u32[]{:S(2)}) %collective-permute-start.7) | collective-permute-done | bytes 524320 | tf_op jit(solution)/shard_map/ppermute | solution.py:370
  98.8 2.2 %combine.1 = (bf16[64,1024]{1,0:T(8,128)(2,1)}, bf16[64,1024]{1,0:T(8,128)(2,1)}, bf16[64,1024]{1,0:T(8,128)(2,1)}, bf16[64,1024]{1,0:T(8,128)(2,1)}) custom-call(f32[256,1024]{1,0:T(8,128)} %get-tuple-element.11.keep, bf16[256,1024]{1,0:T(8,128)(2,1)} %copy-done.2), custom_call_target="tpu_custom_call" | custom-call | flops 262144 | bytes 2097152 | tf_op jit(solution)/shard_map/combine/pallas_call | solution.py:332
  101.0 1.7 %collective-permute-start.8 = (bf16[64,1024]{1,0:T(8,128)(2,1)}, bf16[64,1024]{1,0:T(8,128)(2,1)S(1)}, u32[]{:S(2)}, u32[]{:S(2)}) collective-permute-start(bf16[64,1024]{1,0:T(8,128)(2,1)} %get-tuple-element.14), channel_id=1, source_target_pairs={{0,16},{1,17},{2,18},{3,19},{4,20},{5,21},{6,22},{7,23},{8,24},{9,... | collective-permute-start | bytes 393224 | tf_op jit(solution)/shard_map/ppermute | solution.py:370
  103.2 1.3 %collective-permute-start.10 = (bf16[64,1024]{1,0:T(8,128)(2,1)}, bf16[64,1024]{1,0:T(8,128)(2,1)S(1)}, u32[]{:S(2)}, u32[]{:S(2)}) collective-permute-start(bf16[64,1024]{1,0:T(8,128)(2,1)} %get-tuple-element.16), channel_id=1, source_target_pairs={{0,48},{1,49},{2,50},{3,51},{4,52},{5,53},{6,54},{7,55},{8,56},{9,... | collective-permute-start | bytes 393224 | tf_op jit(solution)/shard_map/ppermute | solution.py:370
  104.5 2.3 %collective-permute-done.8.refs_1_ = bf16[64,1024]{1,0:T(8,128)(2,1)S(1)} collective-permute-done((bf16[64,1024]{1,0:T(8,128)(2,1)}, bf16[64,1024]{1,0:T(8,128)(2,1)S(1)}, u32[]{:S(2)}, u32[]{:S(2)}) %collective-permute-start.8) | collective-permute-done | bytes 131104 | tf_op jit(solution)/shard_map/ppermute | solution.py:370
  106.8 2.6 %collective-permute-done.9.refs_2_ = bf16[64,1024]{1,0:T(8,128)(2,1)S(1)} collective-permute-done((bf16[64,1024]{1,0:T(8,128)(2,1)}, bf16[64,1024]{1,0:T(8,128)(2,1)S(1)}, u32[]{:S(2)}, u32[]{:S(2)}) %collective-permute-start.9) | collective-permute-done | bytes 131104 | tf_op jit(solution)/shard_map/ppermute | solution.py:370
  109.3 1.4 %collective-permute-done.10.refs_3_ = bf16[64,1024]{1,0:T(8,128)(2,1)S(1)} collective-permute-done((bf16[64,1024]{1,0:T(8,128)(2,1)}, bf16[64,1024]{1,0:T(8,128)(2,1)S(1)}, u32[]{:S(2)}, u32[]{:S(2)}) %collective-permute-start.10) | collective-permute-done | bytes 131104 | tf_op jit(solution)/shard_map/ppermute | solution.py:370
  111.4 1.9 %assemble.1 = bf16[64,4096]{1,0:T(8,128)(2,1)} custom-call(bf16[64,1024]{1,0:T(8,128)(2,1)} %get-tuple-element.13.refs_0_, bf16[64,1024]{1,0:T(8,128)(2,1)} %copy-done.5, bf16[64,1024]{1,0:T(8,128)(2,1)} %copy-done.6, bf16[64,1024]{1,0:T(8,128)(2,1)} %copy-done.7), custom_call_target="tpu_custom_call" | custom-call | bytes 1048576 | tf_op jit(solution)/shard_map/assemble/pallas_call | solution.py:351
  (37 shorter events, 4.0 us)
Async XLA Ops:
  0.0 42.2 %copy-start = (bf16[256,4096]{1,0:T(8,128)(2,1)S(1)}, bf16[256,4096]{1,0:T(8,128)(2,1)}, u32[]{:S(2)}) copy-start(bf16[256,4096]{1,0:T(8,128)(2,1)} %param.18) | copy-start | bytes 6291460
  2.1 14.4 %all-to-all-start = ((bf16[16,16,640]{2,1,0:T(8,128)(2,1)}), bf16[16,16,640]{2,1,0:T(8,128)(2,1)S(1)}, u32[]{:S(2)}, u32[]{:S(2)}) async-start(bf16[16,16,640]{2,1,0:T(8,128)(2,1)} %pack.1), calls=%async_computation | async-start | bytes 655360 | tf_op jit(solution)/shard_map/all_to_all | solution.py:384
  31.0 59.7 %all-to-all-start.1 = ((bf16[64,16,512]{2,1,0:T(8,128)(2,1)}), bf16[64,16,512]{2,1,0:T(8,128)(2,1)S(1)}, u32[]{:S(2)}, u32[]{:S(2)}) async-start(bf16[64,16,512]{2,1,0:T(8,128)(2,1)} %bitcast.9), calls=%async_computation.1 | async-start | bytes 2097152 | tf_op jit(solution)/shard_map/all_to_all | solution.py:387
  42.3 48.4 %copy-start.4 = (bf16[8,16,1024]{2,1,0:T(8,128)(2,1)}, bf16[8,16,1024]{2,1,0:T(8,128)(2,1)S(1)}, u32[]{:S(2)}) copy-start(bf16[8,16,1024]{2,1,0:T(8,128)(2,1)S(1)} %constant_dynamic-slice_fusion) | copy-start | bytes 786436
  42.3 37.6 %collective-permute-start.6 = (bf16[128,1024]{1,0:T(8,128)(2,1)S(1)}, bf16[128,1024]{1,0:T(8,128)(2,1)S(1)}, u32[]{:S(2)}, u32[]{:S(2)}) collective-permute-start(bf16[128,1024]{1,0:T(8,128)(2,1)S(1)} %bitcast.11), channel_id=1, source_target_pairs={{0,7},{1,6},{2,5},{3,4},{4,3},{5,2},{6,1},{7,0},{8,15},{9,14},{10,... | collective-permute-start | bytes 786440 | tf_op jit(solution)/shard_map/ppermute | solution.py:370
  47.6 33.8 %collective-permute-start.5 = (bf16[128,1024]{1,0:T(8,128)(2,1)S(1)}, bf16[128,1024]{1,0:T(8,128)(2,1)S(1)}, u32[]{:S(2)}, u32[]{:S(2)}) collective-permute-start(bf16[128,1024]{1,0:T(8,128)(2,1)S(1)} %bitcast.12), channel_id=1, source_target_pairs={{0,6},{1,7},{2,4},{3,5},{4,2},{5,3},{6,0},{7,1},{8,14},{9,15},{10,... | collective-permute-start | bytes 786440 | tf_op jit(solution)/shard_map/ppermute | solution.py:370
  48.1 35.8 %collective-permute-start.4 = (bf16[128,1024]{1,0:T(8,128)(2,1)S(1)}, bf16[128,1024]{1,0:T(8,128)(2,1)S(1)}, u32[]{:S(2)}, u32[]{:S(2)}) collective-permute-start(bf16[128,1024]{1,0:T(8,128)(2,1)S(1)} %bitcast.13), channel_id=1, source_target_pairs={{0,5},{1,4},{2,7},{3,6},{4,1},{5,0},{6,3},{7,2},{8,13},{9,12},{10,... | collective-permute-start | bytes 786440 | tf_op jit(solution)/shard_map/ppermute | solution.py:370
  49.9 34.1 %collective-permute-start.3 = (bf16[128,1024]{1,0:T(8,128)(2,1)S(1)}, bf16[128,1024]{1,0:T(8,128)(2,1)S(1)}, u32[]{:S(2)}, u32[]{:S(2)}) collective-permute-start(bf16[128,1024]{1,0:T(8,128)(2,1)S(1)} %bitcast.14), channel_id=1, source_target_pairs={{0,4},{1,5},{2,6},{3,7},{4,0},{5,1},{6,2},{7,3},{8,12},{9,13},{10,... | collective-permute-start | bytes 786440 | tf_op jit(solution)/shard_map/ppermute | solution.py:370
  51.5 32.4 %collective-permute-start.2 = (bf16[128,1024]{1,0:T(8,128)(2,1)S(1)}, bf16[128,1024]{1,0:T(8,128)(2,1)S(1)}, u32[]{:S(2)}, u32[]{:S(2)}) collective-permute-start(bf16[128,1024]{1,0:T(8,128)(2,1)S(1)} %bitcast.15), channel_id=1, source_target_pairs={{0,3},{1,2},{2,1},{3,0},{4,7},{5,6},{6,5},{7,4},{8,11},{9,10},{10,... | collective-permute-start | bytes 786440 | tf_op jit(solution)/shard_map/ppermute | solution.py:370
  79.8 6.6 %copy-start.8 = (bf16[128,1024]{1,0:T(8,128)(2,1)}, bf16[128,1024]{1,0:T(8,128)(2,1)S(1)}, u32[]{:S(2)}) copy-start(bf16[128,1024]{1,0:T(8,128)(2,1)S(1)} %collective-permute-done.6.refs_7_) | copy-start | bytes 786436
  79.8 6.6 %collective-permute-start.1 = (bf16[128,1024]{1,0:T(8,128)(2,1)S(1)}, bf16[128,1024]{1,0:T(8,128)(2,1)S(1)}, u32[]{:S(2)}, u32[]{:S(2)}) collective-permute-start(bf16[128,1024]{1,0:T(8,128)(2,1)S(1)} %bitcast.16), channel_id=1, source_target_pairs={{0,2},{1,3},{2,0},{3,1},{4,6},{5,7},{6,4},{7,5},{8,10},{9,11},{10,... | collective-permute-start | bytes 786440 | tf_op jit(solution)/shard_map/ppermute | solution.py:370
  81.4 5.1 %copy-start.9 = (bf16[128,1024]{1,0:T(8,128)(2,1)}, bf16[128,1024]{1,0:T(8,128)(2,1)S(1)}, u32[]{:S(2)}) copy-start(bf16[128,1024]{1,0:T(8,128)(2,1)S(1)} %collective-permute-done.5.refs_6_) | copy-start | bytes 786436
  81.4 9.3 %collective-permute-start = (bf16[128,1024]{1,0:T(8,128)(2,1)S(1)}, bf16[128,1024]{1,0:T(8,128)(2,1)}, u32[]{:S(2)}, u32[]{:S(2)}) collective-permute-start(bf16[128,1024]{1,0:T(8,128)(2,1)S(1)} %bitcast.17), channel_id=1, source_target_pairs={{0,1},{1,0},{2,3},{3,2},{4,5},{5,4},{6,7},{7,6},{8,9},{9,8},{10,11... | collective-permute-start | bytes 786440 | tf_op jit(solution)/shard_map/ppermute | solution.py:370
  83.9 2.5 %copy-start.10 = (bf16[128,1024]{1,0:T(8,128)(2,1)}, bf16[128,1024]{1,0:T(8,128)(2,1)S(1)}, u32[]{:S(2)}) copy-start(bf16[128,1024]{1,0:T(8,128)(2,1)S(1)} %collective-permute-done.4.refs_5_) | copy-start | bytes 786436
  83.9 2.5 %copy-start.11 = (bf16[128,1024]{1,0:T(8,128)(2,1)}, bf16[128,1024]{1,0:T(8,128)(2,1)S(1)}, u32[]{:S(2)}) copy-start(bf16[128,1024]{1,0:T(8,128)(2,1)S(1)} %collective-permute-done.3.refs_4_) | copy-start | bytes 786436
  84.0 2.5 %copy-start.12 = (bf16[128,1024]{1,0:T(8,128)(2,1)}, bf16[128,1024]{1,0:T(8,128)(2,1)S(1)}, u32[]{:S(2)}) copy-start(bf16[128,1024]{1,0:T(8,128)(2,1)S(1)} %collective-permute-done.2.refs_3_) | copy-start | bytes 786436
  90.7 1.0 copy-start.1
  95.9 2.1 %collective-permute-start.7 = (bf16[256,1024]{1,0:T(8,128)(2,1)}, bf16[256,1024]{1,0:T(8,128)(2,1)S(1)}, u32[]{:S(2)}, u32[]{:S(2)}) collective-permute-start(bf16[256,1024]{1,0:T(8,128)(2,1)} %get-tuple-element.12), channel_id=1, source_target_pairs={{0,8},{1,9},{2,10},{3,11},{4,12},{5,13},{6,14},{7,15},{8,0},{9,1},... | collective-permute-start | bytes 1572872 | tf_op jit(solution)/shard_map/ppermute | solution.py:370
  98.0 0.8 copy-start.2
  101.0 5.8 %collective-permute-start.8 = (bf16[64,1024]{1,0:T(8,128)(2,1)}, bf16[64,1024]{1,0:T(8,128)(2,1)S(1)}, u32[]{:S(2)}, u32[]{:S(2)}) collective-permute-start(bf16[64,1024]{1,0:T(8,128)(2,1)} %get-tuple-element.14), channel_id=1, source_target_pairs={{0,16},{1,17},{2,18},{3,19},{4,20},{5,21},{6,22},{7,23},{8,24},{9,... | collective-permute-start | bytes 393224 | tf_op jit(solution)/shard_map/ppermute | solution.py:370
  102.8 6.6 %collective-permute-start.9 = (bf16[64,1024]{1,0:T(8,128)(2,1)}, bf16[64,1024]{1,0:T(8,128)(2,1)S(1)}, u32[]{:S(2)}, u32[]{:S(2)}) collective-permute-start(bf16[64,1024]{1,0:T(8,128)(2,1)} %get-tuple-element.15), channel_id=1, source_target_pairs={{0,32},{1,33},{2,34},{3,35},{4,36},{5,37},{6,38},{7,39},{8,40},{9,... | collective-permute-start | bytes 393224 | tf_op jit(solution)/shard_map/ppermute | solution.py:370
  103.2 7.5 %collective-permute-start.10 = (bf16[64,1024]{1,0:T(8,128)(2,1)}, bf16[64,1024]{1,0:T(8,128)(2,1)S(1)}, u32[]{:S(2)}, u32[]{:S(2)}) collective-permute-start(bf16[64,1024]{1,0:T(8,128)(2,1)} %get-tuple-element.16), channel_id=1, source_target_pairs={{0,48},{1,49},{2,50},{3,51},{4,52},{5,53},{6,54},{7,55},{8,56},{9,... | collective-permute-start | bytes 393224 | tf_op jit(solution)/shard_map/ppermute | solution.py:370
  106.8 4.0 %copy-start.5 = (bf16[64,1024]{1,0:T(8,128)(2,1)}, bf16[64,1024]{1,0:T(8,128)(2,1)S(1)}, u32[]{:S(2)}) copy-start(bf16[64,1024]{1,0:T(8,128)(2,1)S(1)} %collective-permute-done.8.refs_1_) | copy-start | bytes 393220
  109.3 1.4 %copy-start.6 = (bf16[64,1024]{1,0:T(8,128)(2,1)}, bf16[64,1024]{1,0:T(8,128)(2,1)S(1)}, u32[]{:S(2)}) copy-start(bf16[64,1024]{1,0:T(8,128)(2,1)S(1)} %collective-permute-done.9.refs_2_) | copy-start | bytes 393220
  (3 other events, 2.1 us)
where the time goes:
time: 114 us; the launch traced here: 113 us
  waiting for transfers between devices  41.4 us (36%)
  starting transfers between devices  35.3 us (31%)
  Pallas kernels  32.6 us (29%)
  local copies, waits for them, and re-layouts  3.9 us (3%)
    ppermute x11, waiting for transfers between devices, permuted(): return lax.ppermute(block, AXES, pairs)  41.4 us
    ppermute x11, starting transfers between devices, permuted(): return lax.ppermute(block, AXES, pairs)  18 us
    pallas_call x1, Pallas kernels, convolve(): pl.pallas_call(convolve_kernel, out_shape=jax.ShapeDtypeStruct((2, 2, 2,...  13.8 us
    all_to_all x1, starting transfers between devices, body(): lax.all_to_all(chunks.reshape(64, CH, 512), ('y', 'zl', 'x', 'zh'), 0, 0,...  11.2 us
    pallas_call x1, Pallas kernels, vocab(): pl.pallas_call(vocab_kernel, out_shape=jax.ShapeDtypeStruct((3 * CH, 512)...  8.35 us
    all_to_all x1, starting transfers between devices, body(): recv = lax.all_to_all(payload, SEQ, 0, 0, tiled=True)  6.04 us
    pallas_call x1, Pallas kernels, project(): pl.pallas_call(project_kernel, out_shape=(jax.ShapeDtypeStruct((256, 1024...  4.17 us
    unnamed x28, local copies, waits for them, and re-layouts  3.87 us
  transfers between devices with their start and end apart: 13, of which 8 were waited for; matrix products, arithmetic and copies ran while one was open for 0% of the time, Pallas kernels for 7%

commit v1 on v0

--- a/solution.py
+++ b/solution.py
@@ -71,10 +71,6 @@
     return (lax.axis_index("y") * 2 + lax.axis_index("zl")) * 2 + lax.axis_index("core")
 
 
-def chan_index():
-    return lax.axis_index("x") * 2 + lax.axis_index("zh")
-
-
 def column_index():
     return lax.rem(lax.axis_index("y"), 2) * 2 + lax.axis_index("zl")
 
@@ -96,6 +92,7 @@
         in_specs=[whole, whole],
         out_specs=whole,
         cost_estimate=pl.CostEstimate(flops=1 << 18, bytes_accessed=1 << 20, transcendentals=0),
+        compiler_params=pltpu.CompilerParams(vmem_limit_bytes=6 << 20),
         name="pack",
     )(long_filter, token_ids.reshape(4, 128))
 
@@ -139,7 +136,9 @@
             out_specs=pl.BlockSpec((3 * CH, 512), lambda i: (0, 0)),
             scratch_shapes=[pltpu.VMEM((512, 384), F32)],
         ),
-        compiler_params=pltpu.CompilerParams(dimension_semantics=("arbitrary",)),
+        compiler_params=pltpu.CompilerParams(
+            dimension_semantics=("arbitrary",), vmem_limit_bytes=61 << 20
+        ),
         cost_estimate=pl.CostEstimate(flops=2 * 512 * 4096 * 384, bytes_accessed=8 << 20, transcendentals=0),
         name="vocab",
     )(embed_table, in_weight.transpose(1, 0, 2))
@@ -290,19 +289,20 @@
             pltpu.VMEM((64 * CH, 128), F32),
         ],
         cost_estimate=pl.CostEstimate(flops=4 << 30, bytes_accessed=4 << 20, transcendentals=0),
+        compiler_params=pltpu.CompilerParams(vmem_limit_bytes=20 << 20),
         name="convolve",
     )(recv, table, short_filter, skip_gain[None, :], *consts)
 
 
 def project_kernel(recv, *refs):
-    weights, keep, send = refs[:8], refs[8], refs[9]
+    weights, keep, send = refs[:4], refs[4], refs[5]
+    chan = lax.axis_index("x") * 2 + lax.axis_index("zh")
     total = None
-    for pair in range(4):
+    for index in range(4):
         lhs = jnp.concatenate(
-            [recv[:, jnp.bitwise_xor(chan_index(), 2 * pair + i)].reshape(128, 512) for i in range(2)], 0
+            [recv[:, jnp.bitwise_xor(chan, 2 * index + i)].reshape(128, 512) for i in range(2)], 0
         )
-        rhs = jnp.concatenate([weights[2 * pair + i][...] for i in range(2)], 0)
-        part = mm(lhs, rhs, (((0,), (0,)), ((), ())))
+        part = mm(lhs, weights[index][...], (((0,), (0,)), ((), ())))
         total = part if total is None else total + part
     keep[...] = total[:256]
     send[...] = total[256:].astype(BF)
@@ -313,9 +313,10 @@
     return pl.pallas_call(
         project_kernel,
         out_shape=(jax.ShapeDtypeStruct((256, 1024), F32), jax.ShapeDtypeStruct((256, 1024), BF)),
-        in_specs=[whole] * 9,
+        in_specs=[whole] * 5,
         out_specs=(whole, whole),
         cost_estimate=pl.CostEstimate(flops=1 << 30, bytes_accessed=5 << 20, transcendentals=0),
+        compiler_params=pltpu.CompilerParams(vmem_limit_bytes=20 << 20),
         name="project",
     )(recv.reshape(8, 8, CH, 512), *weights)
 
@@ -335,6 +336,7 @@
         in_specs=[whole, whole],
         out_specs=(whole,) * 4,
         cost_estimate=pl.CostEstimate(flops=1 << 18, bytes_accessed=2 << 20, transcendentals=0),
+        compiler_params=pltpu.CompilerParams(vmem_limit_bytes=6 << 20),
         name="combine",
     )(keep, came)
 
@@ -354,6 +356,7 @@
         in_specs=[whole] * 4,
         out_specs=whole,
         cost_estimate=pl.CostEstimate(flops=0, bytes_accessed=1 << 20, transcendentals=0),
+        compiler_params=pltpu.CompilerParams(vmem_limit_bytes=4 << 20),
         name="assemble",
     )(*pieces)
 
@@ -376,10 +379,11 @@
         (0, lax.axis_index("core") * CH, column_index() * 1024),
         (8, CH, 1024),
     ).reshape(128, 1024)
-    weights = [held]
-    for index in range(1, 8):
-        dx, dz = index // 2, index % 2
-        weights.append(permuted(held, lambda d: {"x": d["x"] ^ dx, "zh": d["zh"] ^ dz}))
+    across = permuted(held, lambda d: {"zh": d["zh"] ^ 1})
+    both = jnp.concatenate([held, across], 0)
+    weights = [both]
+    for index in range(1, 4):
+        weights.append(permuted(both, lambda d: {"x": d["x"] ^ index}))
     payload = pack(long_filter, token_ids)
     recv = lax.all_to_all(payload, SEQ, 0, 0, tiled=True)
     table = vocab(embed_table, in_weight)
@@ -389,7 +393,9 @@
     came = permuted(send, lambda d: {"core": 1 - d["core"]})
     pieces = list(combine(keep, came))
     for index in range(1, 4):
-        pieces[index] = permuted(pieces[index], lambda d: {"y": d["y"] ^ (index // 2), "zl": d["zl"] ^ (index % 2)})
+        pieces[index] = permuted(
+            pieces[index], lambda d: {"y": d["y"] ^ (index // 2), "zl": d["zl"] ^ (index % 2)}
+        )
     return assemble(pieces)
 
 

time: 114 us -> 110 us (0.965)
  Pallas kernels: 32.6 us -> 24.1 us
  starting transfers between devices: 35.3 us -> 28.2 us
  local copies, waits for them, and re-layouts: 3.9 us -> 10.2 us
  waiting for transfers between devices: 41.4 us -> 46.8 us
    ppermute x11 -> x8, starting transfers between devices: 18 us -> 11 us  [permuted(): return lax.ppermute(block, AXES, pairs)]
    unnamed x28 -> x38, local copies, waits for them, and re-layouts: 3.87 us -> 10.2 us
    ppermute x11 -> x8, waiting for transfers between devices: 41.4 us -> 46.8 us  [permuted(): return lax.ppermute(block, AXES, pairs)]
    pallas_call x1, Pallas kernels: 4.17 us -> 1.28 us  [project(): pl.pallas_call(project_kernel, out_shape=(jax.ShapeDtypeStruct((256, 1024...]
    pallas_call x1, Pallas kernels: 2.24 us -> 0.09 us  [combine(): pl.pallas_call(combine_kernel, out_shape=(jax.ShapeDtypeStruct((64, 1024)...]
    pallas_call x1, Pallas kernels: 13.8 us -> 12.6 us  [convolve(): pl.pallas_call(convolve_kernel, out_shape=jax.ShapeDtypeStruct((2, 2, 2,...]
    pallas_call x1, Pallas kernels: 2.05 us -> 0.86 us  [pack(): pl.pallas_call(pack_kernel, out_shape=jax.ShapeDtypeStruct((16, CH, 640),...]
  transfers between devices with their start and end apart: 13 -> 10, of which waited for: 8 -> 6; matrix products, arithmetic and copies ran while one was open for 0% -> 0% of each run, Pallas kernels for 7% -> 8%
where the time goes in v1:
time: 110 us
  waiting for transfers between devices  46.8 us (43%)
  starting transfers between devices  28.2 us (26%)
  Pallas kernels  24.1 us (22%)
  local copies, waits for them, and re-layouts  10.2 us (9%)
    ppermute x8, waiting for transfers between devices, permuted(): return lax.ppermute(block, AXES, pairs)  46.8 us
    pallas_call x1, Pallas kernels, convolve(): pl.pallas_call(convolve_kernel, out_shape=jax.ShapeDtypeStruct((2, 2, 2,...  12.6 us
    all_to_all x1, starting transfers between devices, body(): lax.all_to_all(chunks.reshape(64, CH, 512), ('y', 'zl', 'x', 'zh'), 0, 0,...  11.2 us
    ppermute x8, starting transfers between devices, permuted(): return lax.ppermute(block, AXES, pairs)  11 us
    unnamed x38, local copies, waits for them, and re-layouts  10.2 us
    pallas_call x1, Pallas kernels, vocab(): pl.pallas_call(vocab_kernel, out_shape=jax.ShapeDtypeStruct((3 * CH, 512)...  8.42 us
    all_to_all x1, starting transfers between devices, body(): recv = lax.all_to_all(payload, SEQ, 0, 0, tiled=True)  6.04 us
  transfers between devices with their start and end apart: 10, of which 6 were waited for; matrix products, arithmetic and copies ran while one was open for 0% of the time, Pallas kernels for 8%

profile of v1, /device:TPU:0, one launch (start us, length us, event | category | flops | bytes accessed | tf_op | source)
XLA Modules:
  0.0 109.6 jit_solution(3748256805873925691)
XLA Ops:
  0.0 1.2 %copy-done.3 = f32[512,256]{1,0:T(8,128)S(1)} copy-done((f32[512,256]{1,0:T(8,128)S(1)}, f32[512,256]{1,0:T(8,128)}, u32[]{:S(2)}) %copy-start.3) | copy-done | bytes 524312
  1.9 0.9 pack.1
  2.7 6.0 %all-to-all-start = ((bf16[16,16,640]{2,1,0:T(8,128)(2,1)}), bf16[16,16,640]{2,1,0:T(8,128)(2,1)S(1)}, u32[]{:S(2)}, u32[]{:S(2)}) async-start(bf16[16,16,640]{2,1,0:T(8,128)(2,1)} %pack.1), calls=%async_computation | async-start | bytes 655360 | tf_op jit(solution)/shard_map/all_to_all | solution.py:388
  8.9 8.4 %vocab.1.table = f32[48,512]{1,0:T(8,128)} custom-call(bf16[512,4096]{1,0:T(8,128)(2,1)} %embed.1, bf16[3,4096,256]{2,1,0:T(8,128)(2,1)} %bitcast.11), custom_call_target="tpu_custom_call" | custom-call | flops 1610612736 | bytes 8388608 | tf_op jit(solution)/shard_map/vocab/pallas_call | solution.py:126
  17.4 0.9 copy-done.4
  18.3 12.6 %convolve.1 = bf16[2,2,2,8,16,512]{5,4,3,2,1,0:T(8,128)(2,1)} custom-call(bf16[16,16,640]{2,1,0:T(8,128)(2,1)S(1)} %all-to-all-done.recv, f32[48,512]{1,0:T(8,128)S(1)} %copy-done.4, f32[3,3,256]{2,1,0:T(4,128)S(1)} %copy-done.12, f32[1,256]{1,0:T(1,128)S(1)} %bitcast.10, bf16[144,256]{1,0:T(8,128)(2,1)S(1)} %copy-done.16, bf16[144,128]{1,0:T(8,128)(2,1)S(1)} %copy-done.18, ...), custom_call_target="tpu_custom_call" | custom-call | flops 4294967296 | bytes 4194304 | tf_op jit(solution)/shard_map/convolve/pallas_call | solution.py:276
  30.9 11.2 %all-to-all-start.1 = ((bf16[64,16,512]{2,1,0:T(8,128)(2,1)}), bf16[64,16,512]{2,1,0:T(8,128)(2,1)S(1)}, u32[]{:S(2)}, u32[]{:S(2)}) async-start(bf16[64,16,512]{2,1,0:T(8,128)(2,1)} %bitcast.3), calls=%async_computation.1 | async-start | bytes 2097152 | tf_op jit(solution)/shard_map/all_to_all | solution.py:391
  42.1 3.2 %collective-permute-start = (bf16[128,1024]{1,0:T(8,128)(2,1)S(1)}, bf16[128,1024]{1,0:T(8,128)(2,1)S(1)}, u32[]{:S(2)}, u32[]{:S(2)}) collective-permute-start(bf16[128,1024]{1,0:T(8,128)(2,1)S(1)} %bitcast.12), channel_id=1, source_target_pairs={{0,1},{1,0},{2,3},{3,2},{4,5},{5,4},{6,7},{7,6},{8,9},{9,8},{10,11... | collective-permute-start | bytes 786440 | tf_op jit(solution)/shard_map/ppermute | solution.py:373
  45.3 18.1 %collective-permute-done = bf16[128,1024]{1,0:T(8,128)(2,1)S(1)} collective-permute-done((bf16[128,1024]{1,0:T(8,128)(2,1)S(1)}, bf16[128,1024]{1,0:T(8,128)(2,1)S(1)}, u32[]{:S(2)}, u32[]{:S(2)}) %collective-permute-start) | collective-permute-done | bytes 262176 | tf_op jit(solution)/shard_map/ppermute | solution.py:373
  63.4 2.2 %collective-permute-start.3 = (bf16[256,1024]{1,0:T(8,128)(2,1)S(1)}, bf16[256,1024]{1,0:T(8,128)(2,1)S(1)}, u32[]{:S(2)}, u32[]{:S(2)}) collective-permute-start(bf16[256,1024]{1,0:T(8,128)(2,1)S(1)} %pad_maximum_fusion.refs_0_), channel_id=1, source_target_pairs={{0,6},{1,7},{2,4},{3,5},{4,2},{5,3},{6,0},{7,1},{8,14},{9,15},{10,... | collective-permute-start | bytes 1572872 | tf_op jit(solution)/shard_map/ppermute | solution.py:373
  65.7 1.1 collective-permute-start.2
  68.4 20.8 %collective-permute-done.3.refs_3_ = bf16[256,1024]{1,0:T(8,128)(2,1)S(1)} collective-permute-done((bf16[256,1024]{1,0:T(8,128)(2,1)S(1)}, bf16[256,1024]{1,0:T(8,128)(2,1)S(1)}, u32[]{:S(2)}, u32[]{:S(2)}) %collective-permute-start.3) | collective-permute-done | bytes 524320 | tf_op jit(solution)/shard_map/ppermute | solution.py:373
  91.6 1.0 copy-done.2
  92.7 1.0 copy-done.7
  93.7 1.0 copy-done.9
  94.8 1.0 copy-done.11
  95.8 1.3 %project.1 = (f32[256,1024]{1,0:T(8,128)S(1)}, bf16[256,1024]{1,0:T(8,128)(2,1)S(1)}) custom-call(bf16[8,8,16,512]{3,2,1,0:T(8,128)(2,1)S(1)} %bitcast.8, bf16[256,1024]{1,0:T(8,128)(2,1)S(1)} %copy-done.2, bf16[256,1024]{1,0:T(8,128)(2,1)S(1)} %copy-done.11, bf16[256,1024]{1,0:T(8,128)(2,1)S(1)} %copy-done.9, bf16[256,1024]{1,0:T(8,128)(2,1)S(1)} %copy-done.7), custom_call_target="tpu_custom_call" | custom-call | flops 1073741824 | bytes 5242880 | tf_op jit(solution)/shard_map/project/pallas_call | solution.py:313
  97.2 1.9 %collective-permute-done.4.came = bf16[256,1024]{1,0:T(8,128)(2,1)S(1)} collective-permute-done((bf16[256,1024]{1,0:T(8,128)(2,1)S(1)}, bf16[256,1024]{1,0:T(8,128)(2,1)S(1)}, u32[]{:S(2)}, u32[]{:S(2)}) %collective-permute-start.4) | collective-permute-done | bytes 524320 | tf_op jit(solution)/shard_map/ppermute | solution.py:373
  99.2 0.9 collective-permute-start.5
  100.1 1.4 %collective-permute-start.6 = (bf16[64,1024]{1,0:T(8,128)(2,1)S(1)}, bf16[64,1024]{1,0:T(8,128)(2,1)S(1)}, u32[]{:S(2)}, u32[]{:S(2)}) collective-permute-start(bf16[64,1024]{1,0:T(8,128)(2,1)S(1)} %get-tuple-element.15), channel_id=1, source_target_pairs={{0,32},{1,33},{2,34},{3,35},{4,36},{5,37},{6,38},{7,39},{8,40},{9,... | collective-permute-start | bytes 393224 | tf_op jit(solution)/shard_map/ppermute | solution.py:373
  101.4 1.3 %collective-permute-start.7 = (bf16[64,1024]{1,0:T(8,128)(2,1)S(1)}, bf16[64,1024]{1,0:T(8,128)(2,1)S(1)}, u32[]{:S(2)}, u32[]{:S(2)}) collective-permute-start(bf16[64,1024]{1,0:T(8,128)(2,1)S(1)} %get-tuple-element.16), channel_id=1, source_target_pairs={{0,48},{1,49},{2,50},{3,51},{4,52},{5,53},{6,54},{7,55},{8,56},{9,... | collective-permute-start | bytes 393224 | tf_op jit(solution)/shard_map/ppermute | solution.py:373
  102.7 2.0 %collective-permute-done.5.refs_1_ = bf16[64,1024]{1,0:T(8,128)(2,1)S(1)} collective-permute-done((bf16[64,1024]{1,0:T(8,128)(2,1)S(1)}, bf16[64,1024]{1,0:T(8,128)(2,1)S(1)}, u32[]{:S(2)}, u32[]{:S(2)}) %collective-permute-start.5) | collective-permute-done | bytes 131104 | tf_op jit(solution)/shard_map/ppermute | solution.py:373
  104.8 1.5 %collective-permute-done.6.refs_2_ = bf16[64,1024]{1,0:T(8,128)(2,1)S(1)} collective-permute-done((bf16[64,1024]{1,0:T(8,128)(2,1)S(1)}, bf16[64,1024]{1,0:T(8,128)(2,1)S(1)}, u32[]{:S(2)}, u32[]{:S(2)}) %collective-permute-start.6) | collective-permute-done | bytes 131104 | tf_op jit(solution)/shard_map/ppermute | solution.py:373
  106.3 2.5 %collective-permute-done.7.refs_3_ = bf16[64,1024]{1,0:T(8,128)(2,1)S(1)} collective-permute-done((bf16[64,1024]{1,0:T(8,128)(2,1)S(1)}, bf16[64,1024]{1,0:T(8,128)(2,1)S(1)}, u32[]{:S(2)}, u32[]{:S(2)}) %collective-permute-start.7) | collective-permute-done | bytes 131104 | tf_op jit(solution)/shard_map/ppermute | solution.py:373
  (42 shorter events, 5.9 us)
Async XLA Ops:
  0.0 42.1 %copy-start = (bf16[256,4096]{1,0:T(8,128)(2,1)S(1)}, bf16[256,4096]{1,0:T(8,128)(2,1)}, u32[]{:S(2)}) copy-start(bf16[256,4096]{1,0:T(8,128)(2,1)} %param.18) | copy-start | bytes 6291460
  0.0 1.2 %copy-start.3 = (f32[512,256]{1,0:T(8,128)S(1)}, f32[512,256]{1,0:T(8,128)}, u32[]{:S(2)}) copy-start(f32[512,256]{1,0:T(8,128)} %filt.1) | copy-start | bytes 1572868
  2.7 14.6 %all-to-all-start = ((bf16[16,16,640]{2,1,0:T(8,128)(2,1)}), bf16[16,16,640]{2,1,0:T(8,128)(2,1)S(1)}, u32[]{:S(2)}, u32[]{:S(2)}) async-start(bf16[16,16,640]{2,1,0:T(8,128)(2,1)} %pack.1), calls=%async_computation | async-start | bytes 655360 | tf_op jit(solution)/shard_map/all_to_all | solution.py:388
  8.8 8.5 %copy-start.12 = (f32[3,3,256]{2,1,0:T(4,128)S(1)}, f32[3,3,256]{2,1,0:T(4,128)}, u32[]{:S(2)}) copy-start(f32[3,3,256]{2,1,0:T(4,128)} %short.1) | copy-start | bytes 27652
  8.8 8.5 %copy-start.13 = (f32[256]{0:T(256)S(1)}, f32[256]{0:T(256)}, u32[]{:S(2)}) copy-start(f32[256]{0:T(256)} %param.17) | copy-start | bytes 3076
  8.8 8.5 %copy-start.14 = (bf16[2,256,256]{2,1,0:T(8,128)(2,1)S(1)}, bf16[2,256,256]{2,1,0:T(8,128)(2,1)}, u32[]{:S(2)}) copy-start(bf16[2,256,256]{2,1,0:T(8,128)(2,1)} %constant.43.clone.second) | copy-start | bytes 786436
  8.8 8.5 %copy-start.15 = (f32[2,72,128]{2,1,0:T(8,128)S(1)}, f32[2,72,128]{2,1,0:T(8,128)}, u32[]{:S(2)}) copy-start(f32[2,72,128]{2,1,0:T(8,128)} %constant.42.clone.twiddle) | copy-start | bytes 221188
  8.8 8.5 %copy-start.16 = (bf16[144,256]{1,0:T(8,128)(2,1)S(1)}, bf16[144,256]{1,0:T(8,128)(2,1)}, u32[]{:S(2)}) copy-start(bf16[144,256]{1,0:T(8,128)(2,1)} %constant.40.clone.first_signal) | copy-start | bytes 221188
  8.9 8.5 %copy-start.17 = (bf16[64,512]{1,0:T(8,128)(2,1)S(1)}, bf16[64,512]{1,0:T(8,128)(2,1)}, u32[]{:S(2)}) copy-start(bf16[64,512]{1,0:T(8,128)(2,1)} %constant.44.clone.last) | copy-start | bytes 196612
  8.9 8.5 %copy-start.18 = (bf16[144,128]{1,0:T(8,128)(2,1)S(1)}, bf16[144,128]{1,0:T(8,128)(2,1)}, u32[]{:S(2)}) copy-start(bf16[144,128]{1,0:T(8,128)(2,1)} %constant.41.clone.first_filter) | copy-start | bytes 110596
  17.4 0.9 copy-start.4
  30.9 60.7 %all-to-all-start.1 = ((bf16[64,16,512]{2,1,0:T(8,128)(2,1)}), bf16[64,16,512]{2,1,0:T(8,128)(2,1)S(1)}, u32[]{:S(2)}, u32[]{:S(2)}) async-start(bf16[64,16,512]{2,1,0:T(8,128)(2,1)} %bitcast.3), calls=%async_computation.1 | async-start | bytes 2097152 | tf_op jit(solution)/shard_map/all_to_all | solution.py:391
  42.1 21.2 %collective-permute-start = (bf16[128,1024]{1,0:T(8,128)(2,1)S(1)}, bf16[128,1024]{1,0:T(8,128)(2,1)S(1)}, u32[]{:S(2)}, u32[]{:S(2)}) collective-permute-start(bf16[128,1024]{1,0:T(8,128)(2,1)S(1)} %bitcast.12), channel_id=1, source_target_pairs={{0,1},{1,0},{2,3},{3,2},{4,5},{5,4},{6,7},{7,6},{8,9},{9,8},{10,11... | collective-permute-start | bytes 786440 | tf_op jit(solution)/shard_map/ppermute | solution.py:373
  63.4 25.8 %collective-permute-start.3 = (bf16[256,1024]{1,0:T(8,128)(2,1)S(1)}, bf16[256,1024]{1,0:T(8,128)(2,1)S(1)}, u32[]{:S(2)}, u32[]{:S(2)}) collective-permute-start(bf16[256,1024]{1,0:T(8,128)(2,1)S(1)} %pad_maximum_fusion.refs_0_), channel_id=1, source_target_pairs={{0,6},{1,7},{2,4},{3,5},{4,2},{5,3},{6,0},{7,1},{8,14},{9,15},{10,... | collective-permute-start | bytes 1572872 | tf_op jit(solution)/shard_map/ppermute | solution.py:373
  65.7 24.4 %collective-permute-start.2 = (bf16[256,1024]{1,0:T(8,128)(2,1)S(1)}, bf16[256,1024]{1,0:T(8,128)(2,1)S(1)}, u32[]{:S(2)}, u32[]{:S(2)}) collective-permute-start(bf16[256,1024]{1,0:T(8,128)(2,1)S(1)} %pad_maximum_fusion.refs_0_), channel_id=1, source_target_pairs={{0,4},{1,5},{2,6},{3,7},{4,0},{5,1},{6,2},{7,3},{8,12},{9,13},{10,... | collective-permute-start | bytes 1572872 | tf_op jit(solution)/shard_map/ppermute | solution.py:373
  66.7 24.1 %collective-permute-start.1 = (bf16[256,1024]{1,0:T(8,128)(2,1)S(1)}, bf16[256,1024]{1,0:T(8,128)(2,1)S(1)}, u32[]{:S(2)}, u32[]{:S(2)}) collective-permute-start(bf16[256,1024]{1,0:T(8,128)(2,1)S(1)} %pad_maximum_fusion.refs_0_), channel_id=1, source_target_pairs={{0,2},{1,3},{2,0},{3,1},{4,6},{5,7},{6,4},{7,5},{8,10},{9,11},{10,... | collective-permute-start | bytes 1572872 | tf_op jit(solution)/shard_map/ppermute | solution.py:373
  91.6 1.0 copy-start.2
  92.7 1.0 copy-start.7
  93.7 1.0 copy-start.9
  94.8 1.0 copy-start.11
  97.1 2.0 %collective-permute-start.4 = (bf16[256,1024]{1,0:T(8,128)(2,1)S(1)}, bf16[256,1024]{1,0:T(8,128)(2,1)S(1)}, u32[]{:S(2)}, u32[]{:S(2)}) collective-permute-start(bf16[256,1024]{1,0:T(8,128)(2,1)S(1)} %get-tuple-element.12), channel_id=1, source_target_pairs={{0,8},{1,9},{2,10},{3,11},{4,12},{5,13},{6,14},{7,15},{8,0},{9,1},... | collective-permute-start | bytes 1572872 | tf_op jit(solution)/shard_map/ppermute | solution.py:373
  99.2 5.6 %collective-permute-start.5 = (bf16[64,1024]{1,0:T(8,128)(2,1)S(1)}, bf16[64,1024]{1,0:T(8,128)(2,1)S(1)}, u32[]{:S(2)}, u32[]{:S(2)}) collective-permute-start(bf16[64,1024]{1,0:T(8,128)(2,1)S(1)} %get-tuple-element.14), channel_id=1, source_target_pairs={{0,16},{1,17},{2,18},{3,19},{4,20},{5,21},{6,22},{7,23},{8,24},{9,... | collective-permute-start | bytes 393224 | tf_op jit(solution)/shard_map/ppermute | solution.py:373
  100.1 6.2 %collective-permute-start.6 = (bf16[64,1024]{1,0:T(8,128)(2,1)S(1)}, bf16[64,1024]{1,0:T(8,128)(2,1)S(1)}, u32[]{:S(2)}, u32[]{:S(2)}) collective-permute-start(bf16[64,1024]{1,0:T(8,128)(2,1)S(1)} %get-tuple-element.15), channel_id=1, source_target_pairs={{0,32},{1,33},{2,34},{3,35},{4,36},{5,37},{6,38},{7,39},{8,40},{9,... | collective-permute-start | bytes 393224 | tf_op jit(solution)/shard_map/ppermute | solution.py:373
  101.4 7.4 %collective-permute-start.7 = (bf16[64,1024]{1,0:T(8,128)(2,1)S(1)}, bf16[64,1024]{1,0:T(8,128)(2,1)S(1)}, u32[]{:S(2)}, u32[]{:S(2)}) collective-permute-start(bf16[64,1024]{1,0:T(8,128)(2,1)S(1)} %get-tuple-element.16), channel_id=1, source_target_pairs={{0,48},{1,49},{2,50},{3,51},{4,52},{5,53},{6,54},{7,55},{8,56},{9,... | collective-permute-start | bytes 393224 | tf_op jit(solution)/shard_map/ppermute | solution.py:373
  (5 other events, 3.9 us)

commit v2 on v1

--- a/solution.py
+++ b/solution.py
@@ -67,6 +67,10 @@
     return lax.dot_general(left, right, dims, preferred_element_type=F32)
 
 
+def in_hbm(array):
+    return pltpu.with_memory_space_constraint(array, pltpu.HBM)
+
+
 def seq_index():
     return (lax.axis_index("y") * 2 + lax.axis_index("zl")) * 2 + lax.axis_index("core")
 
@@ -75,79 +79,116 @@
     return lax.rem(lax.axis_index("y"), 2) * 2 + lax.axis_index("zl")
 
 
-def pack_kernel(filt, tokens, payload):
-    payload[:, :, :512] = filt[...].T.astype(BF).reshape(16, CH, 512)
+def pack_kernel(filt_hbm, tokens_hbm, payload, filt, tokens, sems):
+    parts = 4
+    rows = 512 // parts
+    copies = [
+        pltpu.make_async_copy(filt_hbm.at[i * rows : (i + 1) * rows], filt.at[i * rows : (i + 1) * rows], sems.at[i])
+        for i in range(parts)
+    ]
+    copies.append(pltpu.make_async_copy(tokens_hbm, tokens, sems.at[parts]))
+    for copy in copies:
+        copy.start()
+    copies[parts].wait()
     high = jnp.right_shift(tokens[...], 4)
     low = jnp.bitwise_and(tokens[...], 15)
     gap = jnp.zeros((4, 128), F32)
     digits = jnp.concatenate([high.astype(F32), gap, low.astype(F32), gap], 0).astype(BF)
     payload[:, :, 512:] = jnp.broadcast_to(digits[None], (16, CH, 128))
+    for i in range(parts):
+        copies[i].wait()
+        at = slice(i * rows, (i + 1) * rows)
+        payload[:, :, at] = filt[at, :].T.astype(BF).reshape(16, CH, rows)
 
 
 def pack(long_filter, token_ids):
-    whole = pl.BlockSpec(memory_space=pltpu.VMEM)
+    hbm = pl.BlockSpec(memory_space=pltpu.HBM)
     return pl.pallas_call(
         pack_kernel,
         out_shape=jax.ShapeDtypeStruct((16, CH, 640), BF),
-        in_specs=[whole, whole],
-        out_specs=whole,
+        in_specs=[hbm, hbm],
+        out_specs=pl.BlockSpec(memory_space=pltpu.VMEM),
+        scratch_shapes=[
+            pltpu.VMEM((512, 256), F32),
+            pltpu.VMEM((4, 128), jnp.int32),
+            pltpu.SemaphoreType.DMA((5,)),
+        ],
         cost_estimate=pl.CostEstimate(flops=1 << 18, bytes_accessed=1 << 20, transcendentals=0),
         compiler_params=pltpu.CompilerParams(vmem_limit_bytes=6 << 20),
         name="pack",
-    )(long_filter, token_ids.reshape(4, 128))
-
-
-def vocab_kernel(embed, weight, table, acc):
-    step = pl.program_id(0)
-    wide = jnp.concatenate([weight[0], weight[1], weight[2]], 1)
-    part = mm(embed[...], wide)
-
-    @pl.when(step == 0)
-    def _():
-        acc[...] = part
-
-    @pl.when(step > 0)
-    def _():
-        acc[...] += part
-
-    @pl.when(step == pl.num_programs(0) - 1)
-    def _():
-        lane = lax.broadcasted_iota(jnp.int32, (CH, 128), 1)
-        row = lax.broadcasted_iota(jnp.int32, (CH, 128), 0)
-        pick = (lane == row + CH * lax.rem(seq_index(), 8)).astype(F32).astype(BF)
+    )(in_hbm(long_filter), in_hbm(token_ids.reshape(4, 128)))
+
+
+STEPS = 4
+GROUP = 8
+UNROLL = 16
+
+
+def vocab_kernel(embed_hbm, weight_hbm, table, embed, weight, sems):
+    depth = 4096 // STEPS
+    lanes = pl.ds(pl.multiple_of(lax.div(seq_index(), 8) * 128, 128), 128)
+    copies = []
+    for step in range(STEPS):
+        at = slice(step * depth, (step + 1) * depth)
+        pair = [pltpu.make_async_copy(embed_hbm.at[:, at], embed.at[:, at], sems.at[4 * step + 3])]
         for branch in range(3):
-            rows = acc[:, branch * 128 : (branch + 1) * 128].astype(BF)
-            table[branch * CH : (branch + 1) * CH, :] = mm(pick, rows, (((1,), (1,)), ((), ())))
+            pair.append(
+                pltpu.make_async_copy(
+                    weight_hbm.at[branch, at, lanes],
+                    weight.at[at, branch * 128 : (branch + 1) * 128],
+                    sems.at[4 * step + branch],
+                )
+            )
+        copies.append(pair)
+    for pair in copies:
+        for copy in pair:
+            copy.start()
+    total = None
+    for step, pair in enumerate(copies):
+        for copy in pair:
+            copy.wait()
+        at = slice(step * depth, (step + 1) * depth)
+        part = mm(embed[:, at], weight[at, :])
+        total = part if total is None else total + part
+    lane = lax.broadcasted_iota(jnp.int32, (CH, 128), 1)
+    row = lax.broadcasted_iota(jnp.int32, (CH, 128), 0)
+    pick = (lane == row + CH * lax.rem(seq_index(), 8)).astype(F32).astype(BF)
+    for branch in range(3):
+        rows = total[:, branch * 128 : (branch + 1) * 128].astype(BF)
+        table[branch * CH : (branch + 1) * CH, :] = mm(pick, rows, (((1,), (1,)), ((), ())))
 
 
 def vocab(embed_table, in_weight):
-    steps = 8
-    depth = in_weight.shape[0] // steps
+    hbm = pl.BlockSpec(memory_space=pltpu.HBM)
     return pl.pallas_call(
         vocab_kernel,
         out_shape=jax.ShapeDtypeStruct((3 * CH, 512), F32),
-        grid_spec=pltpu.PrefetchScalarGridSpec(
-            num_scalar_prefetch=0,
-            grid=(steps,),
-            in_specs=[
-                pl.BlockSpec((512, depth), lambda i: (0, i)),
-                pl.BlockSpec((3, depth, 128), lambda i: (0, i, lax.div(seq_index(), 8))),
-            ],
-            out_specs=pl.BlockSpec((3 * CH, 512), lambda i: (0, 0)),
-            scratch_shapes=[pltpu.VMEM((512, 384), F32)],
-        ),
-        compiler_params=pltpu.CompilerParams(
-            dimension_semantics=("arbitrary",), vmem_limit_bytes=61 << 20
-        ),
+        in_specs=[hbm, hbm],
+        out_specs=pl.BlockSpec(memory_space=pltpu.VMEM),
+        scratch_shapes=[
+            pltpu.VMEM((512, 4096), BF),
+            pltpu.VMEM((4096, 384), BF),
+            pltpu.SemaphoreType.DMA((4 * STEPS,)),
+        ],
+        compiler_params=pltpu.CompilerParams(vmem_limit_bytes=16 << 20),
         cost_estimate=pl.CostEstimate(flops=2 * 512 * 4096 * 384, bytes_accessed=8 << 20, transcendentals=0),
         name="vocab",
-    )(embed_table, in_weight.transpose(1, 0, 2))
+    )(in_hbm(embed_table), in_hbm(in_weight.transpose(1, 0, 2)))
 
 
 def convolve_kernel(
-    recv, table, short, direct, first_signal, first_filter, twiddle, second, last,
-    out, taps, token, gated, other, shaped, spec_high, spec_low, lags,
+    recv, table, *refs,
 ):
+    sources, (out, taps, token, gated, other, shaped, spec_high, spec_low, lags) = refs[:7], refs[7:16]
+    short, direct, first_signal, first_filter, twiddle, second, last = held = refs[16:23]
+    copies = [
+        pltpu.make_async_copy(source, target, refs[23].at[index])
+        for index, (source, target) in enumerate(zip(sources, held))
+    ]
+    for copy in copies:
+        copy.start()
+    copies[0].wait()
+    copies[1].wait()
     seq, core = seq_index(), lax.axis_index("core")
     lane = lax.broadcasted_iota(jnp.int32, (CH, 256), 1)
     row = lax.broadcasted_iota(jnp.int32, (CH, 256), 0)
@@ -164,36 +205,38 @@
             rows = slice(q * 256 + source * CH, q * 256 + (source + 1) * CH)
             lags[rows, :] = recv[source, :, q * 128 : (q + 1) * 128].astype(F32)
 
-    position = lax.broadcasted_iota(jnp.int32, (3 * CH, 128), 1)
-
-    def select(source, carried):
-        before_one, before_two = carried
-        for quarter in range(4):
-            ids = jnp.broadcast_to(token[pl.ds(source * 8 + quarter, 1), :], (3 * CH, 128))
-            place = jnp.bitwise_and(ids, 127)
-            bank = jnp.right_shift(ids, 7)
-            value = None
-            for index in range(4):
-                found = jnp.take_along_axis(
-                    table[:, index * 128 : (index + 1) * 128], place, axis=1, mode="promise_in_bounds"
-                )
-                value = found if index == 0 else jnp.where(bank == index, found, value)
-            one = pltpu.roll(value, 1, 1)
-            two = pltpu.roll(value, 2, 1)
-            lag_one = jnp.where(position < 1, before_one, one)
-            lag_two = jnp.where(position < 2, before_two, two)
-            before_one, before_two = one, two
-            filtered = taps[: 3 * CH, :] * value
-            filtered = filtered + taps[3 * CH : 6 * CH, :] * lag_one
-            filtered = filtered + taps[6 * CH : 9 * CH, :] * lag_two
-            rows = pl.ds(pl.multiple_of((source * 4 + quarter) * CH, CH), CH)
-            gated[rows, :] = filtered[:CH] * filtered[2 * CH :]
-            other[rows, :] = filtered[CH : 2 * CH]
-        return before_one, before_two
-
-    nothing = jnp.zeros((3 * CH, 128), F32)
-    lax.fori_loop(0, 16, select, (nothing, nothing))
-
+    banks = jnp.concatenate([table[:, i * 128 : (i + 1) * 128] for i in range(4)], 0).astype(BF)
+    line = lax.broadcasted_iota(jnp.int32, (256, 256), 0)
+    lane = lax.broadcasted_iota(jnp.int32, (256, 256), 1)
+    shift = (line == jnp.where(lane < 128, lane + 127, lane - 2)).astype(F32).astype(BF)
+    entry = lax.broadcasted_iota(jnp.int32, (128, 128), 0)
+
+    def select(source, before):
+        rows = [token[pl.ds(source * 8 + q, 1), :] for q in range(4)]
+        chosen = [(entry == jnp.bitwise_and(row, 127)).astype(F32).astype(BF) for row in rows]
+        found = mm(banks, jnp.concatenate(chosen, 1))
+        bank = jnp.right_shift(jnp.concatenate(rows, 1), 7)
+        value = found[: 3 * CH]
+        for i in range(1, 4):
+            value = jnp.where(bank == i, found[i * 3 * CH : (i + 1) * 3 * CH], value)
+        narrow = value.astype(BF)
+        blocks = [before] + [narrow[:, q * 128 : (q + 1) * 128] for q in range(4)]
+        pairs = [jnp.concatenate([blocks[q], blocks[q + 1]], 1) for q in range(4)]
+        lagged = mm(jnp.concatenate(pairs, 0), shift)
+        for q in range(4):
+            lag = lagged[q * 3 * CH : (q + 1) * 3 * CH]
+            filtered = taps[: 3 * CH, :] * value[:, q * 128 : (q + 1) * 128]
+            filtered = filtered + taps[3 * CH : 6 * CH, :] * lag[:, :128]
+            filtered = filtered + taps[6 * CH : 9 * CH, :] * lag[:, 128:]
+            at = pl.ds(pl.multiple_of((source * 4 + q) * CH, CH), CH)
+            gated[at, :] = filtered[:CH] * filtered[2 * CH :]
+            other[at, :] = filtered[CH : 2 * CH]
+        return blocks[4]
+
+    lax.fori_loop(0, 16, select, jnp.zeros((3 * CH, 128), BF), unroll=UNROLL)
+
+    for copy in copies[2:]:
+        copy.wait()
     cos_turn, sin_turn = twiddle[0], twiddle[1]
     rows_all = CH * HALF
 
@@ -226,8 +269,9 @@
         return mm(high, second[0], dims) + (mm(low, second[0], dims) + mm(high, second[1], dims))
 
     straight, flipped = (((1,), (0,)), ((), ())), (((1,), (1,)), ((), ()))
-    for pair in range(CH // 2):
-        at = slice(pair * 2 * HALF, (pair + 1) * 2 * HALF)
+    span = 2 * HALF
+    for start in range(0, CH // 2, GROUP):
+        at = slice(start * span, (start + GROUP) * span)
         left = transform(at, straight)
         right = transform(slice(rows_all + at.start, rows_all + at.stop), straight)
         left_real, left_imag, right_real, right_imag = left[:, :128], left[:, 128:], right[:, :128], right[:, 128:]
@@ -236,20 +280,20 @@
         )
         spec_high[at, :], spec_low[at, :] = halves(product)
 
-    for pair in range(CH // 2):
-        at = slice(pair * 2 * HALF, (pair + 1) * 2 * HALF)
-        back = transform(at, flipped)
-        columns = []
-        for i in range(2):
-            part = back[i * HALF : (i + 1) * HALF]
-            real, imag = part[:, :128], part[:, 128:]
-            columns.append(
-                jnp.concatenate([real * cos_turn + imag * sin_turn, imag * cos_turn - real * sin_turn], 0)
-            )
-        high, low = halves(jnp.concatenate(columns, 1))
-        result = mm(last[...], jnp.concatenate([high, low, high, high[:80]], 0))
-        for i in range(2):
-            shaped[pl.ds(2 * pair + i, 64, stride=CH), :] = result[:, i * 128 : (i + 1) * 128]
+    for start in range(0, CH // 2, GROUP):
+        backs = transform(slice(start * span, (start + GROUP) * span), flipped)
+        for pair in range(start, start + GROUP):
+            columns = []
+            for i in range(2):
+                top = ((pair - start) * 2 + i) * HALF
+                real, imag = backs[top : top + HALF, :128], backs[top : top + HALF, 128:]
+                columns.append(
+                    jnp.concatenate([real * cos_turn + imag * sin_turn, imag * cos_turn - real * sin_turn], 0)
+                )
+            high, low = halves(jnp.concatenate(columns, 1))
+            result = mm(last[...], jnp.concatenate([high, low, high, high[:80]], 0))
+            for i in range(2):
+                shaped[pl.ds(2 * pair + i, 64, stride=CH), :] = result[:, i * 128 : (i + 1) * 128]
 
     skip = taps[9 * CH :, :]
     low_half = lax.broadcasted_iota(jnp.int32, (CH, 128), 1) < 64
@@ -271,12 +315,13 @@
 
 def convolve(recv, table, short_filter, skip_gain):
     consts = [jnp.asarray(c) for c in tables()]
-    whole = pl.BlockSpec(memory_space=pltpu.VMEM)
+    whole, hbm = pl.BlockSpec(memory_space=pltpu.VMEM), pl.BlockSpec(memory_space=pltpu.HBM)
     positions = 8192
+    fetched = [short_filter, skip_gain[None, :], *consts]
     return pl.pallas_call(
         convolve_kernel,
         out_shape=jax.ShapeDtypeStruct((2, 2, 2, 8, CH, 512), BF),
-        in_specs=[whole] * 9,
+        in_specs=[whole] * 2 + [hbm] * 7,
         out_specs=whole,
         scratch_shapes=[
             pltpu.VMEM((10 * CH, 128), F32),
@@ -287,11 +332,13 @@
             pltpu.VMEM((2 * CH * HALF, 256), BF),
             pltpu.VMEM((2 * CH * HALF, 256), BF),
             pltpu.VMEM((64 * CH, 128), F32),
+            *[pltpu.VMEM(array.shape, array.dtype) for array in fetched],
+            pltpu.SemaphoreType.DMA((len(fetched),)),
         ],
         cost_estimate=pl.CostEstimate(flops=4 << 30, bytes_accessed=4 << 20, transcendentals=0),
         compiler_params=pltpu.CompilerParams(vmem_limit_bytes=20 << 20),
         name="convolve",
-    )(recv, table, short_filter, skip_gain[None, :], *consts)
+    )(recv, table, *[in_hbm(array) for array in fetched])
 
 
 def project_kernel(recv, *refs):

time: 110 us -> 102 us (0.927)
  Pallas kernels: 24.1 us -> 17.6 us
  waiting for transfers between devices: 46.8 us -> 50.4 us
  local copies, waits for them, and re-layouts: 10.2 us -> 7.38 us
  starting transfers between devices: 28.2 us -> 26.1 us
    pallas_call x1, Pallas kernels: 12.6 us -> 8.3 us  [convolve(): pl.pallas_call(convolve_kernel, out_shape=jax.ShapeDtypeStruct((2, 2, 2,...]
    pallas_call x1, Pallas kernels: 8.42 us -> 4.81 us  [vocab(): pl.pallas_call(vocab_kernel, out_shape=jax.ShapeDtypeStruct((3 * CH, 512)...]
    all_to_all x1, waiting for transfers between devices: 0.01 us -> 3.47 us  [body(): recv = lax.all_to_all(payload, SEQ, 0, 0, tiled=True)]
    unnamed x38 -> x18, local copies, waits for them, and re-layouts: 10.2 us -> 7.35 us
    all_to_all x1, starting transfers between devices: 11.2 us -> 9.11 us  [body(): lax.all_to_all(chunks.reshape(64, CH, 512), ('y', 'zl', 'x', 'zh'), 0, 0,...]
    pallas_call x1, Pallas kernels: 0.86 us -> 2.28 us  [pack(): pl.pallas_call(pack_kernel, out_shape=jax.ShapeDtypeStruct((16, CH, 640),...]
  transfers between devices with their start and end apart: 10 -> 10, of which waited for: 6 -> 7; matrix products, arithmetic and copies ran while one was open for 0% -> 0% of each run, Pallas kernels for 8% -> 5%
where the time goes in v2:
time: 102 us
  waiting for transfers between devices  50.4 us (49%)
  starting transfers between devices  26.1 us (26%)
  Pallas kernels  17.6 us (17%)
  local copies, waits for them, and re-layouts  7.38 us (7%)
    ppermute x8, waiting for transfers between devices, permuted(): return lax.ppermute(block, AXES, pairs)  46.9 us
    ppermute x8, starting transfers between devices, permuted(): return lax.ppermute(block, AXES, pairs)  11 us
    all_to_all x1, starting transfers between devices, body(): lax.all_to_all(chunks.reshape(64, CH, 512), ('y', 'zl', 'x', 'zh'), 0, 0,...  9.11 us
    pallas_call x1, Pallas kernels, convolve(): pl.pallas_call(convolve_kernel, out_shape=jax.ShapeDtypeStruct((2, 2, 2,...  8.3 us
    unnamed x18, local copies, waits for them, and re-layouts  7.35 us
    all_to_all x1, starting transfers between devices, body(): recv = lax.all_to_all(payload, SEQ, 0, 0, tiled=True)  6.05 us
    pallas_call x1, Pallas kernels, vocab(): pl.pallas_call(vocab_kernel, out_shape=jax.ShapeDtypeStruct((3 * CH, 512)...  4.81 us
    all_to_all x1, waiting for transfers between devices, body(): recv = lax.all_to_all(payload, SEQ, 0, 0, tiled=True)  3.47 us
  transfers between devices with their start and end apart: 10, of which 7 were waited for; matrix products, arithmetic and copies ran while one was open for 0% of the time, Pallas kernels for 5%

profile of v2, /device:TPU:0, one launch (start us, length us, event | category | flops | bytes accessed | tf_op | source)
XLA Modules:
  0.0 101.6 jit_solution(11119742487394684087)
XLA Ops:
  0.0 2.3 %pack.1 = bf16[16,16,640]{2,1,0:T(8,128)(2,1)} custom-call(f32[512,256]{1,0:T(8,128)} %filt_hbm.1, s32[4,128]{1,0:T(4,128)} %bitcast.12), custom_call_target="tpu_custom_call" | custom-call | flops 262144 | bytes 1048576 | tf_op jit(solution)/shard_map/pack/pallas_call | solution.py:106
  2.3 6.1 %all-to-all-start = ((bf16[16,16,640]{2,1,0:T(8,128)(2,1)}), bf16[16,16,640]{2,1,0:T(8,128)(2,1)S(1)}, u32[]{:S(2)}, u32[]{:S(2)}) async-start(bf16[16,16,640]{2,1,0:T(8,128)(2,1)} %pack.1), calls=%async_computation | async-start | bytes 655360 | tf_op jit(solution)/shard_map/all_to_all | solution.py:435
  8.4 4.8 %vocab.1.table = f32[48,512]{1,0:T(8,128)S(1)} custom-call(bf16[512,4096]{1,0:T(8,128)(2,1)} %embed_hbm.1, bf16[3,4096,256]{2,1,0:T(8,128)(2,1)} %bitcast.9), custom_call_target="tpu_custom_call" | custom-call | flops 1610612736 | bytes 8388608 | tf_op jit(solution)/shard_map/vocab/pallas_call | solution.py:163
  13.2 3.5 %all-to-all-done.recv = bf16[16,16,640]{2,1,0:T(8,128)(2,1)S(1)} async-done(((bf16[16,16,640]{2,1,0:T(8,128)(2,1)}), bf16[16,16,640]{2,1,0:T(8,128)(2,1)S(1)}, u32[]{:S(2)}, u32[]{:S(2)}) %all-to-all-start) | async-done | bytes 327712 | tf_op jit(solution)/shard_map/all_to_all | solution.py:435
  16.6 8.3 %convolve.1 = bf16[2,2,2,8,16,512]{5,4,3,2,1,0:T(8,128)(2,1)} custom-call(bf16[16,16,640]{2,1,0:T(8,128)(2,1)S(1)} %all-to-all-done.recv, f32[48,512]{1,0:T(8,128)S(1)} %vocab.1.table, f32[3,3,256]{2,1,0:T(4,128)} %refs_0_.1, f32[1,256]{1,0:T(1,128)} %bitcast.13, bf16[144,256]{1,0:T(8,128)(2,1)} %constant.40.clone.refs_2_, ...), custom_call_target="tpu_custom_call" | custom-call | flops 4294967296 | bytes 4194304 | tf_op jit(solution)/shard_map/convolve/pallas_call | solution.py:321
  24.9 9.1 %all-to-all-start.1 = ((bf16[64,16,512]{2,1,0:T(8,128)(2,1)}), bf16[64,16,512]{2,1,0:T(8,128)(2,1)S(1)}, u32[]{:S(2)}, u32[]{:S(2)}) async-start(bf16[64,16,512]{2,1,0:T(8,128)(2,1)} %bitcast.3), calls=%async_computation.1 | async-start | bytes 2097152 | tf_op jit(solution)/shard_map/all_to_all | solution.py:438
  34.1 3.2 %collective-permute-start = (bf16[128,1024]{1,0:T(8,128)(2,1)S(1)}, bf16[128,1024]{1,0:T(8,128)(2,1)S(1)}, u32[]{:S(2)}, u32[]{:S(2)}) collective-permute-start(bf16[128,1024]{1,0:T(8,128)(2,1)S(1)} %bitcast.10), channel_id=1, source_target_pairs={{0,1},{1,0},{2,3},{3,2},{4,5},{5,4},{6,7},{7,6},{8,9},{9,8},{10,11... | collective-permute-start | bytes 786440 | tf_op jit(solution)/shard_map/ppermute | solution.py:420
  37.3 18.1 %collective-permute-done = bf16[128,1024]{1,0:T(8,128)(2,1)S(1)} collective-permute-done((bf16[128,1024]{1,0:T(8,128)(2,1)S(1)}, bf16[128,1024]{1,0:T(8,128)(2,1)S(1)}, u32[]{:S(2)}, u32[]{:S(2)}) %collective-permute-start) | collective-permute-done | bytes 262176 | tf_op jit(solution)/shard_map/ppermute | solution.py:420
  55.4 2.2 %collective-permute-start.3 = (bf16[256,1024]{1,0:T(8,128)(2,1)S(1)}, bf16[256,1024]{1,0:T(8,128)(2,1)S(1)}, u32[]{:S(2)}, u32[]{:S(2)}) collective-permute-start(bf16[256,1024]{1,0:T(8,128)(2,1)S(1)} %pad_maximum_fusion.refs_0_), channel_id=1, source_target_pairs={{0,6},{1,7},{2,4},{3,5},{4,2},{5,3},{6,0},{7,1},{8,14},{9,15},{10,... | collective-permute-start | bytes 1572872 | tf_op jit(solution)/shard_map/ppermute | solution.py:420
  57.6 1.1 %collective-permute-start.2 = (bf16[256,1024]{1,0:T(8,128)(2,1)S(1)}, bf16[256,1024]{1,0:T(8,128)(2,1)S(1)}, u32[]{:S(2)}, u32[]{:S(2)}) collective-permute-start(bf16[256,1024]{1,0:T(8,128)(2,1)S(1)} %pad_maximum_fusion.refs_0_), channel_id=1, source_target_pairs={{0,4},{1,5},{2,6},{3,7},{4,0},{5,1},{6,2},{7,3},{8,12},{9,13},{10,... | collective-permute-start | bytes 1572872 | tf_op jit(solution)/shard_map/ppermute | solution.py:420
  60.4 20.8 %collective-permute-done.3.refs_3_ = bf16[256,1024]{1,0:T(8,128)(2,1)S(1)} collective-permute-done((bf16[256,1024]{1,0:T(8,128)(2,1)S(1)}, bf16[256,1024]{1,0:T(8,128)(2,1)S(1)}, u32[]{:S(2)}, u32[]{:S(2)}) %collective-permute-start.3) | collective-permute-done | bytes 524320 | tf_op jit(solution)/shard_map/ppermute | solution.py:420
  83.6 1.0 %copy-done.2 = bf16[256,1024]{1,0:T(8,128)(2,1)S(1)} copy-done((bf16[256,1024]{1,0:T(8,128)(2,1)S(1)}, bf16[256,1024]{1,0:T(8,128)(2,1)}, u32[]{:S(2)}) %copy-start.2) | copy-done | bytes 524312
  84.7 1.0 %copy-done.4 = bf16[256,1024]{1,0:T(8,128)(2,1)S(1)} copy-done((bf16[256,1024]{1,0:T(8,128)(2,1)S(1)}, bf16[256,1024]{1,0:T(8,128)(2,1)}, u32[]{:S(2)}) %copy-start.4) | copy-done | bytes 524312
  85.7 1.0 %copy-done.6 = bf16[256,1024]{1,0:T(8,128)(2,1)S(1)} copy-done((bf16[256,1024]{1,0:T(8,128)(2,1)S(1)}, bf16[256,1024]{1,0:T(8,128)(2,1)}, u32[]{:S(2)}) %copy-start.6) | copy-done | bytes 524312
  86.8 1.0 %copy-done.8 = bf16[256,1024]{1,0:T(8,128)(2,1)S(1)} copy-done((bf16[256,1024]{1,0:T(8,128)(2,1)S(1)}, bf16[256,1024]{1,0:T(8,128)(2,1)}, u32[]{:S(2)}) %copy-start.8) | copy-done | bytes 524312
  87.8 1.3 %project.1 = (f32[256,1024]{1,0:T(8,128)S(1)}, bf16[256,1024]{1,0:T(8,128)(2,1)S(1)}) custom-call(bf16[8,8,16,512]{3,2,1,0:T(8,128)(2,1)S(1)} %bitcast.8, bf16[256,1024]{1,0:T(8,128)(2,1)S(1)} %copy-done.2, bf16[256,1024]{1,0:T(8,128)(2,1)S(1)} %copy-done.8, bf16[256,1024]{1,0:T(8,128)(2,1)S(1)} %copy-done.6, bf16[256,1024]{1,0:T(8,128)(2,1)S(1)} %copy-done.4), custom_call_target="tpu_custom_call" | custom-call | flops 1073741824 | bytes 5242880 | tf_op jit(solution)/shard_map/project/pallas_call | solution.py:360
  89.2 1.9 %collective-permute-done.4.came = bf16[256,1024]{1,0:T(8,128)(2,1)S(1)} collective-permute-done((bf16[256,1024]{1,0:T(8,128)(2,1)S(1)}, bf16[256,1024]{1,0:T(8,128)(2,1)S(1)}, u32[]{:S(2)}, u32[]{:S(2)}) %collective-permute-start.4) | collective-permute-done | bytes 524320 | tf_op jit(solution)/shard_map/ppermute | solution.py:420
  91.2 0.9 collective-permute-start.5
  92.0 1.3 %collective-permute-start.6 = (bf16[64,1024]{1,0:T(8,128)(2,1)S(1)}, bf16[64,1024]{1,0:T(8,128)(2,1)S(1)}, u32[]{:S(2)}, u32[]{:S(2)}) collective-permute-start(bf16[64,1024]{1,0:T(8,128)(2,1)S(1)} %get-tuple-element.15), channel_id=1, source_target_pairs={{0,32},{1,33},{2,34},{3,35},{4,36},{5,37},{6,38},{7,39},{8,40},{9,... | collective-permute-start | bytes 393224 | tf_op jit(solution)/shard_map/ppermute | solution.py:420
  93.3 1.4 %collective-permute-start.7 = (bf16[64,1024]{1,0:T(8,128)(2,1)S(1)}, bf16[64,1024]{1,0:T(8,128)(2,1)S(1)}, u32[]{:S(2)}, u32[]{:S(2)}) collective-permute-start(bf16[64,1024]{1,0:T(8,128)(2,1)S(1)} %get-tuple-element.16), channel_id=1, source_target_pairs={{0,48},{1,49},{2,50},{3,51},{4,52},{5,53},{6,54},{7,55},{8,56},{9,... | collective-permute-start | bytes 393224 | tf_op jit(solution)/shard_map/ppermute | solution.py:420
  94.7 2.0 %collective-permute-done.5.refs_1_ = bf16[64,1024]{1,0:T(8,128)(2,1)S(1)} collective-permute-done((bf16[64,1024]{1,0:T(8,128)(2,1)S(1)}, bf16[64,1024]{1,0:T(8,128)(2,1)S(1)}, u32[]{:S(2)}, u32[]{:S(2)}) %collective-permute-start.5) | collective-permute-done | bytes 131104 | tf_op jit(solution)/shard_map/ppermute | solution.py:420
  96.8 1.4 %collective-permute-done.6.refs_2_ = bf16[64,1024]{1,0:T(8,128)(2,1)S(1)} collective-permute-done((bf16[64,1024]{1,0:T(8,128)(2,1)S(1)}, bf16[64,1024]{1,0:T(8,128)(2,1)S(1)}, u32[]{:S(2)}, u32[]{:S(2)}) %collective-permute-start.6) | collective-permute-done | bytes 131104 | tf_op jit(solution)/shard_map/ppermute | solution.py:420
  98.2 2.6 %collective-permute-done.7.refs_3_ = bf16[64,1024]{1,0:T(8,128)(2,1)S(1)} collective-permute-done((bf16[64,1024]{1,0:T(8,128)(2,1)S(1)}, bf16[64,1024]{1,0:T(8,128)(2,1)S(1)}, u32[]{:S(2)}, u32[]{:S(2)}) %collective-permute-start.7) | collective-permute-done | bytes 131104 | tf_op jit(solution)/shard_map/ppermute | solution.py:420
  100.8 0.8 assemble.1
  (22 shorter events, 4.3 us)
Async XLA Ops:
  0.0 34.1 %copy-start = (bf16[256,4096]{1,0:T(8,128)(2,1)S(1)}, bf16[256,4096]{1,0:T(8,128)(2,1)}, u32[]{:S(2)}) copy-start(bf16[256,4096]{1,0:T(8,128)(2,1)} %param.18) | copy-start | bytes 6291460
  2.3 14.3 %all-to-all-start = ((bf16[16,16,640]{2,1,0:T(8,128)(2,1)}), bf16[16,16,640]{2,1,0:T(8,128)(2,1)S(1)}, u32[]{:S(2)}, u32[]{:S(2)}) async-start(bf16[16,16,640]{2,1,0:T(8,128)(2,1)} %pack.1), calls=%async_computation | async-start | bytes 655360 | tf_op jit(solution)/shard_map/all_to_all | solution.py:435
  24.9 58.7 %all-to-all-start.1 = ((bf16[64,16,512]{2,1,0:T(8,128)(2,1)}), bf16[64,16,512]{2,1,0:T(8,128)(2,1)S(1)}, u32[]{:S(2)}, u32[]{:S(2)}) async-start(bf16[64,16,512]{2,1,0:T(8,128)(2,1)} %bitcast.3), calls=%async_computation.1 | async-start | bytes 2097152 | tf_op jit(solution)/shard_map/all_to_all | solution.py:438
  34.1 21.3 %collective-permute-start = (bf16[128,1024]{1,0:T(8,128)(2,1)S(1)}, bf16[128,1024]{1,0:T(8,128)(2,1)S(1)}, u32[]{:S(2)}, u32[]{:S(2)}) collective-permute-start(bf16[128,1024]{1,0:T(8,128)(2,1)S(1)} %bitcast.10), channel_id=1, source_target_pairs={{0,1},{1,0},{2,3},{3,2},{4,5},{5,4},{6,7},{7,6},{8,9},{9,8},{10,11... | collective-permute-start | bytes 786440 | tf_op jit(solution)/shard_map/ppermute | solution.py:420
  55.4 25.8 %collective-permute-start.3 = (bf16[256,1024]{1,0:T(8,128)(2,1)S(1)}, bf16[256,1024]{1,0:T(8,128)(2,1)S(1)}, u32[]{:S(2)}, u32[]{:S(2)}) collective-permute-start(bf16[256,1024]{1,0:T(8,128)(2,1)S(1)} %pad_maximum_fusion.refs_0_), channel_id=1, source_target_pairs={{0,6},{1,7},{2,4},{3,5},{4,2},{5,3},{6,0},{7,1},{8,14},{9,15},{10,... | collective-permute-start | bytes 1572872 | tf_op jit(solution)/shard_map/ppermute | solution.py:420
  57.6 24.4 %collective-permute-start.2 = (bf16[256,1024]{1,0:T(8,128)(2,1)S(1)}, bf16[256,1024]{1,0:T(8,128)(2,1)S(1)}, u32[]{:S(2)}, u32[]{:S(2)}) collective-permute-start(bf16[256,1024]{1,0:T(8,128)(2,1)S(1)} %pad_maximum_fusion.refs_0_), channel_id=1, source_target_pairs={{0,4},{1,5},{2,6},{3,7},{4,0},{5,1},{6,2},{7,3},{8,12},{9,13},{10,... | collective-permute-start | bytes 1572872 | tf_op jit(solution)/shard_map/ppermute | solution.py:420
  58.8 24.1 %collective-permute-start.1 = (bf16[256,1024]{1,0:T(8,128)(2,1)S(1)}, bf16[256,1024]{1,0:T(8,128)(2,1)S(1)}, u32[]{:S(2)}, u32[]{:S(2)}) collective-permute-start(bf16[256,1024]{1,0:T(8,128)(2,1)S(1)} %pad_maximum_fusion.refs_0_), channel_id=1, source_target_pairs={{0,2},{1,3},{2,0},{3,1},{4,6},{5,7},{6,4},{7,5},{8,10},{9,11},{10,... | collective-permute-start | bytes 1572872 | tf_op jit(solution)/shard_map/ppermute | solution.py:420
  59.6 0.8 copy-start.1
  81.2 0.8 copy-start.3
  82.0 0.8 copy-start.5
  82.8 0.8 copy-start.7
  83.6 1.0 %copy-start.2 = (bf16[256,1024]{1,0:T(8,128)(2,1)S(1)}, bf16[256,1024]{1,0:T(8,128)(2,1)}, u32[]{:S(2)}) copy-start(bf16[256,1024]{1,0:T(8,128)(2,1)} %copy-done.1) | copy-start | bytes 1572868
  84.7 1.0 %copy-start.4 = (bf16[256,1024]{1,0:T(8,128)(2,1)S(1)}, bf16[256,1024]{1,0:T(8,128)(2,1)}, u32[]{:S(2)}) copy-start(bf16[256,1024]{1,0:T(8,128)(2,1)} %copy-done.3) | copy-start | bytes 1572868
  85.7 1.0 %copy-start.6 = (bf16[256,1024]{1,0:T(8,128)(2,1)S(1)}, bf16[256,1024]{1,0:T(8,128)(2,1)}, u32[]{:S(2)}) copy-start(bf16[256,1024]{1,0:T(8,128)(2,1)} %copy-done.5) | copy-start | bytes 1572868
  86.8 1.0 %copy-start.8 = (bf16[256,1024]{1,0:T(8,128)(2,1)S(1)}, bf16[256,1024]{1,0:T(8,128)(2,1)}, u32[]{:S(2)}) copy-start(bf16[256,1024]{1,0:T(8,128)(2,1)} %copy-done.7) | copy-start | bytes 1572868
  89.1 2.0 %collective-permute-start.4 = (bf16[256,1024]{1,0:T(8,128)(2,1)S(1)}, bf16[256,1024]{1,0:T(8,128)(2,1)S(1)}, u32[]{:S(2)}, u32[]{:S(2)}) collective-permute-start(bf16[256,1024]{1,0:T(8,128)(2,1)S(1)} %get-tuple-element.12), channel_id=1, source_target_pairs={{0,8},{1,9},{2,10},{3,11},{4,12},{5,13},{6,14},{7,15},{8,0},{9,1},... | collective-permute-start | bytes 1572872 | tf_op jit(solution)/shard_map/ppermute | solution.py:420
  91.2 5.6 %collective-permute-start.5 = (bf16[64,1024]{1,0:T(8,128)(2,1)S(1)}, bf16[64,1024]{1,0:T(8,128)(2,1)S(1)}, u32[]{:S(2)}, u32[]{:S(2)}) collective-permute-start(bf16[64,1024]{1,0:T(8,128)(2,1)S(1)} %get-tuple-element.14), channel_id=1, source_target_pairs={{0,16},{1,17},{2,18},{3,19},{4,20},{5,21},{6,22},{7,23},{8,24},{9,... | collective-permute-start | bytes 393224 | tf_op jit(solution)/shard_map/ppermute | solution.py:420
  92.0 6.1 %collective-permute-start.6 = (bf16[64,1024]{1,0:T(8,128)(2,1)S(1)}, bf16[64,1024]{1,0:T(8,128)(2,1)S(1)}, u32[]{:S(2)}, u32[]{:S(2)}) collective-permute-start(bf16[64,1024]{1,0:T(8,128)(2,1)S(1)} %get-tuple-element.15), channel_id=1, source_target_pairs={{0,32},{1,33},{2,34},{3,35},{4,36},{5,37},{6,38},{7,39},{8,40},{9,... | collective-permute-start | bytes 393224 | tf_op jit(solution)/shard_map/ppermute | solution.py:420
  93.3 7.5 %collective-permute-start.7 = (bf16[64,1024]{1,0:T(8,128)(2,1)S(1)}, bf16[64,1024]{1,0:T(8,128)(2,1)S(1)}, u32[]{:S(2)}, u32[]{:S(2)}) collective-permute-start(bf16[64,1024]{1,0:T(8,128)(2,1)S(1)} %get-tuple-element.16), channel_id=1, source_target_pairs={{0,48},{1,49},{2,50},{3,51},{4,52},{5,53},{6,54},{7,55},{8,56},{9,... | collective-permute-start | bytes 393224 | tf_op jit(solution)/shard_map/ppermute | solution.py:420

commit v3 on v2

--- a/solution.py
+++ b/solution.py
@@ -79,14 +79,20 @@
     return lax.rem(lax.axis_index("y"), 2) * 2 + lax.axis_index("zl")
 
 
-def pack_kernel(filt_hbm, tokens_hbm, payload, filt, tokens, sems):
+def pack_kernel(filt_hbm, tokens_hbm, weight_hbm, payload, held, filt, tokens, sems):
     parts = 4
+    mine = weight_hbm.at[
+        :,
+        pl.ds(pl.multiple_of(lax.axis_index("core") * CH, CH), CH),
+        pl.ds(pl.multiple_of(column_index() * 1024, 1024), 1024),
+    ]
     rows = 512 // parts
     copies = [
         pltpu.make_async_copy(filt_hbm.at[i * rows : (i + 1) * rows], filt.at[i * rows : (i + 1) * rows], sems.at[i])
         for i in range(parts)
     ]
     copies.append(pltpu.make_async_copy(tokens_hbm, tokens, sems.at[parts]))
+    copies.append(pltpu.make_async_copy(mine, held, sems.at[parts + 1]))
     for copy in copies:
         copy.start()
     copies[parts].wait()
@@ -99,24 +105,28 @@
         copies[i].wait()
         at = slice(i * rows, (i + 1) * rows)
         payload[:, :, at] = filt[at, :].T.astype(BF).reshape(16, CH, rows)
-
-
-def pack(long_filter, token_ids):
-    hbm = pl.BlockSpec(memory_space=pltpu.HBM)
+    copies[parts + 1].wait()
+
+
+def pack(long_filter, token_ids, out_weight):
+    hbm, whole = pl.BlockSpec(memory_space=pltpu.HBM), pl.BlockSpec(memory_space=pltpu.VMEM)
     return pl.pallas_call(
         pack_kernel,
-        out_shape=jax.ShapeDtypeStruct((16, CH, 640), BF),
-        in_specs=[hbm, hbm],
-        out_specs=pl.BlockSpec(memory_space=pltpu.VMEM),
+        out_shape=(
+            jax.ShapeDtypeStruct((16, CH, 640), BF),
+            jax.ShapeDtypeStruct((8, CH, 1024), BF),
+        ),
+        in_specs=[hbm] * 3,
+        out_specs=(whole, whole),
         scratch_shapes=[
             pltpu.VMEM((512, 256), F32),
             pltpu.VMEM((4, 128), jnp.int32),
-            pltpu.SemaphoreType.DMA((5,)),
+            pltpu.SemaphoreType.DMA((6,)),
         ],
         cost_estimate=pl.CostEstimate(flops=1 << 18, bytes_accessed=1 << 20, transcendentals=0),
         compiler_params=pltpu.CompilerParams(vmem_limit_bytes=6 << 20),
         name="pack",
-    )(in_hbm(long_filter), in_hbm(token_ids.reshape(4, 128)))
+    )(in_hbm(long_filter), in_hbm(token_ids.reshape(4, 128)), in_hbm(out_weight.reshape(8, 2 * CH, 4096)))
 
 
 STEPS = 4
@@ -421,17 +431,13 @@
 
 
 def body(token_ids, embed_table, in_weight, short_filter, long_filter, skip_gain, out_weight):
-    held = lax.dynamic_slice(
-        out_weight.reshape(8, 2 * CH, 4096),
-        (0, lax.axis_index("core") * CH, column_index() * 1024),
-        (8, CH, 1024),
-    ).reshape(128, 1024)
+    payload, held = pack(long_filter, token_ids, out_weight)
+    held = held.reshape(128, 1024)
     across = permuted(held, lambda d: {"zh": d["zh"] ^ 1})
     both = jnp.concatenate([held, across], 0)
     weights = [both]
     for index in range(1, 4):
         weights.append(permuted(both, lambda d: {"x": d["x"] ^ index}))
-    payload = pack(long_filter, token_ids)
     recv = lax.all_to_all(payload, SEQ, 0, 0, tiled=True)
     table = vocab(embed_table, in_weight)
     chunks = convolve(recv, table, short_filter, skip_gain)
@@ -440,9 +446,7 @@
     came = permuted(send, lambda d: {"core": 1 - d["core"]})
     pieces = list(combine(keep, came))
     for index in range(1, 4):
-        pieces[index] = permuted(
-            pieces[index], lambda d: {"y": d["y"] ^ (index // 2), "zl": d["zl"] ^ (index % 2)}
-        )
+        pieces[index] = permuted(pieces[index], lambda d: {"y": d["y"] ^ (index // 2), "zl": d["zl"] ^ (index % 2)})
     return assemble(pieces)
 
 

time: 102 us -> 95.7 us (0.938)
  local copies, waits for them, and re-layouts: 7.38 us -> 0 us
  waiting for transfers between devices: 50.4 us -> 51.7 us
    unnamed x18 -> x0, local copies, waits for them, and re-layouts: 7.35 us -> none
    ppermute x8, waiting for transfers between devices: 46.9 us -> 48.2 us  [permuted(): return lax.ppermute(block, AXES, pairs)]
  transfers between devices with their start and end apart: 10 -> 10, of which waited for: 7 -> 8; matrix products, arithmetic and copies ran while one was open for 0% -> 0% of each run, Pallas kernels for 5% -> 5%
where the time goes in v3:
time: 95.7 us; the launch traced here: 95.4 us
  waiting for transfers between devices  51.7 us (54%)
  starting transfers between devices  26.1 us (27%)
  Pallas kernels  17.4 us (18%)
    ppermute x8, waiting for transfers between devices, permuted(): return lax.ppermute(block, AXES, pairs)  48.2 us
    ppermute x8, starting transfers between devices, permuted(): return lax.ppermute(block, AXES, pairs)  11 us
    all_to_all x1, starting transfers between devices, body(): lax.all_to_all(chunks.reshape(64, CH, 512), ('y', 'zl', 'x', 'zh'), 0, 0,...  9.11 us
    pallas_call x1, Pallas kernels, convolve(): pl.pallas_call(convolve_kernel, out_shape=jax.ShapeDtypeStruct((2, 2, 2,...  8.28 us
    all_to_all x1, starting transfers between devices, body(): recv = lax.all_to_all(payload, SEQ, 0, 0, tiled=True)  6.05 us
    pallas_call x1, Pallas kernels, vocab(): pl.pallas_call(vocab_kernel, out_shape=jax.ShapeDtypeStruct((3 * CH, 512)...  4.8 us
    all_to_all x1, waiting for transfers between devices, body(): recv = lax.all_to_all(payload, SEQ, 0, 0, tiled=True)  3.48 us
    pallas_call x1, Pallas kernels, pack(): pl.pallas_call(pack_kernel, out_shape=(jax.ShapeDtypeStruct((16, CH, 640)...  2.14 us
  transfers between devices with their start and end apart: 10, of which 8 were waited for; matrix products, arithmetic and copies ran while one was open for 0% of the time, Pallas kernels for 5%

profile of v3, /device:TPU:0, one launch (start us, length us, event | category | flops | bytes accessed | tf_op | source)
XLA Modules:
  0.0 95.4 jit_solution(4184264330389161933)
XLA Ops:
  0.0 2.1 %pack.1 = (bf16[16,16,640]{2,1,0:T(8,128)(2,1)}, bf16[8,16,1024]{2,1,0:T(8,128)(2,1)S(1)}) custom-call(f32[512,256]{1,0:T(8,128)} %filt_hbm.1, s32[4,128]{1,0:T(4,128)} %bitcast.12, bf16[8,32,4096]{2,1,0:T(8,128)(2,1)} %bitcast.11), custom_call_target="tpu_custom_call" | custom-call | flops 262144 | bytes 1048576 | tf_op jit(solution)/shard_map/pack/pallas_call | solution.py:113
  2.1 6.1 %all-to-all-start = ((bf16[16,16,640]{2,1,0:T(8,128)(2,1)}), bf16[16,16,640]{2,1,0:T(8,128)(2,1)S(1)}, u32[]{:S(2)}, u32[]{:S(2)}) async-start(bf16[16,16,640]{2,1,0:T(8,128)(2,1)} %get-tuple-element.13), calls=%async_computation | async-start | bytes 655360 | tf_op jit(solution)/shard_map/all_to_all | solution.py:441
  8.2 4.8 %vocab.1.table = f32[48,512]{1,0:T(8,128)S(1)} custom-call(bf16[512,4096]{1,0:T(8,128)(2,1)} %embed_hbm.1, bf16[3,4096,256]{2,1,0:T(8,128)(2,1)} %bitcast.10), custom_call_target="tpu_custom_call" | custom-call | flops 1610612736 | bytes 8388608 | tf_op jit(solution)/shard_map/vocab/pallas_call | solution.py:173
  13.0 3.5 %all-to-all-done.recv = bf16[16,16,640]{2,1,0:T(8,128)(2,1)S(1)} async-done(((bf16[16,16,640]{2,1,0:T(8,128)(2,1)}), bf16[16,16,640]{2,1,0:T(8,128)(2,1)S(1)}, u32[]{:S(2)}, u32[]{:S(2)}) %all-to-all-start) | async-done | bytes 327712 | tf_op jit(solution)/shard_map/all_to_all | solution.py:441
  16.5 8.3 %convolve.1 = bf16[2,2,2,8,16,512]{5,4,3,2,1,0:T(8,128)(2,1)} custom-call(bf16[16,16,640]{2,1,0:T(8,128)(2,1)S(1)} %all-to-all-done.recv, f32[48,512]{1,0:T(8,128)S(1)} %vocab.1.table, f32[3,3,256]{2,1,0:T(4,128)} %refs_0_.1, f32[1,256]{1,0:T(1,128)} %bitcast.13, bf16[144,256]{1,0:T(8,128)(2,1)} %constant.10.clone.refs_2_, ...), custom_call_target="tpu_custom_call" | custom-call | flops 4294967296 | bytes 4194304 | tf_op jit(solution)/shard_map/convolve/pallas_call | solution.py:331
  24.8 9.1 %all-to-all-start.1 = ((bf16[64,16,512]{2,1,0:T(8,128)(2,1)}), bf16[64,16,512]{2,1,0:T(8,128)(2,1)S(1)}, u32[]{:S(2)}, u32[]{:S(2)}) async-start(bf16[64,16,512]{2,1,0:T(8,128)(2,1)} %bitcast.4), calls=%async_computation.1 | async-start | bytes 2097152 | tf_op jit(solution)/shard_map/all_to_all | solution.py:444
  33.9 3.2 %collective-permute-start = (bf16[128,1024]{1,0:T(8,128)(2,1)S(1)}, bf16[128,1024]{1,0:T(8,128)(2,1)S(1)}, u32[]{:S(2)}, u32[]{:S(2)}) collective-permute-start(bf16[128,1024]{1,0:T(8,128)(2,1)S(1)} %bitcast.8), channel_id=1, source_target_pairs={{0,1},{1,0},{2,3},{3,2},{4,5},{5,4},{6,7},{7,6},{8,9},{9,8},{10,11... | collective-permute-start | bytes 786440 | tf_op jit(solution)/shard_map/ppermute | solution.py:430
  37.0 18.1 %collective-permute-done = bf16[128,1024]{1,0:T(8,128)(2,1)S(1)} collective-permute-done((bf16[128,1024]{1,0:T(8,128)(2,1)S(1)}, bf16[128,1024]{1,0:T(8,128)(2,1)S(1)}, u32[]{:S(2)}, u32[]{:S(2)}) %collective-permute-start) | collective-permute-done | bytes 262176 | tf_op jit(solution)/shard_map/ppermute | solution.py:430
  55.2 2.2 %collective-permute-start.3 = (bf16[256,1024]{1,0:T(8,128)(2,1)S(1)}, bf16[256,1024]{1,0:T(8,128)(2,1)S(1)}, u32[]{:S(2)}, u32[]{:S(2)}) collective-permute-start(bf16[256,1024]{1,0:T(8,128)(2,1)S(1)} %pad_maximum_fusion.refs_0_), channel_id=1, source_target_pairs={{0,6},{1,7},{2,4},{3,5},{4,2},{5,3},{6,0},{7,1},{8,14},{9,15},{10,... | collective-permute-start | bytes 1572872 | tf_op jit(solution)/shard_map/ppermute | solution.py:430
  57.4 1.1 %collective-permute-start.2 = (bf16[256,1024]{1,0:T(8,128)(2,1)S(1)}, bf16[256,1024]{1,0:T(8,128)(2,1)S(1)}, u32[]{:S(2)}, u32[]{:S(2)}) collective-permute-start(bf16[256,1024]{1,0:T(8,128)(2,1)S(1)} %pad_maximum_fusion.refs_0_), channel_id=1, source_target_pairs={{0,4},{1,5},{2,6},{3,7},{4,0},{5,1},{6,2},{7,3},{8,12},{9,13},{10,... | collective-permute-start | bytes 1572872 | tf_op jit(solution)/shard_map/ppermute | solution.py:430
  58.5 0.8 collective-permute-start.1
  59.4 21.6 %collective-permute-done.3.refs_3_ = bf16[256,1024]{1,0:T(8,128)(2,1)S(1)} collective-permute-done((bf16[256,1024]{1,0:T(8,128)(2,1)S(1)}, bf16[256,1024]{1,0:T(8,128)(2,1)S(1)}, u32[]{:S(2)}, u32[]{:S(2)}) %collective-permute-start.3) | collective-permute-done | bytes 524320 | tf_op jit(solution)/shard_map/ppermute | solution.py:430
  80.9 0.6 collective-permute-done.1.refs_1_
  81.6 1.3 %project.1 = (f32[256,1024]{1,0:T(8,128)S(1)}, bf16[256,1024]{1,0:T(8,128)(2,1)S(1)}) custom-call(bf16[8,8,16,512]{3,2,1,0:T(8,128)(2,1)S(1)} %bitcast.7, bf16[256,1024]{1,0:T(8,128)(2,1)S(1)} %pad_maximum_fusion.refs_0_, bf16[256,1024]{1,0:T(8,128)(2,1)S(1)} %collective-permute-done.1.refs_1_, bf16[256,1024]{1,0:T(8,128)(2,1)S(1)} %collective-permute-done.2.refs_2_, ...), custom_call_target="tpu_custom_call" | custom-call | flops 1073741824 | bytes 5242880 | tf_op jit(solution)/shard_map/project/pallas_call | solution.py:370
  82.9 0.1 collective-permute-start.4
  82.9 1.9 %collective-permute-done.4.came = bf16[256,1024]{1,0:T(8,128)(2,1)S(1)} collective-permute-done((bf16[256,1024]{1,0:T(8,128)(2,1)S(1)}, bf16[256,1024]{1,0:T(8,128)(2,1)S(1)}, u32[]{:S(2)}, u32[]{:S(2)}) %collective-permute-start.4) | collective-permute-done | bytes 524320 | tf_op jit(solution)/shard_map/ppermute | solution.py:430
  84.8 0.1 combine.1
  84.9 1.0 %collective-permute-start.5 = (bf16[64,1024]{1,0:T(8,128)(2,1)S(1)}, bf16[64,1024]{1,0:T(8,128)(2,1)S(1)}, u32[]{:S(2)}, u32[]{:S(2)}) collective-permute-start(bf16[64,1024]{1,0:T(8,128)(2,1)S(1)} %get-tuple-element.18), channel_id=1, source_target_pairs={{0,16},{1,17},{2,18},{3,19},{4,20},{5,21},{6,22},{7,23},{8,24},{9,... | collective-permute-start | bytes 393224 | tf_op jit(solution)/shard_map/ppermute | solution.py:430
  85.9 1.3 %collective-permute-start.6 = (bf16[64,1024]{1,0:T(8,128)(2,1)S(1)}, bf16[64,1024]{1,0:T(8,128)(2,1)S(1)}, u32[]{:S(2)}, u32[]{:S(2)}) collective-permute-start(bf16[64,1024]{1,0:T(8,128)(2,1)S(1)} %get-tuple-element.19), channel_id=1, source_target_pairs={{0,32},{1,33},{2,34},{3,35},{4,36},{5,37},{6,38},{7,39},{8,40},{9,... | collective-permute-start | bytes 393224 | tf_op jit(solution)/shard_map/ppermute | solution.py:430
  87.2 1.3 %collective-permute-start.7 = (bf16[64,1024]{1,0:T(8,128)(2,1)S(1)}, bf16[64,1024]{1,0:T(8,128)(2,1)S(1)}, u32[]{:S(2)}, u32[]{:S(2)}) collective-permute-start(bf16[64,1024]{1,0:T(8,128)(2,1)S(1)} %get-tuple-element.20), channel_id=1, source_target_pairs={{0,48},{1,49},{2,50},{3,51},{4,52},{5,53},{6,54},{7,55},{8,56},{9,... | collective-permute-start | bytes 393224 | tf_op jit(solution)/shard_map/ppermute | solution.py:430
  88.5 2.0 %collective-permute-done.5.refs_1_ = bf16[64,1024]{1,0:T(8,128)(2,1)S(1)} collective-permute-done((bf16[64,1024]{1,0:T(8,128)(2,1)S(1)}, bf16[64,1024]{1,0:T(8,128)(2,1)S(1)}, u32[]{:S(2)}, u32[]{:S(2)}) %collective-permute-start.5) | collective-permute-done | bytes 131104 | tf_op jit(solution)/shard_map/ppermute | solution.py:430
  90.6 1.6 %collective-permute-done.6.refs_2_ = bf16[64,1024]{1,0:T(8,128)(2,1)S(1)} collective-permute-done((bf16[64,1024]{1,0:T(8,128)(2,1)S(1)}, bf16[64,1024]{1,0:T(8,128)(2,1)S(1)}, u32[]{:S(2)}, u32[]{:S(2)}) %collective-permute-start.6) | collective-permute-done | bytes 131104 | tf_op jit(solution)/shard_map/ppermute | solution.py:430
  92.2 2.4 %collective-permute-done.7.refs_3_ = bf16[64,1024]{1,0:T(8,128)(2,1)S(1)} collective-permute-done((bf16[64,1024]{1,0:T(8,128)(2,1)S(1)}, bf16[64,1024]{1,0:T(8,128)(2,1)S(1)}, u32[]{:S(2)}, u32[]{:S(2)}) %collective-permute-start.7) | collective-permute-done | bytes 131104 | tf_op jit(solution)/shard_map/ppermute | solution.py:430
  94.5 0.8 assemble.1
  (3 shorter events, 0.0 us)
Async XLA Ops:
  2.1 14.3 %all-to-all-start = ((bf16[16,16,640]{2,1,0:T(8,128)(2,1)}), bf16[16,16,640]{2,1,0:T(8,128)(2,1)S(1)}, u32[]{:S(2)}, u32[]{:S(2)}) async-start(bf16[16,16,640]{2,1,0:T(8,128)(2,1)} %get-tuple-element.13), calls=%async_computation | async-start | bytes 655360 | tf_op jit(solution)/shard_map/all_to_all | solution.py:441
  24.8 56.8 %all-to-all-start.1 = ((bf16[64,16,512]{2,1,0:T(8,128)(2,1)}), bf16[64,16,512]{2,1,0:T(8,128)(2,1)S(1)}, u32[]{:S(2)}, u32[]{:S(2)}) async-start(bf16[64,16,512]{2,1,0:T(8,128)(2,1)} %bitcast.4), calls=%async_computation.1 | async-start | bytes 2097152 | tf_op jit(solution)/shard_map/all_to_all | solution.py:444
  33.9 21.3 %collective-permute-start = (bf16[128,1024]{1,0:T(8,128)(2,1)S(1)}, bf16[128,1024]{1,0:T(8,128)(2,1)S(1)}, u32[]{:S(2)}, u32[]{:S(2)}) collective-permute-start(bf16[128,1024]{1,0:T(8,128)(2,1)S(1)} %bitcast.8), channel_id=1, source_target_pairs={{0,1},{1,0},{2,3},{3,2},{4,5},{5,4},{6,7},{7,6},{8,9},{9,8},{10,11... | collective-permute-start | bytes 786440 | tf_op jit(solution)/shard_map/ppermute | solution.py:430
  55.2 25.7 %collective-permute-start.3 = (bf16[256,1024]{1,0:T(8,128)(2,1)S(1)}, bf16[256,1024]{1,0:T(8,128)(2,1)S(1)}, u32[]{:S(2)}, u32[]{:S(2)}) collective-permute-start(bf16[256,1024]{1,0:T(8,128)(2,1)S(1)} %pad_maximum_fusion.refs_0_), channel_id=1, source_target_pairs={{0,6},{1,7},{2,4},{3,5},{4,2},{5,3},{6,0},{7,1},{8,14},{9,15},{10,... | collective-permute-start | bytes 1572872 | tf_op jit(solution)/shard_map/ppermute | solution.py:430
  57.4 23.5 %collective-permute-start.2 = (bf16[256,1024]{1,0:T(8,128)(2,1)S(1)}, bf16[256,1024]{1,0:T(8,128)(2,1)S(1)}, u32[]{:S(2)}, u32[]{:S(2)}) collective-permute-start(bf16[256,1024]{1,0:T(8,128)(2,1)S(1)} %pad_maximum_fusion.refs_0_), channel_id=1, source_target_pairs={{0,4},{1,5},{2,6},{3,7},{4,0},{5,1},{6,2},{7,3},{8,12},{9,13},{10,... | collective-permute-start | bytes 1572872 | tf_op jit(solution)/shard_map/ppermute | solution.py:430
  58.5 23.0 %collective-permute-start.1 = (bf16[256,1024]{1,0:T(8,128)(2,1)S(1)}, bf16[256,1024]{1,0:T(8,128)(2,1)S(1)}, u32[]{:S(2)}, u32[]{:S(2)}) collective-permute-start(bf16[256,1024]{1,0:T(8,128)(2,1)S(1)} %pad_maximum_fusion.refs_0_), channel_id=1, source_target_pairs={{0,2},{1,3},{2,0},{3,1},{4,6},{5,7},{6,4},{7,5},{8,10},{9,11},{10,... | collective-permute-start | bytes 1572872 | tf_op jit(solution)/shard_map/ppermute | solution.py:430
  82.9 2.0 %collective-permute-start.4 = (bf16[256,1024]{1,0:T(8,128)(2,1)S(1)}, bf16[256,1024]{1,0:T(8,128)(2,1)S(1)}, u32[]{:S(2)}, u32[]{:S(2)}) collective-permute-start(bf16[256,1024]{1,0:T(8,128)(2,1)S(1)} %get-tuple-element.16), channel_id=1, source_target_pairs={{0,8},{1,9},{2,10},{3,11},{4,12},{5,13},{6,14},{7,15},{8,0},{9,1},... | collective-permute-start | bytes 1572872 | tf_op jit(solution)/shard_map/ppermute | solution.py:430
  84.9 5.6 %collective-permute-start.5 = (bf16[64,1024]{1,0:T(8,128)(2,1)S(1)}, bf16[64,1024]{1,0:T(8,128)(2,1)S(1)}, u32[]{:S(2)}, u32[]{:S(2)}) collective-permute-start(bf16[64,1024]{1,0:T(8,128)(2,1)S(1)} %get-tuple-element.18), channel_id=1, source_target_pairs={{0,16},{1,17},{2,18},{3,19},{4,20},{5,21},{6,22},{7,23},{8,24},{9,... | collective-permute-start | bytes 393224 | tf_op jit(solution)/shard_map/ppermute | solution.py:430
  85.9 6.2 %collective-permute-start.6 = (bf16[64,1024]{1,0:T(8,128)(2,1)S(1)}, bf16[64,1024]{1,0:T(8,128)(2,1)S(1)}, u32[]{:S(2)}, u32[]{:S(2)}) collective-permute-start(bf16[64,1024]{1,0:T(8,128)(2,1)S(1)} %get-tuple-element.19), channel_id=1, source_target_pairs={{0,32},{1,33},{2,34},{3,35},{4,36},{5,37},{6,38},{7,39},{8,40},{9,... | collective-permute-start | bytes 393224 | tf_op jit(solution)/shard_map/ppermute | solution.py:430
  87.2 7.4 %collective-permute-start.7 = (bf16[64,1024]{1,0:T(8,128)(2,1)S(1)}, bf16[64,1024]{1,0:T(8,128)(2,1)S(1)}, u32[]{:S(2)}, u32[]{:S(2)}) collective-permute-start(bf16[64,1024]{1,0:T(8,128)(2,1)S(1)} %get-tuple-element.20), channel_id=1, source_target_pairs={{0,48},{1,49},{2,50},{3,51},{4,52},{5,53},{6,54},{7,55},{8,56},{9,... | collective-permute-start | bytes 393224 | tf_op jit(solution)/shard_map/ppermute | solution.py:430

commit v4 on v3

--- a/solution.py
+++ b/solution.py
@@ -191,6 +191,7 @@
 ):
     sources, (out, taps, token, gated, other, shaped, spec_high, spec_low, lags) = refs[:7], refs[7:16]
     short, direct, first_signal, first_filter, twiddle, second, last = held = refs[16:23]
+    chunk, out_sems = refs[24:]
     copies = [
         pltpu.make_async_copy(source, target, refs[23].at[index])
         for index, (source, target) in enumerate(zip(sources, held))
@@ -307,20 +308,30 @@
 
     skip = taps[9 * CH :, :]
     low_half = lax.broadcasted_iota(jnp.int32, (CH, 128), 1) < 64
-    for a, top, core_to, h in itertools.product(range(2), range(2), range(2), range(4)):
-        done = []
-        for zl in range(2):
-            shard = 8 * a + top * 4 + zl * 2 + core_to
-            rows = slice((4 * shard + h) * CH, (4 * shard + h + 1) * CH)
-            done.append(other[rows, :] * (shaped[rows, :] + skip * gated[rows, :]))
-        first, then = done
-        even = jnp.where(low_half, first, pltpu.roll(then, 64, 1)).astype(BF)
-        odd = jnp.where(low_half, pltpu.roll(first, 64, 1), then).astype(BF)
-        half = jnp.bitwise_xor(core, core_to) if core_to else core
-        columns = pl.ds(pl.multiple_of(half * 256 + top * 128, 128), 128)
-        for to_y, to_z in itertools.product(range(2), range(2)):
-            out[a, to_y, to_z, 2 * h, :, columns] = even
-            out[a, to_y, to_z, 2 * h + 1, :, columns] = odd
+    copies = []
+    for a, h in itertools.product(range(2), range(4)):
+        for top, core_to in itertools.product(range(2), range(2)):
+            done = []
+            for zl in range(2):
+                shard = 8 * a + top * 4 + zl * 2 + core_to
+                rows = slice((4 * shard + h) * CH, (4 * shard + h + 1) * CH)
+                done.append(other[rows, :] * (shaped[rows, :] + skip * gated[rows, :]))
+            first, then = done
+            half = jnp.bitwise_xor(core, core_to) if core_to else core
+            columns = pl.ds(pl.multiple_of(half * 256 + top * 128, 128), 128)
+            chunk[a * 8 + 2 * h, :, columns] = jnp.where(low_half, first, pltpu.roll(then, 64, 1)).astype(BF)
+            chunk[a * 8 + 2 * h + 1, :, columns] = jnp.where(low_half, pltpu.roll(first, 64, 1), then).astype(BF)
+        for member in range(4):
+            copies.append(
+                pltpu.make_async_copy(
+                    chunk.at[a * 8 + 2 * h : a * 8 + 2 * h + 2],
+                    out.at[pl.ds((a * 4 + member) * 8 + 2 * h, 2)],
+                    out_sems.at[(a * 4 + h) * 4 + member],
+                )
+            )
+            copies[-1].start()
+    for copy in copies:
+        copy.wait()
 
 
 def convolve(recv, table, short_filter, skip_gain):
@@ -330,9 +341,9 @@
     fetched = [short_filter, skip_gain[None, :], *consts]
     return pl.pallas_call(
         convolve_kernel,
-        out_shape=jax.ShapeDtypeStruct((2, 2, 2, 8, CH, 512), BF),
+        out_shape=pltpu.HBM((64, CH, 512), BF),
         in_specs=[whole] * 2 + [hbm] * 7,
-        out_specs=whole,
+        out_specs=hbm,
         scratch_shapes=[
             pltpu.VMEM((10 * CH, 128), F32),
             pltpu.VMEM((128, 128), jnp.int32),
@@ -344,6 +355,8 @@
             pltpu.VMEM((64 * CH, 128), F32),
             *[pltpu.VMEM(array.shape, array.dtype) for array in fetched],
             pltpu.SemaphoreType.DMA((len(fetched),)),
+            pltpu.VMEM((16, CH, 512), BF),
+            pltpu.SemaphoreType.DMA((32,)),
         ],
         cost_estimate=pl.CostEstimate(flops=4 << 30, bytes_accessed=4 << 20, transcendentals=0),
         compiler_params=pltpu.CompilerParams(vmem_limit_bytes=20 << 20),
@@ -351,30 +364,33 @@
     )(recv, table, *[in_hbm(array) for array in fetched])
 
 
-def project_kernel(recv, *refs):
-    weights, keep, send = refs[:4], refs[4], refs[5]
+def project_kernel(half, recv, own, one, upper, lower, three, out):
     chan = lax.axis_index("x") * 2 + lax.axis_index("zh")
     total = None
     for index in range(4):
         lhs = jnp.concatenate(
-            [recv[:, jnp.bitwise_xor(chan, 2 * index + i)].reshape(128, 512) for i in range(2)], 0
+            [
+                recv[:, jnp.bitwise_xor(chan, 2 * index + i), :, half * 256 : (half + 1) * 256].reshape(128, 256)
+                for i in range(2)
+            ],
+            0,
         )
-        part = mm(lhs, weights[index][...], (((0,), (0,)), ((), ())))
+        rhs = jnp.concatenate([upper[...], lower[...]], 0) if index == 2 else (own, one, None, three)[index][...]
+        part = mm(lhs, rhs, (((0,), (0,)), ((), ())))
         total = part if total is None else total + part
-    keep[...] = total[:256]
-    send[...] = total[256:].astype(BF)
-
-
-def project(recv, weights):
+    out[...] = total.astype(out.dtype)
+
+
+def project(recv, weights, half):
     whole = pl.BlockSpec(memory_space=pltpu.VMEM)
     return pl.pallas_call(
-        project_kernel,
-        out_shape=(jax.ShapeDtypeStruct((256, 1024), F32), jax.ShapeDtypeStruct((256, 1024), BF)),
-        in_specs=[whole] * 5,
-        out_specs=(whole, whole),
-        cost_estimate=pl.CostEstimate(flops=1 << 30, bytes_accessed=5 << 20, transcendentals=0),
+        functools.partial(project_kernel, half),
+        out_shape=jax.ShapeDtypeStruct((256, 1024), BF if half else F32),
+        in_specs=[whole] * 6,
+        out_specs=whole,
+        cost_estimate=pl.CostEstimate(flops=1 << 29, bytes_accessed=4 << 20, transcendentals=0),
         compiler_params=pltpu.CompilerParams(vmem_limit_bytes=20 << 20),
-        name="project",
+        name="send" if half else "keep",
     )(recv.reshape(8, 8, CH, 512), *weights)
 
 
@@ -435,15 +451,19 @@
     held = held.reshape(128, 1024)
     across = permuted(held, lambda d: {"zh": d["zh"] ^ 1})
     both = jnp.concatenate([held, across], 0)
-    weights = [both]
-    for index in range(1, 4):
-        weights.append(permuted(both, lambda d: {"x": d["x"] ^ index}))
+    beside = {}
+    for index in (1, 3):
+        beside[index] = permuted(both, lambda d: {"x": d["x"] ^ index})
     recv = lax.all_to_all(payload, SEQ, 0, 0, tiled=True)
     table = vocab(embed_table, in_weight)
     chunks = convolve(recv, table, short_filter, skip_gain)
-    recv = lax.all_to_all(chunks.reshape(64, CH, 512), ("y", "zl", "x", "zh"), 0, 0, tiled=True)
-    keep, send = project(recv, weights)
+    recv = lax.all_to_all(chunks, ("y", "zl", "x", "zh"), 0, 0, tiled=True)
+    upper = permuted(beside[3][:128], lambda d: {"x": d["x"] ^ 1})
+    lower = permuted(beside[1][128:], lambda d: {"x": d["x"] ^ 3})
+    weights = [both, beside[1], upper, lower, beside[3]]
+    send = project(recv, weights, 1)
     came = permuted(send, lambda d: {"core": 1 - d["core"]})
+    keep = project(recv, weights, 0)
     pieces = list(combine(keep, came))
     for index in range(1, 4):
         pieces[index] = permuted(pieces[index], lambda d: {"y": d["y"] ^ (index // 2), "zl": d["zl"] ^ (index % 2)})

time: 95.7 us -> 83.1 us (0.87)
  waiting for transfers between devices: 51.7 us -> 37.6 us
    ppermute x8 -> x9, waiting for transfers between devices: 48.2 us -> 37.6 us  [permuted(): return lax.ppermute(block, AXES, pairs)]
    all_to_all x1, waiting for transfers between devices: 3.48 us -> 0.01 us  [body(): recv = lax.all_to_all(payload, SEQ, 0, 0, tiled=True)]
    ppermute x8 -> x9, starting transfers between devices: 11 us -> 12 us  [permuted(): return lax.ppermute(block, AXES, pairs)]
    pallas_call x2 -> x3, Pallas kernels: 9.56 us -> 9.92 us  [the longest x1 8.45 us: convolve(): pl.pallas_call(convolve_kernel, out_shape=pltpu.HBM((64, CH, 512), BF), i...]
  transfers between devices with their start and end apart: 10 -> 11, of which waited for: 8 -> 7; matrix products, arithmetic and copies ran while one was open for 0% -> 0% of each run, Pallas kernels for 5% -> 17%
where the time goes in v4:
time: 83.1 us; the launch traced here: 82.5 us
  waiting for transfers between devices  37.6 us (45%)
  starting transfers between devices  27 us (32%)
  Pallas kernels  17.8 us (21%)
    ppermute x9, waiting for transfers between devices, permuted(): return lax.ppermute(block, AXES, pairs)  37.6 us
    ppermute x9, starting transfers between devices, permuted(): return lax.ppermute(block, AXES, pairs)  12 us
    all_to_all x1, starting transfers between devices, body(): recv = lax.all_to_all(chunks, ('y', 'zl', 'x', 'zh'), 0, 0, tiled=True)  8.91 us
    pallas_call x1, Pallas kernels, convolve(): pl.pallas_call(convolve_kernel, out_shape=pltpu.HBM((64, CH, 512), BF), i...  8.45 us
    all_to_all x1, starting transfers between devices, body(): recv = lax.all_to_all(payload, SEQ, 0, 0, tiled=True)  6.05 us
    pallas_call x1, Pallas kernels, vocab(): pl.pallas_call(vocab_kernel, out_shape=jax.ShapeDtypeStruct((3 * CH, 512)...  4.8 us
    pallas_call x1, Pallas kernels, pack(): pl.pallas_call(pack_kernel, out_shape=(jax.ShapeDtypeStruct((16, CH, 640)...  2.14 us
  transfers between devices with their start and end apart: 11, of which 7 were waited for; matrix products, arithmetic and copies ran while one was open for 0% of the time, Pallas kernels for 17%

profile of v4, /device:TPU:0, one launch (start us, length us, event | category | flops | bytes accessed | tf_op | source)
XLA Modules:
  0.0 82.5 jit_solution(8655235816671497833)
XLA Ops:
  0.0 2.1 %pack.1 = (bf16[16,16,640]{2,1,0:T(8,128)(2,1)}, bf16[8,16,1024]{2,1,0:T(8,128)(2,1)S(1)}) custom-call(f32[512,256]{1,0:T(8,128)} %filt_hbm.1, s32[4,128]{1,0:T(4,128)} %bitcast.12, bf16[8,32,4096]{2,1,0:T(8,128)(2,1)} %bitcast.11), custom_call_target="tpu_custom_call" | custom-call | flops 262144 | bytes 1048576 | tf_op jit(solution)/shard_map/pack/pallas_call | solution.py:113
  2.1 6.1 %all-to-all-start = ((bf16[16,16,640]{2,1,0:T(8,128)(2,1)}), bf16[16,16,640]{2,1,0:T(8,128)(2,1)S(1)}, u32[]{:S(2)}, u32[]{:S(2)}) async-start(bf16[16,16,640]{2,1,0:T(8,128)(2,1)} %get-tuple-element.11), calls=%async_computation | async-start | bytes 655360 | tf_op jit(solution)/shard_map/all_to_all | solution.py:457
  8.2 3.7 %collective-permute-start = (bf16[128,1024]{1,0:T(8,128)(2,1)S(1)}, bf16[128,1024]{1,0:T(8,128)(2,1)S(1)}, u32[]{:S(2)}, u32[]{:S(2)}) collective-permute-start(bf16[128,1024]{1,0:T(8,128)(2,1)S(1)} %bitcast.8), channel_id=1, source_target_pairs={{0,1},{1,0},{2,3},{3,2},{4,5},{5,4},{6,7},{7,6},{8,9},{9,8},{10,11... | collective-permute-start | bytes 786440 | tf_op jit(solution)/shard_map/ppermute | solution.py:446
  11.9 4.8 %vocab.1.table = f32[48,512]{1,0:T(8,128)S(1)} custom-call(bf16[512,4096]{1,0:T(8,128)(2,1)} %embed_hbm.1, bf16[3,4096,256]{2,1,0:T(8,128)(2,1)} %bitcast.10), custom_call_target="tpu_custom_call" | custom-call | flops 1610612736 | bytes 8388608 | tf_op jit(solution)/shard_map/vocab/pallas_call | solution.py:173
  16.7 8.4 %convolve.1 = bf16[64,16,512]{2,1,0:T(8,128)(2,1)} custom-call(bf16[16,16,640]{2,1,0:T(8,128)(2,1)S(1)} %all-to-all-done.recv, f32[48,512]{1,0:T(8,128)S(1)} %vocab.1.table, f32[3,3,256]{2,1,0:T(4,128)} %refs_0_.1, f32[1,256]{1,0:T(1,128)} %bitcast.13, bf16[144,256]{1,0:T(8,128)(2,1)} %constant.10.clone.refs_2_, bf16[144,128]{1,0:T(8,128)(2,1)} %constant.11.clone.refs_3_, ...), custom_call_target="tpu_custom_call" | custom-call | flops 4294967296 | bytes 4194304 | tf_op jit(solution)/shard_map/convolve/pallas_call | solution.py:342
  25.1 8.9 %all-to-all-start.1 = ((bf16[64,16,512]{2,1,0:T(8,128)(2,1)}), bf16[64,16,512]{2,1,0:T(8,128)(2,1)S(1)}, u32[]{:S(2)}, u32[]{:S(2)}) async-start(bf16[64,16,512]{2,1,0:T(8,128)(2,1)} %convolve.1), calls=%async_computation.1 | async-start | bytes 2097152 | tf_op jit(solution)/shard_map/all_to_all | solution.py:460
  34.1 2.9 %collective-permute-start.2 = (bf16[256,1024]{1,0:T(8,128)(2,1)S(1)}, bf16[256,1024]{1,0:T(8,128)(2,1)S(1)}, u32[]{:S(2)}, u32[]{:S(2)}) collective-permute-start(bf16[256,1024]{1,0:T(8,128)(2,1)S(1)} %pad_maximum_fusion.own), channel_id=1, source_target_pairs={{0,6},{1,7},{2,4},{3,5},{4,2},{5,3},{6,0},{7,1},{8,14},{9,15},{10,... | collective-permute-start | bytes 1572872 | tf_op jit(solution)/shard_map/ppermute | solution.py:446
  37.0 0.3 collective-permute-start.1
  37.2 22.7 %collective-permute-done.2.three = bf16[256,1024]{1,0:T(8,128)(2,1)S(1)} collective-permute-done((bf16[256,1024]{1,0:T(8,128)(2,1)S(1)}, bf16[256,1024]{1,0:T(8,128)(2,1)S(1)}, u32[]{:S(2)}, u32[]{:S(2)}) %collective-permute-start.2) | collective-permute-done | bytes 524320 | tf_op jit(solution)/shard_map/ppermute | solution.py:446
  59.9 0.3 collective-permute-start.3
  60.3 1.2 %collective-permute-start.4 = (bf16[128,1024]{1,0:T(8,128)(2,1)S(1)}, bf16[128,1024]{1,0:T(8,128)(2,1)S(1)}, u32[]{:S(2)}, u32[]{:S(2)}) collective-permute-start(bf16[128,1024]{1,0:T(8,128)(2,1)S(1)} %slice.9), channel_id=1, source_target_pairs={{0,6},{1,7},{2,4},{3,5},{4,2},{5,3},{6,0},{7,1},{8,14},{9,15},{10,... | collective-permute-start | bytes 786440 | tf_op jit(solution)/shard_map/ppermute | solution.py:446
  61.5 6.4 %collective-permute-done.3.upper = bf16[128,1024]{1,0:T(8,128)(2,1)S(1)} collective-permute-done((bf16[128,1024]{1,0:T(8,128)(2,1)S(1)}, bf16[128,1024]{1,0:T(8,128)(2,1)S(1)}, u32[]{:S(2)}, u32[]{:S(2)}) %collective-permute-start.3) | collective-permute-done | bytes 262176 | tf_op jit(solution)/shard_map/ppermute | solution.py:446
  67.9 1.3 %collective-permute-done.4.lower = bf16[128,1024]{1,0:T(8,128)(2,1)S(1)} collective-permute-done((bf16[128,1024]{1,0:T(8,128)(2,1)S(1)}, bf16[128,1024]{1,0:T(8,128)(2,1)S(1)}, u32[]{:S(2)}, u32[]{:S(2)}) %collective-permute-start.4) | collective-permute-done | bytes 262176 | tf_op jit(solution)/shard_map/ppermute | solution.py:446
  69.3 0.7 send.1
  70.1 0.7 keep.1
  70.8 1.2 %collective-permute-done.5.came = bf16[256,1024]{1,0:T(8,128)(2,1)S(1)} collective-permute-done((bf16[256,1024]{1,0:T(8,128)(2,1)S(1)}, bf16[256,1024]{1,0:T(8,128)(2,1)S(1)}, u32[]{:S(2)}, u32[]{:S(2)}) %collective-permute-start.5) | collective-permute-done | bytes 524320 | tf_op jit(solution)/shard_map/ppermute | solution.py:446
  72.0 0.1 combine.1
  72.1 1.5 %collective-permute-start.6 = (bf16[64,1024]{1,0:T(8,128)(2,1)S(1)}, bf16[64,1024]{1,0:T(8,128)(2,1)S(1)}, u32[]{:S(2)}, u32[]{:S(2)}) collective-permute-start(bf16[64,1024]{1,0:T(8,128)(2,1)S(1)} %get-tuple-element.14), channel_id=1, source_target_pairs={{0,16},{1,17},{2,18},{3,19},{4,20},{5,21},{6,22},{7,23},{8,24},{9,... | collective-permute-start | bytes 393224 | tf_op jit(solution)/shard_map/ppermute | solution.py:446
  73.6 1.5 %collective-permute-start.7 = (bf16[64,1024]{1,0:T(8,128)(2,1)S(1)}, bf16[64,1024]{1,0:T(8,128)(2,1)S(1)}, u32[]{:S(2)}, u32[]{:S(2)}) collective-permute-start(bf16[64,1024]{1,0:T(8,128)(2,1)S(1)} %get-tuple-element.15), channel_id=1, source_target_pairs={{0,32},{1,33},{2,34},{3,35},{4,36},{5,37},{6,38},{7,39},{8,40},{9,... | collective-permute-start | bytes 393224 | tf_op jit(solution)/shard_map/ppermute | solution.py:446
  75.2 0.5 collective-permute-start.8
  75.6 2.0 %collective-permute-done.6.refs_1_ = bf16[64,1024]{1,0:T(8,128)(2,1)S(1)} collective-permute-done((bf16[64,1024]{1,0:T(8,128)(2,1)S(1)}, bf16[64,1024]{1,0:T(8,128)(2,1)S(1)}, u32[]{:S(2)}, u32[]{:S(2)}) %collective-permute-start.6) | collective-permute-done | bytes 131104 | tf_op jit(solution)/shard_map/ppermute | solution.py:446
  77.7 2.3 %collective-permute-done.7.refs_2_ = bf16[64,1024]{1,0:T(8,128)(2,1)S(1)} collective-permute-done((bf16[64,1024]{1,0:T(8,128)(2,1)S(1)}, bf16[64,1024]{1,0:T(8,128)(2,1)S(1)}, u32[]{:S(2)}, u32[]{:S(2)}) %collective-permute-start.7) | collective-permute-done | bytes 131104 | tf_op jit(solution)/shard_map/ppermute | solution.py:446
  80.0 1.7 %collective-permute-done.8.refs_3_ = bf16[64,1024]{1,0:T(8,128)(2,1)S(1)} collective-permute-done((bf16[64,1024]{1,0:T(8,128)(2,1)S(1)}, bf16[64,1024]{1,0:T(8,128)(2,1)S(1)}, u32[]{:S(2)}, u32[]{:S(2)}) %collective-permute-start.8) | collective-permute-done | bytes 131104 | tf_op jit(solution)/shard_map/ppermute | solution.py:446
  81.7 0.8 %assemble.1 = bf16[64,4096]{1,0:T(8,128)(2,1)} custom-call(bf16[64,1024]{1,0:T(8,128)(2,1)S(1)} %get-tuple-element.13.refs_0_, bf16[64,1024]{1,0:T(8,128)(2,1)S(1)} %collective-permute-done.6.refs_1_, bf16[64,1024]{1,0:T(8,128)(2,1)S(1)} %collective-permute-done.7.refs_2_, bf16[64,1024]{1,0:T(8,128)(2,1)S(1)} %collective-permute-done.8.refs_3_), custom_call_target="tpu_custom_call" | custom-call | bytes 1048576 | tf_op jit(solution)/shard_map/assemble/pallas_call | solution.py:426
  (8 shorter events, 0.2 us)
Async XLA Ops:
  2.1 14.5 %all-to-all-start = ((bf16[16,16,640]{2,1,0:T(8,128)(2,1)}), bf16[16,16,640]{2,1,0:T(8,128)(2,1)S(1)}, u32[]{:S(2)}, u32[]{:S(2)}) async-start(bf16[16,16,640]{2,1,0:T(8,128)(2,1)} %get-tuple-element.11), calls=%async_computation | async-start | bytes 655360 | tf_op jit(solution)/shard_map/all_to_all | solution.py:457
  8.2 25.9 %collective-permute-start = (bf16[128,1024]{1,0:T(8,128)(2,1)S(1)}, bf16[128,1024]{1,0:T(8,128)(2,1)S(1)}, u32[]{:S(2)}, u32[]{:S(2)}) collective-permute-start(bf16[128,1024]{1,0:T(8,128)(2,1)S(1)} %bitcast.8), channel_id=1, source_target_pairs={{0,1},{1,0},{2,3},{3,2},{4,5},{5,4},{6,7},{7,6},{8,9},{9,8},{10,11... | collective-permute-start | bytes 786440 | tf_op jit(solution)/shard_map/ppermute | solution.py:446
  25.1 44.1 %all-to-all-start.1 = ((bf16[64,16,512]{2,1,0:T(8,128)(2,1)}), bf16[64,16,512]{2,1,0:T(8,128)(2,1)S(1)}, u32[]{:S(2)}, u32[]{:S(2)}) async-start(bf16[64,16,512]{2,1,0:T(8,128)(2,1)} %convolve.1), calls=%async_computation.1 | async-start | bytes 2097152 | tf_op jit(solution)/shard_map/all_to_all | solution.py:460
  34.1 25.8 %collective-permute-start.2 = (bf16[256,1024]{1,0:T(8,128)(2,1)S(1)}, bf16[256,1024]{1,0:T(8,128)(2,1)S(1)}, u32[]{:S(2)}, u32[]{:S(2)}) collective-permute-start(bf16[256,1024]{1,0:T(8,128)(2,1)S(1)} %pad_maximum_fusion.own), channel_id=1, source_target_pairs={{0,6},{1,7},{2,4},{3,5},{4,2},{5,3},{6,0},{7,1},{8,14},{9,15},{10,... | collective-permute-start | bytes 1572872 | tf_op jit(solution)/shard_map/ppermute | solution.py:446
  37.0 23.3 %collective-permute-start.1 = (bf16[256,1024]{1,0:T(8,128)(2,1)S(1)}, bf16[256,1024]{1,0:T(8,128)(2,1)S(1)}, u32[]{:S(2)}, u32[]{:S(2)}) collective-permute-start(bf16[256,1024]{1,0:T(8,128)(2,1)S(1)} %pad_maximum_fusion.own), channel_id=1, source_target_pairs={{0,2},{1,3},{2,0},{3,1},{4,6},{5,7},{6,4},{7,5},{8,10},{9,11},{10,... | collective-permute-start | bytes 1572872 | tf_op jit(solution)/shard_map/ppermute | solution.py:446
  59.9 8.0 %collective-permute-start.3 = (bf16[128,1024]{1,0:T(8,128)(2,1)S(1)}, bf16[128,1024]{1,0:T(8,128)(2,1)S(1)}, u32[]{:S(2)}, u32[]{:S(2)}) collective-permute-start(bf16[128,1024]{1,0:T(8,128)(2,1)S(1)} %slice.8), channel_id=1, source_target_pairs={{0,2},{1,3},{2,0},{3,1},{4,6},{5,7},{6,4},{7,5},{8,10},{9,11},{10,... | collective-permute-start | bytes 786440 | tf_op jit(solution)/shard_map/ppermute | solution.py:446
  60.3 9.0 %collective-permute-start.4 = (bf16[128,1024]{1,0:T(8,128)(2,1)S(1)}, bf16[128,1024]{1,0:T(8,128)(2,1)S(1)}, u32[]{:S(2)}, u32[]{:S(2)}) collective-permute-start(bf16[128,1024]{1,0:T(8,128)(2,1)S(1)} %slice.9), channel_id=1, source_target_pairs={{0,6},{1,7},{2,4},{3,5},{4,2},{5,3},{6,0},{7,1},{8,14},{9,15},{10,... | collective-permute-start | bytes 786440 | tf_op jit(solution)/shard_map/ppermute | solution.py:446
  70.0 2.0 %collective-permute-start.5 = (bf16[256,1024]{1,0:T(8,128)(2,1)S(1)}, bf16[256,1024]{1,0:T(8,128)(2,1)S(1)}, u32[]{:S(2)}, u32[]{:S(2)}) collective-permute-start(bf16[256,1024]{1,0:T(8,128)(2,1)S(1)} %send.1), channel_id=1, source_target_pairs={{0,8},{1,9},{2,10},{3,11},{4,12},{5,13},{6,14},{7,15},{8,0},{9,1},... | collective-permute-start | bytes 1572872 | tf_op jit(solution)/shard_map/ppermute | solution.py:446
  72.1 5.6 %collective-permute-start.6 = (bf16[64,1024]{1,0:T(8,128)(2,1)S(1)}, bf16[64,1024]{1,0:T(8,128)(2,1)S(1)}, u32[]{:S(2)}, u32[]{:S(2)}) collective-permute-start(bf16[64,1024]{1,0:T(8,128)(2,1)S(1)} %get-tuple-element.14), channel_id=1, source_target_pairs={{0,16},{1,17},{2,18},{3,19},{4,20},{5,21},{6,22},{7,23},{8,24},{9,... | collective-permute-start | bytes 393224 | tf_op jit(solution)/shard_map/ppermute | solution.py:446
  73.6 6.4 %collective-permute-start.7 = (bf16[64,1024]{1,0:T(8,128)(2,1)S(1)}, bf16[64,1024]{1,0:T(8,128)(2,1)S(1)}, u32[]{:S(2)}, u32[]{:S(2)}) collective-permute-start(bf16[64,1024]{1,0:T(8,128)(2,1)S(1)} %get-tuple-element.15), channel_id=1, source_target_pairs={{0,32},{1,33},{2,34},{3,35},{4,36},{5,37},{6,38},{7,39},{8,40},{9,... | collective-permute-start | bytes 393224 | tf_op jit(solution)/shard_map/ppermute | solution.py:446
  75.2 6.5 %collective-permute-start.8 = (bf16[64,1024]{1,0:T(8,128)(2,1)S(1)}, bf16[64,1024]{1,0:T(8,128)(2,1)S(1)}, u32[]{:S(2)}, u32[]{:S(2)}) collective-permute-start(bf16[64,1024]{1,0:T(8,128)(2,1)S(1)} %get-tuple-element.16), channel_id=1, source_target_pairs={{0,48},{1,49},{2,50},{3,51},{4,52},{5,53},{6,54},{7,55},{8,56},{9,... | collective-permute-start | bytes 393224 | tf_op jit(solution)/shard_map/ppermute | solution.py:446

commit v5 on v4

--- a/solution.py
+++ b/solution.py
@@ -80,7 +80,7 @@
 
 
 def pack_kernel(filt_hbm, tokens_hbm, weight_hbm, payload, held, filt, tokens, sems):
-    parts = 4
+    parts = 2
     mine = weight_hbm.at[
         :,
         pl.ds(pl.multiple_of(lax.axis_index("core") * CH, CH), CH),
@@ -121,7 +121,7 @@
         scratch_shapes=[
             pltpu.VMEM((512, 256), F32),
             pltpu.VMEM((4, 128), jnp.int32),
-            pltpu.SemaphoreType.DMA((6,)),
+            pltpu.SemaphoreType.DMA((4,)),
         ],
         cost_estimate=pl.CostEstimate(flops=1 << 18, bytes_accessed=1 << 20, transcendentals=0),
         compiler_params=pltpu.CompilerParams(vmem_limit_bytes=6 << 20),
@@ -131,7 +131,8 @@
 
 STEPS = 4
 GROUP = 8
-UNROLL = 16
+BATCH = 4
+UNROLL = 4
 
 
 def vocab_kernel(embed_hbm, weight_hbm, table, embed, weight, sems):
@@ -198,6 +199,19 @@
     ]
     for copy in copies:
         copy.start()
+    for source in range(16):
+        digits = recv[source, :, 512:].astype(F32)
+        token[source * 8 : source * 8 + 8, :] = (digits[:8] * 16.0 + digits[8:]).astype(jnp.int32)
+        for q in range(4):
+            rows = slice(q * 256 + source * CH, q * 256 + (source + 1) * CH)
+            lags[rows, :] = recv[source, :, q * 128 : (q + 1) * 128].astype(F32)
+
+    banks = jnp.concatenate([table[:, i * 128 : (i + 1) * 128] for i in range(4)], 0).astype(BF)
+    line = lax.broadcasted_iota(jnp.int32, (256, 256), 0)
+    lane = lax.broadcasted_iota(jnp.int32, (256, 256), 1)
+    shift = (line == jnp.where(lane < 128, lane + 127, lane - 2)).astype(F32).astype(BF)
+    entry = lax.broadcasted_iota(jnp.int32, (128, 128), 0)
+
     copies[0].wait()
     copies[1].wait()
     seq, core = seq_index(), lax.axis_index("core")
@@ -209,42 +223,31 @@
         column = jnp.sum(jnp.where(mine, wide, 0.0), axis=1, keepdims=True)
         taps[index * CH : (index + 1) * CH, :] = jnp.broadcast_to(column, (CH, 128))
 
-    for source in range(16):
-        digits = recv[source, :, 512:].astype(F32)
-        token[source * 8 : source * 8 + 8, :] = (digits[:8] * 16.0 + digits[8:]).astype(jnp.int32)
-        for q in range(4):
-            rows = slice(q * 256 + source * CH, q * 256 + (source + 1) * CH)
-            lags[rows, :] = recv[source, :, q * 128 : (q + 1) * 128].astype(F32)
-
-    banks = jnp.concatenate([table[:, i * 128 : (i + 1) * 128] for i in range(4)], 0).astype(BF)
-    line = lax.broadcasted_iota(jnp.int32, (256, 256), 0)
-    lane = lax.broadcasted_iota(jnp.int32, (256, 256), 1)
-    shift = (line == jnp.where(lane < 128, lane + 127, lane - 2)).astype(F32).astype(BF)
-    entry = lax.broadcasted_iota(jnp.int32, (128, 128), 0)
-
-    def select(source, before):
-        rows = [token[pl.ds(source * 8 + q, 1), :] for q in range(4)]
-        chosen = [(entry == jnp.bitwise_and(row, 127)).astype(F32).astype(BF) for row in rows]
-        found = mm(banks, jnp.concatenate(chosen, 1))
-        bank = jnp.right_shift(jnp.concatenate(rows, 1), 7)
-        value = found[: 3 * CH]
-        for i in range(1, 4):
-            value = jnp.where(bank == i, found[i * 3 * CH : (i + 1) * 3 * CH], value)
-        narrow = value.astype(BF)
-        blocks = [before] + [narrow[:, q * 128 : (q + 1) * 128] for q in range(4)]
-        pairs = [jnp.concatenate([blocks[q], blocks[q + 1]], 1) for q in range(4)]
+    def select(step, before):
+        blocks = [before]
+        for source in range(BATCH):
+            rows = [token[pl.ds((step * BATCH + source) * 8 + q, 1), :] for q in range(4)]
+            chosen = [(entry == jnp.bitwise_and(row, 127)).astype(F32).astype(BF) for row in rows]
+            found = mm(banks, jnp.concatenate(chosen, 1))
+            bank = jnp.right_shift(jnp.concatenate(rows, 1), 7)
+            value = found[: 3 * CH]
+            for i in range(1, 4):
+                value = jnp.where(bank == i, found[i * 3 * CH : (i + 1) * 3 * CH], value)
+            narrow = value.astype(BF)
+            blocks += [narrow[:, q * 128 : (q + 1) * 128] for q in range(4)]
+        pairs = [jnp.concatenate([blocks[q], blocks[q + 1]], 1) for q in range(4 * BATCH)]
         lagged = mm(jnp.concatenate(pairs, 0), shift)
-        for q in range(4):
+        for q in range(4 * BATCH):
             lag = lagged[q * 3 * CH : (q + 1) * 3 * CH]
-            filtered = taps[: 3 * CH, :] * value[:, q * 128 : (q + 1) * 128]
+            filtered = taps[: 3 * CH, :] * blocks[q + 1].astype(F32)
             filtered = filtered + taps[3 * CH : 6 * CH, :] * lag[:, :128]
             filtered = filtered + taps[6 * CH : 9 * CH, :] * lag[:, 128:]
-            at = pl.ds(pl.multiple_of((source * 4 + q) * CH, CH), CH)
+            at = pl.ds(pl.multiple_of((step * 4 * BATCH + q) * CH, CH), CH)
             gated[at, :] = filtered[:CH] * filtered[2 * CH :]
             other[at, :] = filtered[CH : 2 * CH]
-        return blocks[4]
-
-    lax.fori_loop(0, 16, select, jnp.zeros((3 * CH, 128), BF), unroll=UNROLL)
+        return blocks[-1]
+
+    lax.fori_loop(0, 16 // BATCH, select, jnp.zeros((3 * CH, 128), BF), unroll=UNROLL)
 
     for copy in copies[2:]:
         copy.wait()
@@ -415,19 +418,25 @@
 
 
 def assemble_kernel(*refs):
-    out = refs[-1]
-    for index, piece in enumerate(refs[:-1]):
+    pieces, out, sems = refs[:4], refs[4], refs[5]
+    copies = []
+    for index, piece in enumerate(pieces):
         block = jnp.bitwise_xor(column_index(), index)
-        out[:, pl.ds(pl.multiple_of(block * 1024, 1024), 1024)] = piece[...]
+        columns = pl.ds(pl.multiple_of(block * 1024, 1024), 1024)
+        copies.append(pltpu.make_async_copy(piece, out.at[:, columns], sems.at[index]))
+        copies[-1].start()
+    for copy in copies:
+        copy.wait()
 
 
 def assemble(pieces):
-    whole = pl.BlockSpec(memory_space=pltpu.VMEM)
+    anywhere = pl.BlockSpec(memory_space=pl.ANY)
     return pl.pallas_call(
         assemble_kernel,
         out_shape=jax.ShapeDtypeStruct((64, 4096), BF),
-        in_specs=[whole] * 4,
-        out_specs=whole,
+        in_specs=[anywhere] * 4,
+        out_specs=anywhere,
+        scratch_shapes=[pltpu.SemaphoreType.DMA((4,))],
         cost_estimate=pl.CostEstimate(flops=0, bytes_accessed=1 << 20, transcendentals=0),
         compiler_params=pltpu.CompilerParams(vmem_limit_bytes=4 << 20),
         name="assemble",

time: 83.1 us -> 81.1 us (0.976)
  Pallas kernels: 17.8 us -> 15.8 us
    pallas_call x1, Pallas kernels: 8.45 us -> 6.72 us  [convolve(): pl.pallas_call(convolve_kernel, out_shape=pltpu.HBM((64, CH, 512), BF), i...]
  transfers between devices with their start and end apart: 11 -> 11, of which waited for: 7 -> 7; matrix products, arithmetic and copies ran while one was open for 0% -> 0% of each run, Pallas kernels for 17% -> 15%
where the time goes in v5:
time: 81.1 us; the launch traced here: 80.5 us
  waiting for transfers between devices  37.6 us (46%)
  starting transfers between devices  27 us (33%)
  Pallas kernels  15.8 us (19%)
    ppermute x9, waiting for transfers between devices, permuted(): return lax.ppermute(block, AXES, pairs)  37.6 us
    ppermute x9, starting transfers between devices, permuted(): return lax.ppermute(block, AXES, pairs)  12 us
    all_to_all x1, starting transfers between devices, body(): recv = lax.all_to_all(chunks, ('y', 'zl', 'x', 'zh'), 0, 0, tiled=True)  8.92 us
    pallas_call x1, Pallas kernels, convolve(): pl.pallas_call(convolve_kernel, out_shape=pltpu.HBM((64, CH, 512), BF), i...  6.72 us
    all_to_all x1, starting transfers between devices, body(): recv = lax.all_to_all(payload, SEQ, 0, 0, tiled=True)  6.05 us
    pallas_call x1, Pallas kernels, vocab(): pl.pallas_call(vocab_kernel, out_shape=jax.ShapeDtypeStruct((3 * CH, 512)...  4.8 us
    pallas_call x1, Pallas kernels, pack(): pl.pallas_call(pack_kernel, out_shape=(jax.ShapeDtypeStruct((16, CH, 640)...  1.92 us
  transfers between devices with their start and end apart: 11, of which 7 were waited for; matrix products, arithmetic and copies ran while one was open for 0% of the time, Pallas kernels for 15%

profile of v5, /device:TPU:0, one launch (start us, length us, event | category | flops | bytes accessed | tf_op | source)
XLA Modules:
  0.0 80.5 jit_solution(11462667476889708961)
XLA Ops:
  0.0 1.9 %pack.1 = (bf16[16,16,640]{2,1,0:T(8,128)(2,1)}, bf16[8,16,1024]{2,1,0:T(8,128)(2,1)S(1)}) custom-call(f32[512,256]{1,0:T(8,128)} %filt_hbm.1, s32[4,128]{1,0:T(4,128)} %bitcast.12, bf16[8,32,4096]{2,1,0:T(8,128)(2,1)} %bitcast.11), custom_call_target="tpu_custom_call" | custom-call | flops 262144 | bytes 1048576 | tf_op jit(solution)/shard_map/pack/pallas_call | solution.py:113
  1.9 6.1 %all-to-all-start = ((bf16[16,16,640]{2,1,0:T(8,128)(2,1)}), bf16[16,16,640]{2,1,0:T(8,128)(2,1)S(1)}, u32[]{:S(2)}, u32[]{:S(2)}) async-start(bf16[16,16,640]{2,1,0:T(8,128)(2,1)} %get-tuple-element.11), calls=%async_computation | async-start | bytes 655360 | tf_op jit(solution)/shard_map/all_to_all | solution.py:466
  8.0 3.7 %collective-permute-start = (bf16[128,1024]{1,0:T(8,128)(2,1)S(1)}, bf16[128,1024]{1,0:T(8,128)(2,1)S(1)}, u32[]{:S(2)}, u32[]{:S(2)}) collective-permute-start(bf16[128,1024]{1,0:T(8,128)(2,1)S(1)} %bitcast.8), channel_id=1, source_target_pairs={{0,1},{1,0},{2,3},{3,2},{4,5},{5,4},{6,7},{7,6},{8,9},{9,8},{10,11... | collective-permute-start | bytes 786440 | tf_op jit(solution)/shard_map/ppermute | solution.py:455
  11.6 4.8 %vocab.1.table = f32[48,512]{1,0:T(8,128)S(1)} custom-call(bf16[512,4096]{1,0:T(8,128)(2,1)} %embed_hbm.1, bf16[3,4096,256]{2,1,0:T(8,128)(2,1)} %bitcast.10), custom_call_target="tpu_custom_call" | custom-call | flops 1610612736 | bytes 8388608 | tf_op jit(solution)/shard_map/vocab/pallas_call | solution.py:174
  16.5 6.7 %convolve.1 = bf16[64,16,512]{2,1,0:T(8,128)(2,1)} custom-call(bf16[16,16,640]{2,1,0:T(8,128)(2,1)S(1)} %all-to-all-done.recv, f32[48,512]{1,0:T(8,128)S(1)} %vocab.1.table, f32[3,3,256]{2,1,0:T(4,128)} %refs_0_.1, f32[1,256]{1,0:T(1,128)} %bitcast.13, bf16[144,256]{1,0:T(8,128)(2,1)} %constant.10.clone.refs_2_, bf16[144,128]{1,0:T(8,128)(2,1)} %constant.11.clone.refs_3_, ...), custom_call_target="tpu_custom_call" | custom-call | flops 4294967296 | bytes 4194304 | tf_op jit(solution)/shard_map/convolve/pallas_call | solution.py:345
  23.2 8.9 %all-to-all-start.1 = ((bf16[64,16,512]{2,1,0:T(8,128)(2,1)}), bf16[64,16,512]{2,1,0:T(8,128)(2,1)S(1)}, u32[]{:S(2)}, u32[]{:S(2)}) async-start(bf16[64,16,512]{2,1,0:T(8,128)(2,1)} %convolve.1), calls=%async_computation.1 | async-start | bytes 2097152 | tf_op jit(solution)/shard_map/all_to_all | solution.py:469
  32.2 2.9 %collective-permute-start.2 = (bf16[256,1024]{1,0:T(8,128)(2,1)S(1)}, bf16[256,1024]{1,0:T(8,128)(2,1)S(1)}, u32[]{:S(2)}, u32[]{:S(2)}) collective-permute-start(bf16[256,1024]{1,0:T(8,128)(2,1)S(1)} %pad_maximum_fusion.own), channel_id=1, source_target_pairs={{0,6},{1,7},{2,4},{3,5},{4,2},{5,3},{6,0},{7,1},{8,14},{9,15},{10,... | collective-permute-start | bytes 1572872 | tf_op jit(solution)/shard_map/ppermute | solution.py:455
  35.0 0.3 collective-permute-start.1
  35.3 22.7 %collective-permute-done.2.three = bf16[256,1024]{1,0:T(8,128)(2,1)S(1)} collective-permute-done((bf16[256,1024]{1,0:T(8,128)(2,1)S(1)}, bf16[256,1024]{1,0:T(8,128)(2,1)S(1)}, u32[]{:S(2)}, u32[]{:S(2)}) %collective-permute-start.2) | collective-permute-done | bytes 524320 | tf_op jit(solution)/shard_map/ppermute | solution.py:455
  58.0 0.3 collective-permute-start.3
  58.3 1.2 %collective-permute-start.4 = (bf16[128,1024]{1,0:T(8,128)(2,1)S(1)}, bf16[128,1024]{1,0:T(8,128)(2,1)S(1)}, u32[]{:S(2)}, u32[]{:S(2)}) collective-permute-start(bf16[128,1024]{1,0:T(8,128)(2,1)S(1)} %slice.9), channel_id=1, source_target_pairs={{0,6},{1,7},{2,4},{3,5},{4,2},{5,3},{6,0},{7,1},{8,14},{9,15},{10,... | collective-permute-start | bytes 786440 | tf_op jit(solution)/shard_map/ppermute | solution.py:455
  59.6 6.4 %collective-permute-done.3.upper = bf16[128,1024]{1,0:T(8,128)(2,1)S(1)} collective-permute-done((bf16[128,1024]{1,0:T(8,128)(2,1)S(1)}, bf16[128,1024]{1,0:T(8,128)(2,1)S(1)}, u32[]{:S(2)}, u32[]{:S(2)}) %collective-permute-start.3) | collective-permute-done | bytes 262176 | tf_op jit(solution)/shard_map/ppermute | solution.py:455
  65.9 1.3 %collective-permute-done.4.lower = bf16[128,1024]{1,0:T(8,128)(2,1)S(1)} collective-permute-done((bf16[128,1024]{1,0:T(8,128)(2,1)S(1)}, bf16[128,1024]{1,0:T(8,128)(2,1)S(1)}, u32[]{:S(2)}, u32[]{:S(2)}) %collective-permute-start.4) | collective-permute-done | bytes 262176 | tf_op jit(solution)/shard_map/ppermute | solution.py:455
  67.3 0.7 send.1
  68.1 0.7 keep.1
  68.9 1.2 %collective-permute-done.5.came = bf16[256,1024]{1,0:T(8,128)(2,1)S(1)} collective-permute-done((bf16[256,1024]{1,0:T(8,128)(2,1)S(1)}, bf16[256,1024]{1,0:T(8,128)(2,1)S(1)}, u32[]{:S(2)}, u32[]{:S(2)}) %collective-permute-start.5) | collective-permute-done | bytes 524320 | tf_op jit(solution)/shard_map/ppermute | solution.py:455
  70.0 0.1 combine.1
  70.1 1.5 %collective-permute-start.6 = (bf16[64,1024]{1,0:T(8,128)(2,1)S(1)}, bf16[64,1024]{1,0:T(8,128)(2,1)S(1)}, u32[]{:S(2)}, u32[]{:S(2)}) collective-permute-start(bf16[64,1024]{1,0:T(8,128)(2,1)S(1)} %get-tuple-element.14), channel_id=1, source_target_pairs={{0,16},{1,17},{2,18},{3,19},{4,20},{5,21},{6,22},{7,23},{8,24},{9,... | collective-permute-start | bytes 393224 | tf_op jit(solution)/shard_map/ppermute | solution.py:455
  71.7 1.5 %collective-permute-start.7 = (bf16[64,1024]{1,0:T(8,128)(2,1)S(1)}, bf16[64,1024]{1,0:T(8,128)(2,1)S(1)}, u32[]{:S(2)}, u32[]{:S(2)}) collective-permute-start(bf16[64,1024]{1,0:T(8,128)(2,1)S(1)} %get-tuple-element.15), channel_id=1, source_target_pairs={{0,32},{1,33},{2,34},{3,35},{4,36},{5,37},{6,38},{7,39},{8,40},{9,... | collective-permute-start | bytes 393224 | tf_op jit(solution)/shard_map/ppermute | solution.py:455
  73.2 0.5 collective-permute-start.8
  73.7 2.0 %collective-permute-done.6.refs_1_ = bf16[64,1024]{1,0:T(8,128)(2,1)S(1)} collective-permute-done((bf16[64,1024]{1,0:T(8,128)(2,1)S(1)}, bf16[64,1024]{1,0:T(8,128)(2,1)S(1)}, u32[]{:S(2)}, u32[]{:S(2)}) %collective-permute-start.6) | collective-permute-done | bytes 131104 | tf_op jit(solution)/shard_map/ppermute | solution.py:455
  75.7 2.3 %collective-permute-done.7.refs_2_ = bf16[64,1024]{1,0:T(8,128)(2,1)S(1)} collective-permute-done((bf16[64,1024]{1,0:T(8,128)(2,1)S(1)}, bf16[64,1024]{1,0:T(8,128)(2,1)S(1)}, u32[]{:S(2)}, u32[]{:S(2)}) %collective-permute-start.7) | collective-permute-done | bytes 131104 | tf_op jit(solution)/shard_map/ppermute | solution.py:455
  78.0 1.7 %collective-permute-done.8.refs_3_ = bf16[64,1024]{1,0:T(8,128)(2,1)S(1)} collective-permute-done((bf16[64,1024]{1,0:T(8,128)(2,1)S(1)}, bf16[64,1024]{1,0:T(8,128)(2,1)S(1)}, u32[]{:S(2)}, u32[]{:S(2)}) %collective-permute-start.8) | collective-permute-done | bytes 131104 | tf_op jit(solution)/shard_map/ppermute | solution.py:455
  79.7 0.8 %assemble.1 = bf16[64,4096]{1,0:T(8,128)(2,1)} custom-call(bf16[64,1024]{1,0:T(8,128)(2,1)S(1)} %get-tuple-element.13.refs_0_, bf16[64,1024]{1,0:T(8,128)(2,1)S(1)} %collective-permute-done.6.refs_1_, bf16[64,1024]{1,0:T(8,128)(2,1)S(1)} %collective-permute-done.7.refs_2_, bf16[64,1024]{1,0:T(8,128)(2,1)S(1)} %collective-permute-done.8.refs_3_), custom_call_target="tpu_custom_call" | custom-call | bytes 1048576 | tf_op jit(solution)/shard_map/assemble/pallas_call | solution.py:434
  (8 shorter events, 0.2 us)
Async XLA Ops:
  1.9 14.5 %all-to-all-start = ((bf16[16,16,640]{2,1,0:T(8,128)(2,1)}), bf16[16,16,640]{2,1,0:T(8,128)(2,1)S(1)}, u32[]{:S(2)}, u32[]{:S(2)}) async-start(bf16[16,16,640]{2,1,0:T(8,128)(2,1)} %get-tuple-element.11), calls=%async_computation | async-start | bytes 655360 | tf_op jit(solution)/shard_map/all_to_all | solution.py:466
  8.0 24.1 %collective-permute-start = (bf16[128,1024]{1,0:T(8,128)(2,1)S(1)}, bf16[128,1024]{1,0:T(8,128)(2,1)S(1)}, u32[]{:S(2)}, u32[]{:S(2)}) collective-permute-start(bf16[128,1024]{1,0:T(8,128)(2,1)S(1)} %bitcast.8), channel_id=1, source_target_pairs={{0,1},{1,0},{2,3},{3,2},{4,5},{5,4},{6,7},{7,6},{8,9},{9,8},{10,11... | collective-permute-start | bytes 786440 | tf_op jit(solution)/shard_map/ppermute | solution.py:455
  23.2 44.1 %all-to-all-start.1 = ((bf16[64,16,512]{2,1,0:T(8,128)(2,1)}), bf16[64,16,512]{2,1,0:T(8,128)(2,1)S(1)}, u32[]{:S(2)}, u32[]{:S(2)}) async-start(bf16[64,16,512]{2,1,0:T(8,128)(2,1)} %convolve.1), calls=%async_computation.1 | async-start | bytes 2097152 | tf_op jit(solution)/shard_map/all_to_all | solution.py:469
  32.2 25.8 %collective-permute-start.2 = (bf16[256,1024]{1,0:T(8,128)(2,1)S(1)}, bf16[256,1024]{1,0:T(8,128)(2,1)S(1)}, u32[]{:S(2)}, u32[]{:S(2)}) collective-permute-start(bf16[256,1024]{1,0:T(8,128)(2,1)S(1)} %pad_maximum_fusion.own), channel_id=1, source_target_pairs={{0,6},{1,7},{2,4},{3,5},{4,2},{5,3},{6,0},{7,1},{8,14},{9,15},{10,... | collective-permute-start | bytes 1572872 | tf_op jit(solution)/shard_map/ppermute | solution.py:455
  35.0 23.3 %collective-permute-start.1 = (bf16[256,1024]{1,0:T(8,128)(2,1)S(1)}, bf16[256,1024]{1,0:T(8,128)(2,1)S(1)}, u32[]{:S(2)}, u32[]{:S(2)}) collective-permute-start(bf16[256,1024]{1,0:T(8,128)(2,1)S(1)} %pad_maximum_fusion.own), channel_id=1, source_target_pairs={{0,2},{1,3},{2,0},{3,1},{4,6},{5,7},{6,4},{7,5},{8,10},{9,11},{10,... | collective-permute-start | bytes 1572872 | tf_op jit(solution)/shard_map/ppermute | solution.py:455
  58.0 8.0 %collective-permute-start.3 = (bf16[128,1024]{1,0:T(8,128)(2,1)S(1)}, bf16[128,1024]{1,0:T(8,128)(2,1)S(1)}, u32[]{:S(2)}, u32[]{:S(2)}) collective-permute-start(bf16[128,1024]{1,0:T(8,128)(2,1)S(1)} %slice.8), channel_id=1, source_target_pairs={{0,2},{1,3},{2,0},{3,1},{4,6},{5,7},{6,4},{7,5},{8,10},{9,11},{10,... | collective-permute-start | bytes 786440 | tf_op jit(solution)/shard_map/ppermute | solution.py:455
  58.3 8.9 %collective-permute-start.4 = (bf16[128,1024]{1,0:T(8,128)(2,1)S(1)}, bf16[128,1024]{1,0:T(8,128)(2,1)S(1)}, u32[]{:S(2)}, u32[]{:S(2)}) collective-permute-start(bf16[128,1024]{1,0:T(8,128)(2,1)S(1)} %slice.9), channel_id=1, source_target_pairs={{0,6},{1,7},{2,4},{3,5},{4,2},{5,3},{6,0},{7,1},{8,14},{9,15},{10,... | collective-permute-start | bytes 786440 | tf_op jit(solution)/shard_map/ppermute | solution.py:455
  68.0 2.0 %collective-permute-start.5 = (bf16[256,1024]{1,0:T(8,128)(2,1)S(1)}, bf16[256,1024]{1,0:T(8,128)(2,1)S(1)}, u32[]{:S(2)}, u32[]{:S(2)}) collective-permute-start(bf16[256,1024]{1,0:T(8,128)(2,1)S(1)} %send.1), channel_id=1, source_target_pairs={{0,8},{1,9},{2,10},{3,11},{4,12},{5,13},{6,14},{7,15},{8,0},{9,1},... | collective-permute-start | bytes 1572872 | tf_op jit(solution)/shard_map/ppermute | solution.py:455
  70.1 5.6 %collective-permute-start.6 = (bf16[64,1024]{1,0:T(8,128)(2,1)S(1)}, bf16[64,1024]{1,0:T(8,128)(2,1)S(1)}, u32[]{:S(2)}, u32[]{:S(2)}) collective-permute-start(bf16[64,1024]{1,0:T(8,128)(2,1)S(1)} %get-tuple-element.14), channel_id=1, source_target_pairs={{0,16},{1,17},{2,18},{3,19},{4,20},{5,21},{6,22},{7,23},{8,24},{9,... | collective-permute-start | bytes 393224 | tf_op jit(solution)/shard_map/ppermute | solution.py:455
  71.7 6.4 %collective-permute-start.7 = (bf16[64,1024]{1,0:T(8,128)(2,1)S(1)}, bf16[64,1024]{1,0:T(8,128)(2,1)S(1)}, u32[]{:S(2)}, u32[]{:S(2)}) collective-permute-start(bf16[64,1024]{1,0:T(8,128)(2,1)S(1)} %get-tuple-element.15), channel_id=1, source_target_pairs={{0,32},{1,33},{2,34},{3,35},{4,36},{5,37},{6,38},{7,39},{8,40},{9,... | collective-permute-start | bytes 393224 | tf_op jit(solution)/shard_map/ppermute | solution.py:455
  73.2 6.5 %collective-permute-start.8 = (bf16[64,1024]{1,0:T(8,128)(2,1)S(1)}, bf16[64,1024]{1,0:T(8,128)(2,1)S(1)}, u32[]{:S(2)}, u32[]{:S(2)}) collective-permute-start(bf16[64,1024]{1,0:T(8,128)(2,1)S(1)} %get-tuple-element.16), channel_id=1, source_target_pairs={{0,48},{1,49},{2,50},{3,51},{4,52},{5,53},{6,54},{7,55},{8,56},{9,... | collective-permute-start | bytes 393224 | tf_op jit(solution)/shard_map/ppermute | solution.py:455

commit v6 on v5

--- a/solution.py
+++ b/solution.py
@@ -417,11 +417,12 @@
     )(keep, came)
 
 
-def assemble_kernel(*refs):
-    pieces, out, sems = refs[:4], refs[4], refs[5]
+def assemble_kernel(first, *refs):
+    pieces, out, sems = refs[: -2], refs[-2], refs[-1]
+    pieces = pieces if first == 0 else pieces[:-1]
     copies = []
     for index, piece in enumerate(pieces):
-        block = jnp.bitwise_xor(column_index(), index)
+        block = jnp.bitwise_xor(column_index(), first + index)
         columns = pl.ds(pl.multiple_of(block * 1024, 1024), 1024)
         copies.append(pltpu.make_async_copy(piece, out.at[:, columns], sems.at[index]))
         copies[-1].start()
@@ -429,18 +430,20 @@
         copy.wait()
 
 
-def assemble(pieces):
+def assemble(pieces, first=0, into=None):
     anywhere = pl.BlockSpec(memory_space=pl.ANY)
+    operands = list(pieces) + ([] if into is None else [into])
     return pl.pallas_call(
-        assemble_kernel,
+        functools.partial(assemble_kernel, first),
         out_shape=jax.ShapeDtypeStruct((64, 4096), BF),
-        in_specs=[anywhere] * 4,
+        in_specs=[anywhere] * len(operands),
         out_specs=anywhere,
-        scratch_shapes=[pltpu.SemaphoreType.DMA((4,))],
+        scratch_shapes=[pltpu.SemaphoreType.DMA((len(pieces),))],
+        input_output_aliases={} if into is None else {len(pieces): 0},
         cost_estimate=pl.CostEstimate(flops=0, bytes_accessed=1 << 20, transcendentals=0),
         compiler_params=pltpu.CompilerParams(vmem_limit_bytes=4 << 20),
-        name="assemble",
-    )(*pieces)
+        name="assemble" if into is None else "finish",
+    )(*operands)
 
 
 def permuted(block, move):
@@ -476,7 +479,8 @@
     pieces = list(combine(keep, came))
     for index in range(1, 4):
         pieces[index] = permuted(pieces[index], lambda d: {"y": d["y"] ^ (index // 2), "zl": d["zl"] ^ (index % 2)})
-    return assemble(pieces)
+    most = assemble(pieces[:3])
+    return assemble(pieces[3:], 3, most)
 
 
 def solution(mesh):

time: 81.1 us -> 80.9 us (level)
  transfers between devices with their start and end apart: 11 -> 11, of which waited for: 7 -> 7; matrix products, arithmetic and copies ran while one was open for 0% -> 0% of each run, Pallas kernels for 15% -> 16%
where the time goes in v6:
time: 80.9 us; the launch traced here: 80.4 us
  waiting for transfers between devices  36.8 us (45%)
  starting transfers between devices  27 us (33%)
  Pallas kernels  16.4 us (20%)
    ppermute x9, waiting for transfers between devices, permuted(): return lax.ppermute(block, AXES, pairs)  36.8 us
    ppermute x9, starting transfers between devices, permuted(): return lax.ppermute(block, AXES, pairs)  12 us
    all_to_all x1, starting transfers between devices, body(): recv = lax.all_to_all(chunks, ('y', 'zl', 'x', 'zh'), 0, 0, tiled=True)  8.92 us
    pallas_call x1, Pallas kernels, convolve(): pl.pallas_call(convolve_kernel, out_shape=pltpu.HBM((64, CH, 512), BF), i...  6.72 us
    all_to_all x1, starting transfers between devices, body(): recv = lax.all_to_all(payload, SEQ, 0, 0, tiled=True)  6.05 us
    pallas_call x1, Pallas kernels, vocab(): pl.pallas_call(vocab_kernel, out_shape=jax.ShapeDtypeStruct((3 * CH, 512)...  4.8 us
    pallas_call x1, Pallas kernels, pack(): pl.pallas_call(pack_kernel, out_shape=(jax.ShapeDtypeStruct((16, CH, 640)...  1.92 us
  transfers between devices with their start and end apart: 11, of which 7 were waited for; matrix products, arithmetic and copies ran while one was open for 0% of the time, Pallas kernels for 16%

profile of v6, /device:TPU:0, one launch (start us, length us, event | category | flops | bytes accessed | tf_op | source)
XLA Modules:
  0.0 80.4 jit_solution(10895229423730857076)
XLA Ops:
  0.0 1.9 %pack.1 = (bf16[16,16,640]{2,1,0:T(8,128)(2,1)}, bf16[8,16,1024]{2,1,0:T(8,128)(2,1)S(1)}) custom-call(f32[512,256]{1,0:T(8,128)} %filt_hbm.1, s32[4,128]{1,0:T(4,128)} %bitcast.12, bf16[8,32,4096]{2,1,0:T(8,128)(2,1)} %bitcast.11), custom_call_target="tpu_custom_call" | custom-call | flops 262144 | bytes 1048576 | tf_op jit(solution)/shard_map/pack/pallas_call | solution.py:113
  1.9 6.1 %all-to-all-start = ((bf16[16,16,640]{2,1,0:T(8,128)(2,1)}), bf16[16,16,640]{2,1,0:T(8,128)(2,1)S(1)}, u32[]{:S(2)}, u32[]{:S(2)}) async-start(bf16[16,16,640]{2,1,0:T(8,128)(2,1)} %get-tuple-element.11), calls=%async_computation | async-start | bytes 655360 | tf_op jit(solution)/shard_map/all_to_all | solution.py:469
  8.0 3.7 %collective-permute-start = (bf16[128,1024]{1,0:T(8,128)(2,1)S(1)}, bf16[128,1024]{1,0:T(8,128)(2,1)S(1)}, u32[]{:S(2)}, u32[]{:S(2)}) collective-permute-start(bf16[128,1024]{1,0:T(8,128)(2,1)S(1)} %bitcast.8), channel_id=1, source_target_pairs={{0,1},{1,0},{2,3},{3,2},{4,5},{5,4},{6,7},{7,6},{8,9},{9,8},{10,11... | collective-permute-start | bytes 786440 | tf_op jit(solution)/shard_map/ppermute | solution.py:458
  11.6 4.8 %vocab.1.table = f32[48,512]{1,0:T(8,128)S(1)} custom-call(bf16[512,4096]{1,0:T(8,128)(2,1)} %embed_hbm.1, bf16[3,4096,256]{2,1,0:T(8,128)(2,1)} %bitcast.10), custom_call_target="tpu_custom_call" | custom-call | flops 1610612736 | bytes 8388608 | tf_op jit(solution)/shard_map/vocab/pallas_call | solution.py:174
  16.5 6.7 %convolve.1 = bf16[64,16,512]{2,1,0:T(8,128)(2,1)} custom-call(bf16[16,16,640]{2,1,0:T(8,128)(2,1)S(1)} %all-to-all-done.recv, f32[48,512]{1,0:T(8,128)S(1)} %vocab.1.table, f32[3,3,256]{2,1,0:T(4,128)} %refs_0_.1, f32[1,256]{1,0:T(1,128)} %bitcast.13, bf16[144,256]{1,0:T(8,128)(2,1)} %constant.10.clone.refs_2_, bf16[144,128]{1,0:T(8,128)(2,1)} %constant.11.clone.refs_3_, ...), custom_call_target="tpu_custom_call" | custom-call | flops 4294967296 | bytes 4194304 | tf_op jit(solution)/shard_map/convolve/pallas_call | solution.py:345
  23.2 8.9 %all-to-all-start.1 = ((bf16[64,16,512]{2,1,0:T(8,128)(2,1)}), bf16[64,16,512]{2,1,0:T(8,128)(2,1)S(1)}, u32[]{:S(2)}, u32[]{:S(2)}) async-start(bf16[64,16,512]{2,1,0:T(8,128)(2,1)} %convolve.1), calls=%async_computation.1 | async-start | bytes 2097152 | tf_op jit(solution)/shard_map/all_to_all | solution.py:472
  32.2 2.9 %collective-permute-start.2 = (bf16[256,1024]{1,0:T(8,128)(2,1)S(1)}, bf16[256,1024]{1,0:T(8,128)(2,1)S(1)}, u32[]{:S(2)}, u32[]{:S(2)}) collective-permute-start(bf16[256,1024]{1,0:T(8,128)(2,1)S(1)} %pad_maximum_fusion.own), channel_id=1, source_target_pairs={{0,6},{1,7},{2,4},{3,5},{4,2},{5,3},{6,0},{7,1},{8,14},{9,15},{10,... | collective-permute-start | bytes 1572872 | tf_op jit(solution)/shard_map/ppermute | solution.py:458
  35.0 0.3 collective-permute-start.1
  35.3 22.7 %collective-permute-done.2.three = bf16[256,1024]{1,0:T(8,128)(2,1)S(1)} collective-permute-done((bf16[256,1024]{1,0:T(8,128)(2,1)S(1)}, bf16[256,1024]{1,0:T(8,128)(2,1)S(1)}, u32[]{:S(2)}, u32[]{:S(2)}) %collective-permute-start.2) | collective-permute-done | bytes 524320 | tf_op jit(solution)/shard_map/ppermute | solution.py:458
  58.0 0.3 collective-permute-start.3
  58.3 1.2 %collective-permute-start.4 = (bf16[128,1024]{1,0:T(8,128)(2,1)S(1)}, bf16[128,1024]{1,0:T(8,128)(2,1)S(1)}, u32[]{:S(2)}, u32[]{:S(2)}) collective-permute-start(bf16[128,1024]{1,0:T(8,128)(2,1)S(1)} %slice.9), channel_id=1, source_target_pairs={{0,6},{1,7},{2,4},{3,5},{4,2},{5,3},{6,0},{7,1},{8,14},{9,15},{10,... | collective-permute-start | bytes 786440 | tf_op jit(solution)/shard_map/ppermute | solution.py:458
  59.6 6.4 %collective-permute-done.3.upper = bf16[128,1024]{1,0:T(8,128)(2,1)S(1)} collective-permute-done((bf16[128,1024]{1,0:T(8,128)(2,1)S(1)}, bf16[128,1024]{1,0:T(8,128)(2,1)S(1)}, u32[]{:S(2)}, u32[]{:S(2)}) %collective-permute-start.3) | collective-permute-done | bytes 262176 | tf_op jit(solution)/shard_map/ppermute | solution.py:458
  65.9 1.3 %collective-permute-done.4.lower = bf16[128,1024]{1,0:T(8,128)(2,1)S(1)} collective-permute-done((bf16[128,1024]{1,0:T(8,128)(2,1)S(1)}, bf16[128,1024]{1,0:T(8,128)(2,1)S(1)}, u32[]{:S(2)}, u32[]{:S(2)}) %collective-permute-start.4) | collective-permute-done | bytes 262176 | tf_op jit(solution)/shard_map/ppermute | solution.py:458
  67.3 0.7 send.1
  68.1 0.7 keep.1
  68.9 1.2 %collective-permute-done.5.came = bf16[256,1024]{1,0:T(8,128)(2,1)S(1)} collective-permute-done((bf16[256,1024]{1,0:T(8,128)(2,1)S(1)}, bf16[256,1024]{1,0:T(8,128)(2,1)S(1)}, u32[]{:S(2)}, u32[]{:S(2)}) %collective-permute-start.5) | collective-permute-done | bytes 524320 | tf_op jit(solution)/shard_map/ppermute | solution.py:458
  70.1 1.5 %collective-permute-start.7 = (bf16[64,1024]{1,0:T(8,128)(2,1)S(1)}, bf16[64,1024]{1,0:T(8,128)(2,1)S(1)}, u32[]{:S(2)}, u32[]{:S(2)}) collective-permute-start(bf16[64,1024]{1,0:T(8,128)(2,1)S(1)} %get-tuple-element.15), channel_id=1, source_target_pairs={{0,16},{1,17},{2,18},{3,19},{4,20},{5,21},{6,22},{7,23},{8,24},{9,... | collective-permute-start | bytes 393224 | tf_op jit(solution)/shard_map/ppermute | solution.py:458
  71.7 1.5 %collective-permute-start.8 = (bf16[64,1024]{1,0:T(8,128)(2,1)S(1)}, bf16[64,1024]{1,0:T(8,128)(2,1)S(1)}, u32[]{:S(2)}, u32[]{:S(2)}) collective-permute-start(bf16[64,1024]{1,0:T(8,128)(2,1)S(1)} %get-tuple-element.16), channel_id=1, source_target_pairs={{0,32},{1,33},{2,34},{3,35},{4,36},{5,37},{6,38},{7,39},{8,40},{9,... | collective-permute-start | bytes 393224 | tf_op jit(solution)/shard_map/ppermute | solution.py:458
  73.2 0.5 collective-permute-start.6
  73.7 2.0 %collective-permute-done.7.refs_1_ = bf16[64,1024]{1,0:T(8,128)(2,1)S(1)} collective-permute-done((bf16[64,1024]{1,0:T(8,128)(2,1)S(1)}, bf16[64,1024]{1,0:T(8,128)(2,1)S(1)}, u32[]{:S(2)}, u32[]{:S(2)}) %collective-permute-start.7) | collective-permute-done | bytes 131104 | tf_op jit(solution)/shard_map/ppermute | solution.py:458
  75.7 2.3 %collective-permute-done.8.refs_2_ = bf16[64,1024]{1,0:T(8,128)(2,1)S(1)} collective-permute-done((bf16[64,1024]{1,0:T(8,128)(2,1)S(1)}, bf16[64,1024]{1,0:T(8,128)(2,1)S(1)}, u32[]{:S(2)}, u32[]{:S(2)}) %collective-permute-start.8) | collective-permute-done | bytes 131104 | tf_op jit(solution)/shard_map/ppermute | solution.py:458
  78.0 0.8 assemble.1.refs_1_
  78.8 0.9 %collective-permute-done.6.refs_0_ = bf16[64,1024]{1,0:T(8,128)(2,1)S(1)} collective-permute-done((bf16[64,1024]{1,0:T(8,128)(2,1)S(1)}, bf16[64,1024]{1,0:T(8,128)(2,1)S(1)}, u32[]{:S(2)}, u32[]{:S(2)}) %collective-permute-start.6) | collective-permute-done | bytes 131104 | tf_op jit(solution)/shard_map/ppermute | solution.py:458
  79.7 0.7 finish.1
  (9 shorter events, 0.3 us)
Async XLA Ops:
  1.9 14.5 %all-to-all-start = ((bf16[16,16,640]{2,1,0:T(8,128)(2,1)}), bf16[16,16,640]{2,1,0:T(8,128)(2,1)S(1)}, u32[]{:S(2)}, u32[]{:S(2)}) async-start(bf16[16,16,640]{2,1,0:T(8,128)(2,1)} %get-tuple-element.11), calls=%async_computation | async-start | bytes 655360 | tf_op jit(solution)/shard_map/all_to_all | solution.py:469
  8.0 24.1 %collective-permute-start = (bf16[128,1024]{1,0:T(8,128)(2,1)S(1)}, bf16[128,1024]{1,0:T(8,128)(2,1)S(1)}, u32[]{:S(2)}, u32[]{:S(2)}) collective-permute-start(bf16[128,1024]{1,0:T(8,128)(2,1)S(1)} %bitcast.8), channel_id=1, source_target_pairs={{0,1},{1,0},{2,3},{3,2},{4,5},{5,4},{6,7},{7,6},{8,9},{9,8},{10,11... | collective-permute-start | bytes 786440 | tf_op jit(solution)/shard_map/ppermute | solution.py:458
  23.2 44.1 %all-to-all-start.1 = ((bf16[64,16,512]{2,1,0:T(8,128)(2,1)}), bf16[64,16,512]{2,1,0:T(8,128)(2,1)S(1)}, u32[]{:S(2)}, u32[]{:S(2)}) async-start(bf16[64,16,512]{2,1,0:T(8,128)(2,1)} %convolve.1), calls=%async_computation.1 | async-start | bytes 2097152 | tf_op jit(solution)/shard_map/all_to_all | solution.py:472
  32.2 25.8 %collective-permute-start.2 = (bf16[256,1024]{1,0:T(8,128)(2,1)S(1)}, bf16[256,1024]{1,0:T(8,128)(2,1)S(1)}, u32[]{:S(2)}, u32[]{:S(2)}) collective-permute-start(bf16[256,1024]{1,0:T(8,128)(2,1)S(1)} %pad_maximum_fusion.own), channel_id=1, source_target_pairs={{0,6},{1,7},{2,4},{3,5},{4,2},{5,3},{6,0},{7,1},{8,14},{9,15},{10,... | collective-permute-start | bytes 1572872 | tf_op jit(solution)/shard_map/ppermute | solution.py:458
  35.0 23.3 %collective-permute-start.1 = (bf16[256,1024]{1,0:T(8,128)(2,1)S(1)}, bf16[256,1024]{1,0:T(8,128)(2,1)S(1)}, u32[]{:S(2)}, u32[]{:S(2)}) collective-permute-start(bf16[256,1024]{1,0:T(8,128)(2,1)S(1)} %pad_maximum_fusion.own), channel_id=1, source_target_pairs={{0,2},{1,3},{2,0},{3,1},{4,6},{5,7},{6,4},{7,5},{8,10},{9,11},{10,... | collective-permute-start | bytes 1572872 | tf_op jit(solution)/shard_map/ppermute | solution.py:458
  58.0 8.0 %collective-permute-start.3 = (bf16[128,1024]{1,0:T(8,128)(2,1)S(1)}, bf16[128,1024]{1,0:T(8,128)(2,1)S(1)}, u32[]{:S(2)}, u32[]{:S(2)}) collective-permute-start(bf16[128,1024]{1,0:T(8,128)(2,1)S(1)} %slice.8), channel_id=1, source_target_pairs={{0,2},{1,3},{2,0},{3,1},{4,6},{5,7},{6,4},{7,5},{8,10},{9,11},{10,... | collective-permute-start | bytes 786440 | tf_op jit(solution)/shard_map/ppermute | solution.py:458
  58.3 8.9 %collective-permute-start.4 = (bf16[128,1024]{1,0:T(8,128)(2,1)S(1)}, bf16[128,1024]{1,0:T(8,128)(2,1)S(1)}, u32[]{:S(2)}, u32[]{:S(2)}) collective-permute-start(bf16[128,1024]{1,0:T(8,128)(2,1)S(1)} %slice.9), channel_id=1, source_target_pairs={{0,6},{1,7},{2,4},{3,5},{4,2},{5,3},{6,0},{7,1},{8,14},{9,15},{10,... | collective-permute-start | bytes 786440 | tf_op jit(solution)/shard_map/ppermute | solution.py:458
  68.0 2.0 %collective-permute-start.5 = (bf16[256,1024]{1,0:T(8,128)(2,1)S(1)}, bf16[256,1024]{1,0:T(8,128)(2,1)S(1)}, u32[]{:S(2)}, u32[]{:S(2)}) collective-permute-start(bf16[256,1024]{1,0:T(8,128)(2,1)S(1)} %send.1), channel_id=1, source_target_pairs={{0,8},{1,9},{2,10},{3,11},{4,12},{5,13},{6,14},{7,15},{8,0},{9,1},... | collective-permute-start | bytes 1572872 | tf_op jit(solution)/shard_map/ppermute | solution.py:458
  70.1 5.6 %collective-permute-start.7 = (bf16[64,1024]{1,0:T(8,128)(2,1)S(1)}, bf16[64,1024]{1,0:T(8,128)(2,1)S(1)}, u32[]{:S(2)}, u32[]{:S(2)}) collective-permute-start(bf16[64,1024]{1,0:T(8,128)(2,1)S(1)} %get-tuple-element.15), channel_id=1, source_target_pairs={{0,16},{1,17},{2,18},{3,19},{4,20},{5,21},{6,22},{7,23},{8,24},{9,... | collective-permute-start | bytes 393224 | tf_op jit(solution)/shard_map/ppermute | solution.py:458
  71.7 6.4 %collective-permute-start.8 = (bf16[64,1024]{1,0:T(8,128)(2,1)S(1)}, bf16[64,1024]{1,0:T(8,128)(2,1)S(1)}, u32[]{:S(2)}, u32[]{:S(2)}) collective-permute-start(bf16[64,1024]{1,0:T(8,128)(2,1)S(1)} %get-tuple-element.16), channel_id=1, source_target_pairs={{0,32},{1,33},{2,34},{3,35},{4,36},{5,37},{6,38},{7,39},{8,40},{9,... | collective-permute-start | bytes 393224 | tf_op jit(solution)/shard_map/ppermute | solution.py:458
  73.2 6.5 %collective-permute-start.6 = (bf16[64,1024]{1,0:T(8,128)(2,1)S(1)}, bf16[64,1024]{1,0:T(8,128)(2,1)S(1)}, u32[]{:S(2)}, u32[]{:S(2)}) collective-permute-start(bf16[64,1024]{1,0:T(8,128)(2,1)S(1)} %get-tuple-element.13), channel_id=1, source_target_pairs={{0,48},{1,49},{2,50},{3,51},{4,52},{5,53},{6,54},{7,55},{8,56},{9,... | collective-permute-start | bytes 393224 | tf_op jit(solution)/shard_map/ppermute | solution.py:458
